TPU v7x, 32 devices: a whole 2x2x4 slice. The times are simulated.
32 devices in a mesh: grp: 1, row: 32 (over z, y, x, core).
Axes of the slice: x: 2, y: 2, z: 4, core: 2. Of those that a mesh axis runs over, the one named last changes fastest.
Arguments:
- features: bfloat16 [64, 192, 2048], P(('grp', 'row')), may hold values from -6 to 6
- branch_kernel_weight: bfloat16 [2048, 10, 128], P('row'), may hold values from -0.046875 to 0.046875
- branch_norm_bias: float32 [2, 128], replicated, may hold values from -3 to 3
- merge_weight: bfloat16 [256, 256], P('row'), may hold values from -0.375 to 0.375
- merge_bias: float32 [256], replicated, may hold values from -3 to 3
- cotangent: bfloat16 [64, 192, 256], P(('grp', 'row')), may hold values from -24 to 24
Outputs:
- merged: bfloat16 [64, 192, 256], P(('grp', 'row'))
- input_grad: bfloat16 [64, 192, 2048], P(('grp', 'row'))
- branch_kernel_gradient: float32 [2048, 10, 128], P(('grp', 'row'))
- grad_merge: float32 [256, 256], P(('grp', 'row'))
All inputs are finite; a program needn't handle non-finite values.
Results may differ from a plain program's by a relative error of at most 0.023.
The roundings to bfloat16 on the way count: a program that leaves them out, or rounds other values in their place, can miss the bound.
Values may be sent and summed in bfloat16 or wider, within the bound.
No kernel may reach another device: no remote copies, remote signals or barrier semaphores. Data moves between devices by JAX's collectives and lax.ppermute only.
A program may use at most 128 MiB of HBM per device.

v0:
```python
import math

import jax
import jax.numpy as jnp
from jax import lax
from jax.sharding import PartitionSpec as P

DILATION_RATE = 18


def passed_along(block, axis, distance):
    devices = range(lax.axis_size(axis))
    route = [(i - distance, i) for i in devices if i - distance in devices]
    return lax.ppermute(block, axis, route)


def transposed_product(left, right):
    return lax.dot_general(
        left, right, (((0,), (0,)), ((), ())), preferred_element_type=jnp.float32
    )


def ndot(left, right):
    return lax.dot_general(
        left, right, (((1,), (1,)), ((), ())), preferred_element_type=jnp.float32
    )


def gather_feature_rows(row_block, device_step):
    return passed_along(row_block, "row", device_step)


def gather_gradient_rows(row_block, device_step):
    return passed_along(row_block, "row", device_step)


def load_row_block(row_block, row_offset, pull_rows):
    block_row_count = row_block.shape[0]
    device_off, inner_off = divmod(row_offset, block_row_count)
    return pull_rows(row_block, -device_off)


def on_device(
    features, branch_kernel_weight, branch_norm_bias, merge_weight, merge_bias, cotangent
):
    block_row_count = features.shape[0]
    width_columns = features.shape[1]
    channel_count = features.shape[2]
    branch_channel_width = branch_kernel_weight.shape[2]
    pixel_count = block_row_count * width_columns
    gradient_scale = 1.0 / math.sqrt(block_row_count * lax.axis_size("row") * width_columns)
    flattened = features.reshape(pixel_count, channel_count)
    row_groups = [
        load_row_block(features, -DILATION_RATE, gather_feature_rows),
        features,
        load_row_block(features, DILATION_RATE, gather_feature_rows),
    ]
    padded_row_groups = [
        jnp.pad(row_group, ((0, 0), (DILATION_RATE, DILATION_RATE), (0, 0)))
        for row_group in row_groups
    ]
    tap_windows = [
        padded_row_groups[tap_number // 3][
            :, tap_number % 3 * DILATION_RATE : tap_number % 3 * DILATION_RATE + width_columns
        ].reshape(pixel_count, channel_count)
        for tap_number in range(9)
    ]
    whole_branch, whole_merge = (
        lax.all_gather(branch_kernel_weight, "row", axis=0, tiled=True),
        lax.all_gather(merge_weight, "row", axis=0, tiled=True),
    )
    z_one = jnp.dot(flattened, whole_branch[:, 0, :], preferred_element_type=jnp.float32)
    dilated_preactivation = jnp.zeros((pixel_count, branch_channel_width), jnp.float32)
    for tap_number in range(9):
        dilated_preactivation = dilated_preactivation + jnp.dot(
            tap_windows[tap_number],
            whole_branch[:, 1 + tap_number, :],
            preferred_element_type=jnp.float32,
        )
    pointwise_activation = jnp.maximum(z_one + branch_norm_bias[0], 0.0).astype(jnp.bfloat16)
    dilated_activation = jnp.maximum(dilated_preactivation + branch_norm_bias[1], 0.0).astype(
        jnp.bfloat16
    )
    combined = jnp.concatenate([pointwise_activation, dilated_activation], axis=1)
    merged = jnp.maximum(
        jnp.dot(combined, whole_merge, preferred_element_type=jnp.float32) + merge_bias, 0.0
    ).astype(jnp.bfloat16)
    grad_out = jnp.where(
        merged > 0, cotangent.reshape(pixel_count, merged.shape[1]), jnp.zeros((), jnp.bfloat16)
    )
    grad_merge = (
        lax.psum_scatter(
            transposed_product(combined, grad_out), "row", scatter_dimension=0, tiled=True
        )
        * gradient_scale
    )
    backward_pass = ndot(grad_out, whole_merge)
    pointwise_gradient = jnp.where(
        pointwise_activation > 0, backward_pass[:, :branch_channel_width], 0.0
    ).astype(jnp.bfloat16)
    dilated_gradient = jnp.where(
        dilated_activation > 0, backward_pass[:, branch_channel_width:], 0.0
    ).astype(jnp.bfloat16)
    gradient_map = dilated_gradient.reshape(block_row_count, width_columns, branch_channel_width)
    gradient_row_groups = [
        load_row_block(gradient_map, DILATION_RATE, gather_gradient_rows),
        gradient_map,
        load_row_block(gradient_map, -DILATION_RATE, gather_gradient_rows),
    ]
    padded_gradient = [
        jnp.pad(gradient_row_group, ((0, 0), (DILATION_RATE, DILATION_RATE), (0, 0)))
        for gradient_row_group in gradient_row_groups
    ]
    grad_views = [
        padded_gradient[tap_number // 3][
            :,
            (2 - tap_number % 3) * DILATION_RATE : (2 - tap_number % 3) * DILATION_RATE
            + width_columns,
        ].reshape(pixel_count, branch_channel_width)
        for tap_number in range(9)
    ]
    pieces_list = [transposed_product(flattened, pointwise_gradient)]
    for branch_tap_number in range(9):
        pieces_list.append(transposed_product(tap_windows[branch_tap_number], dilated_gradient))
    branch_kernel_gradient = (
        lax.psum_scatter(jnp.stack(pieces_list, axis=1), "row", scatter_dimension=0, tiled=True)
        * gradient_scale
    )
    input_total = ndot(pointwise_gradient, whole_branch[:, 0, :])
    for tap_number in range(9):
        input_total = input_total + ndot(grad_views[tap_number], whole_branch[:, 1 + tap_number, :])
    input_grad = input_total.astype(jnp.bfloat16).reshape(
        block_row_count, width_columns, channel_count
    )
    return (
        merged.reshape(block_row_count, width_columns, merged.shape[1]),
        input_grad,
        branch_kernel_gradient,
        grad_merge,
    )


def solution(mesh):
    placed = (
        P(("grp", "row"), None, None),
        P("row", None, None),
        P(),
        P("row", None),
        P(),
        P(("grp", "row"), None, None),
    )
    return jax.shard_map(
        on_device,
        mesh=mesh,
        in_specs=placed,
        out_specs=(
            P(("grp", "row"), None, None),
            P(("grp", "row"), None, None),
            P(("grp", "row"), None, None),
            P(("grp", "row"), None),
        ),
        check_vma=False,
    )
```

profile of v0, /device:TPU:0, one launch (start us, length us, event | category | flops | bytes accessed | tf_op | source)
XLA Modules:
  0.0 479.2 jit_solution(15988764721342532943)
XLA Ops:
  7.9 4.5 collective-permute-start
  13.7 79.9 %all_gather.7 = bf16[256,256]{1,0:T(8,128)(2,1)S(1)} all-gather(bf16[8,256]{1,0:T(8,128)(2,1)} %param.9), channel_id=1, replica_groups=mesh['grp'=1,'row'=32] {'row'}, dimensions={0}, use_global_device_ids=true | all-gather | bytes 135168 | tf_op jit(solution)/shard_map/all_gather | solution.py:70
  94.4 4.3 pad_slice_fusion.2
  98.7 2.3 pad_slice_fusion.5
  101.0 1.8 pad_slice_fusion.1
  102.8 2.7 fusion.26
  105.5 2.5 fusion.28
  108.1 1.7 fusion.24
  118.9 3.0 fusion.5
  121.9 1.5 fusion.8
  124.8 1.5 fusion.3
  129.1 1.5 fusion.1
  130.9 1.5 fusion.6
  133.8 17.5 %copy.65 = f32[2048,10,128]{2,1,0:T(8,128)} copy(f32[2048,10,128]{0,2,1:T(8,128)} %fusion) | data formatting | bytes 20971520 | tf_op jit(solution)/shard_map/stack | solution.py:126
  152.8 29.3 %collective-permute-start.3 = (bf16[2,192,128]{2,1,0:T(8,128)(2,1)S(1)}, bf16[2,192,128]{2,1,0:T(8,128)(2,1)S(1)}, u32[]{:S(2)}, u32[]{:S(2)}) collective-permute-start(bf16[2,192,128]{2,1,0:T(8,128)(2,1)S(1)} %bitcast.183), channel_id=1, source_target_pairs={{0,9},{1,10},{2,11},{3,12},{4,13},{5,14},{6,15},{7,16},{8,17},{9,1... | collective-permute-start | bytes 294920 | tf_op jit(solution)/shard_map/ppermute | solution.py:14
  182.2 1.8 fusion.29
  184.0 1.7 fusion.27
  185.7 3.3 fusion.21
  190.8 2.3 fusion.31
  193.1 2.3 fusion.23
  195.4 2.3 fusion.32
  197.6 7.9 %add_convert_fusion = bf16[384,2048]{1,0:T(8,128)(2,1)} fusion(f32[384,2048]{1,0:T(8,128)} %fusion.32, f32[384,2048]{1,0:T(8,128)} %fusion.31, f32[384,2048]{1,0:T(8,128)S(1)} %fusion.30, f32[384,2048]{1,0:T(8,128)S(1)} %fusion.29, f32[384,2048]{1,0:T(8,128)S(1)} %fusion.27, f32[384,2048]{1,0:T(8,128)S(1)} %fusion.25, f32[384,2048]{1,0:T(8,128)} %fusion.23, ...), kind=kOutput, calls=%fused_computation | convolution fusion | flops 209190912 | bytes 30507008 | tf_op jit(solution)/shard_map/dot_general | solution.py:24
  205.6 83.9 %reduce-scatter.5.cloned.1.call-done = f32[8,256]{1,0:T(8,128)} async-done(((f32[256,256]{1,0:T(8,128)}), f32[8,256]{1,0:T(8,128)}) %reduce-scatter.5.cloned.1.call-update) | async-done | bytes 8208 | tf_op jit(solution)/shard_map/reduce_scatter | solution.py:92
  290.8 180.0 %reduce-scatter.3.cloned.1.call-done = f32[64,10,128]{2,1,0:T(8,128)} async-done(((f32[2048,10,128]{2,1,0:T(8,128)}), f32[64,10,128]{2,1,0:T(8,128)}) %reduce-scatter.3.cloned.1.call-update) | async-done | bytes 327696 | tf_op jit(solution)/shard_map/reduce_scatter | solution.py:126
  (79 shorter events, 24.2 us)
Async XLA Ops:
  7.2 95.7 %all-gather.2.cloned.1.call-start = ((), (), s32[]{:S(2)}) async-start(), calls=%async_computation.2 | async-start | bytes 5406720 | tf_op jit(solution)/shard_map/all_gather | solution.py:69
  7.9 281.6 %reduce-scatter.5.cloned.1.call-start = ((), (), s32[]{:S(2)}) async-start(), calls=%async_computation.4 | async-start | bytes 270336 | tf_op jit(solution)/shard_map/reduce_scatter | solution.py:92
  7.9 90.7 %collective-permute-start = (bf16[2,192,2048]{2,1,0:T(8,128)(2,1)}, bf16[2,192,2048]{2,1,0:T(8,128)(2,1)S(1)}, u32[]{:S(2)}, u32[]{:S(2)}) collective-permute-start(bf16[2,192,2048]{2,1,0:T(8,128)(2,1)} %param.6), channel_id=1, source_target_pairs={{0,9},{1,10},{2,11},{3,12},{4,13},{5,14},{6,15},{7,16},{8,17},{9,1... | collective-permute-start | bytes 4718600 | tf_op jit(solution)/shard_map/ppermute | solution.py:14
  12.4 88.6 %collective-permute-start.1 = (bf16[2,192,2048]{2,1,0:T(8,128)(2,1)}, bf16[2,192,2048]{2,1,0:T(8,128)(2,1)S(1)}, u32[]{:S(2)}, u32[]{:S(2)}) collective-permute-start(bf16[2,192,2048]{2,1,0:T(8,128)(2,1)} %param.6), channel_id=1, source_target_pairs={{9,0},{10,1},{11,2},{12,3},{13,4},{14,5},{15,6},{16,7},{17,8},{18,... | collective-permute-start | bytes 4718600 | tf_op jit(solution)/shard_map/ppermute | solution.py:14
  93.6 20.8 %copy-start.14 = (bf16[256,256]{1,0:T(8,128)(2,1)}, bf16[256,256]{1,0:T(8,128)(2,1)S(1)}, u32[]{:S(2)}) copy-start(bf16[256,256]{1,0:T(8,128)(2,1)S(1)} %all_gather.7) | copy-start | bytes 393220
  98.7 2.3 copy-start.4
  102.8 7.0 %copy-start.2 = (bf16[2,192,2048]{2,1,0:T(8,128)(2,1)}, bf16[2,192,2048]{2,1,0:T(8,128)(2,1)S(1)}, u32[]{:S(2)}) copy-start(bf16[2,192,2048]{2,1,0:T(8,128)(2,1)S(1)} %get-tuple-element.17) | copy-start | bytes 4718596
  102.8 5.3 %copy-start.5 = (bf16[2,192,2048]{2,1,0:T(8,128)(2,1)S(1)}, bf16[2,192,2048]{2,1,0:T(8,128)(2,1)}, u32[]{:S(2)}) copy-start(bf16[2,192,2048]{2,1,0:T(8,128)(2,1)} %copy-done.4) | copy-start | bytes 4718596
  102.8 7.0 %copy-start.1 = (bf16[2048,10,128]{2,0,1:T(8,128)(2,1)S(1)}, bf16[2048,10,128]{2,0,1:T(8,128)(2,1)}, u32[]{:S(2)}) copy-start(bf16[2048,10,128]{2,0,1:T(8,128)(2,1)} %all-gather.2.cloned.1.call-done) | copy-start | bytes 15728644
  108.1 3.0 copy-start.13
  110.5 1.4 copy-start
  111.1 2.0 copy-start.7
  111.9 1.9 copy-start.10
  118.9 3.0 copy-start.6
  118.9 4.4 copy-start.12
  121.9 2.9 copy-start.9
  124.8 2.9 copy-start.8
  126.2 2.9 copy-start.11
  129.1 3.3 copy-start.3
  130.7 340.1 %reduce-scatter.3.cloned.1.call-start = ((), (), s32[]{:S(2)}) async-start(), calls=%async_computation.3 | async-start | bytes 17301504 | tf_op jit(solution)/shard_map/reduce_scatter | solution.py:126
  151.5 38.1 %collective-permute-start.2 = (bf16[2,192,128]{2,1,0:T(8,128)(2,1)S(1)}, bf16[2,192,128]{2,1,0:T(8,128)(2,1)S(1)}, u32[]{:S(2)}, u32[]{:S(2)}) collective-permute-start(bf16[2,192,128]{2,1,0:T(8,128)(2,1)S(1)} %bitcast.182), channel_id=1, source_target_pairs={{9,0},{10,1},{11,2},{12,3},{13,4},{14,5},{15,6},{16,7},{17,8},{18,... | collective-permute-start | bytes 294920 | tf_op jit(solution)/shard_map/ppermute | solution.py:14
  152.8 36.8 %collective-permute-start.3 = (bf16[2,192,128]{2,1,0:T(8,128)(2,1)S(1)}, bf16[2,192,128]{2,1,0:T(8,128)(2,1)S(1)}, u32[]{:S(2)}, u32[]{:S(2)}) collective-permute-start(bf16[2,192,128]{2,1,0:T(8,128)(2,1)S(1)} %bitcast.183), channel_id=1, source_target_pairs={{0,9},{1,10},{2,11},{3,12},{4,13},{5,14},{6,15},{7,16},{8,17},{9,1... | collective-permute-start | bytes 294920 | tf_op jit(solution)/shard_map/ppermute | solution.py:14
  182.2 6.8 %slice-start = ((s8[5242880]{0:T(1024)(128)(4,1)}), s8[4194304]{0:T(1024)(128)(4,1)S(1)}, s32[]{:S(2)}) async-start(s8[5242880]{0:T(1024)(128)(4,1)} %bitcast.162), calls=%async_computation.5 | async-start | bytes 8388608
  184.0 5.0 %slice-start.1 = ((s8[5242880]{0:T(1024)(128)(4,1)}), s8[1048576]{0:T(1024)(128)(4,1)S(1)}, s32[]{:S(2)}) async-start(s8[5242880]{0:T(1024)(128)(4,1)} %bitcast.162), calls=%async_computation.6 | async-start | bytes 2097152
  (2 other events, 2.5 us)
Sparse Core Ops, SparseCore 0:
  10.9 84.0 all-gather.1
  130.8 158.6 reduce-scatter.4
  291.9 178.8 reduce-scatter.2
where the time goes:
time: 480 us; the launch traced here: 479 us
  waiting for transfers between devices  265 us (55%)
  blocking collectives  79.9 us (17%)
  matrix products  53.5 us (11%)
  starting transfers between devices  36.7 us (8%)
  local copies, waits for them, and re-layouts  28.1 us (6%)
  between operations  14.1 us (3%)
    reduce_scatter x1, waiting for transfers between devices, on_device(): lax.psum_scatter(jnp.stack(pieces_list, axis=1), 'row', scatter_dimension...  180 us
    reduce_scatter x1, waiting for transfers between devices, on_device(): lax.psum_scatter(transposed_product(combined, grad_out), 'row', scatter_d...  83.9 us
    all_gather x1, blocking collectives, on_device(): lax.all_gather(merge_weight, 'row', axis=0, tiled=True)  79.9 us
    ppermute x4, starting transfers between devices, passed_along(): return lax.ppermute(block, axis, route)  36.4 us
    dot_general x11, matrix products, ndot(): lax.dot_general(left, right, (((1,), (1,)), ((), ())), preferred_element_...  24.4 us
    another operation x1, local copies, waits for them, and re-layouts, on_device(): jnp.stack(pieces_list, axis=1)  17.5 us
    dot_general x11, matrix products, transposed_product(): lax.dot_general(left, right, (((0,), (0,)), ((), ())), preferred_element_...  16.9 us
    dot_general x9, matrix products, on_device(): jnp.dot(tap_windows[tap_number], whole_branch[:, 1 + tap_number, :], pref...  10.6 us
  transfers between devices with their start and end apart: 7, of which 2 were waited for; matrix products, arithmetic and copies ran while one was open for 11% of the time, Pallas kernels for 0%

commit v1 on v0

v1 whole, which is shorter than its diff:
```python
import math

import jax
import jax.numpy as jnp
from jax import lax
from jax.sharding import PartitionSpec as P

DILATION_RATE = 18
PORTIONS = ((1, 2, 3), (7, 8, 9), (0, 4, 5, 6))


def passed_along(block, distance):
    devices = range(lax.axis_size("row"))
    route = [(i - distance, i) for i in devices if i - distance in devices]
    return lax.ppermute(block, "row", route)


def exchanged(block, bit):
    return lax.ppermute(block, "row", [(i, i ^ (1 << bit)) for i in range(lax.axis_size("row"))])


def dot_f32(left, right, left_dim, right_dim):
    return lax.dot_general(
        left, right, (((left_dim,), (right_dim,)), ((), ())), preferred_element_type=jnp.float32
    )


def bit_orders(bit_count):
    far = list(range(bit_count - 1, 3, -1))
    near = [b for b in (3, 2, 1) if b < bit_count]
    return [far + near[k:] + near[:k] for k in range(3)]


def axis_of(bit, bit_count):
    return 0 if bit == 0 else bit_count - bit


def gather_blocks(blocks, orders, bit_count):
    for step in range(bit_count):
        arrived = [exchanged(b, o[step]) for b, o in zip(blocks, orders)]
        blocks = [
            jnp.concatenate([b, a], axis=axis_of(o[step], bit_count))
            for b, a, o in zip(blocks, arrived, orders)
        ]
    return blocks


def scatter_block(block, order, bit_count, dtype):
    for bit in order:
        axis = axis_of(bit, bit_count)
        own = lax.slice_in_dim(block, 0, 1, axis=axis)
        other = lax.slice_in_dim(block, 1, 2, axis=axis).astype(dtype)
        block = own + exchanged(other, bit).astype(jnp.float32)
    return block


def relative_order(size, device_count, me):
    width = size // device_count
    target = lax.broadcasted_iota(jnp.int32, (size, size), 1)
    source = lax.broadcasted_iota(jnp.int32, (size, size), 0)
    half = device_count // 2
    block, inner = target // width, target % width
    device = (block % half) * 2 + block // half
    return (source == (device ^ me) * width + inner).astype(jnp.bfloat16)


def column_shifted(rows, shift):
    width = rows.shape[1]
    if shift == 0:
        return rows
    if shift > 0:
        return jnp.pad(rows[:, shift:], ((0, 0), (0, shift), (0, 0)))
    return jnp.pad(rows[:, : width + shift], ((0, 0), (-shift, 0), (0, 0)))


def on_device(
    features, branch_kernel_weight, branch_norm_bias, merge_weight, merge_bias, cotangent
):
    device_count = lax.axis_size("row")
    bit_count = device_count.bit_length() - 1
    me = lax.axis_index("row")
    rows, width, channels = features.shape
    taps, branch = branch_kernel_weight.shape[1:]
    own_channels = branch_kernel_weight.shape[0]
    joined_rows, merged_width = merge_weight.shape
    joined_width = joined_rows * device_count
    pixels = rows * width
    scale = 1.0 / math.sqrt(rows * device_count * width)
    device_step = DILATION_RATE // rows
    bits = (1,) * bit_count
    orders = [o + [0] for o in bit_orders(bit_count)]

    weight = branch_kernel_weight.transpose(1, 0, 2)
    blocks = [
        jnp.concatenate([weight[k] for k in portion], axis=1).reshape(bits + (own_channels, -1))
        for portion in PORTIONS
    ]
    blocks = gather_blocks(blocks, orders, bit_count)
    whole = [b.reshape(channels, b.shape[-1]) for b in blocks]
    (merge_block,) = gather_blocks(
        [merge_weight.reshape(bits + merge_weight.shape)], [list(range(bit_count))], bit_count
    )

    to_relative = relative_order(channels, device_count, me)
    flat = dot_f32(features.reshape(pixels, channels), to_relative, 1, 0).astype(jnp.bfloat16)
    merge_to_relative = relative_order(joined_width, device_count, me)
    whole_merge = dot_f32(
        merge_to_relative, merge_block.reshape(joined_width, merged_width), 1, 0
    ).astype(jnp.bfloat16)

    products = [dot_f32(flat, w, 1, 0) for w in whole]

    def row_sum(parts):
        total = None
        for j, part in enumerate(parts):
            moved = column_shifted(part.reshape(rows, width, branch), (j - 1) * DILATION_RATE)
            total = moved if total is None else total + moved
        return total

    def split(product):
        return [product[:, i * branch : (i + 1) * branch] for i in range(product.shape[1] // branch)]

    above = passed_along(row_sum(split(products[0])), device_step)
    below = passed_along(row_sum(split(products[1])), -device_step)
    centre = split(products[2])
    z_dil = (row_sum(centre[1:]) + above + below).reshape(pixels, branch)
    act_one = jnp.maximum(centre[0] + branch_norm_bias[0], 0.0).astype(jnp.bfloat16)
    act_dil = jnp.maximum(z_dil + branch_norm_bias[1], 0.0).astype(jnp.bfloat16)
    joined = jnp.concatenate([act_one, act_dil], axis=1)
    merged = jnp.maximum(dot_f32(joined, whole_merge, 1, 0) + merge_bias, 0.0).astype(jnp.bfloat16)
    grad_out = jnp.where(
        merged > 0, cotangent.reshape(pixels, merged_width), jnp.zeros((), jnp.bfloat16)
    )
    back = dot_f32(grad_out, whole_merge, 1, 1)
    grad_one = jnp.where(act_one > 0, back[:, :branch], 0.0).astype(jnp.bfloat16)
    grad_dil = jnp.where(act_dil > 0, back[:, branch:], 0.0).astype(jnp.bfloat16)
    grad_map = grad_dil.reshape(rows, width, branch)
    grad_rows = [passed_along(grad_map, -device_step), passed_along(grad_map, device_step), grad_map]

    def shifted_gradients(block):
        return [
            column_shifted(block, (1 - j) * DILATION_RATE).reshape(pixels, branch) for j in range(3)
        ]

    gradients = [
        jnp.concatenate(shifted_gradients(grad_rows[0]), axis=1),
        jnp.concatenate(shifted_gradients(grad_rows[1]), axis=1),
        jnp.concatenate([grad_one] + shifted_gradients(grad_rows[2]), axis=1),
    ]

    joined_relative = dot_f32(joined, merge_to_relative, 1, 0).astype(jnp.bfloat16)
    grad_merge = scatter_block(
        dot_f32(joined_relative, grad_out, 0, 0).reshape(
            (2,) * bit_count + (joined_rows, merged_width)
        ),
        list(range(bit_count)),
        bit_count,
        jnp.float32,
    ).reshape(joined_rows, merged_width) * scale

    weight_gradient = [None] * taps
    for portion, gradient, order in list(zip(PORTIONS, gradients, orders))[::-1]:
        total = dot_f32(flat, gradient, 0, 0).reshape(
            (2,) * bit_count + (own_channels, gradient.shape[1])
        )
        own = scatter_block(total, order[::-1], bit_count, jnp.bfloat16).reshape(own_channels, -1)
        for k, part in zip(portion, split(own)):
            weight_gradient[k] = part
    branch_kernel_gradient = jnp.stack(weight_gradient, axis=1) * scale

    input_total = sum(dot_f32(g, w, 1, 1) for g, w in zip(gradients, whole)).astype(jnp.bfloat16)
    input_grad = dot_f32(input_total, to_relative, 1, 1).astype(jnp.bfloat16)
    return (
        merged.reshape(rows, width, merged_width),
        input_grad.reshape(rows, width, channels),
        branch_kernel_gradient,
        grad_merge,
    )


def solution(mesh):
    placed = (
        P(("grp", "row"), None, None),
        P("row", None, None),
        P(),
        P("row", None),
        P(),
        P(("grp", "row"), None, None),
    )
    return jax.shard_map(
        on_device,
        mesh=mesh,
        in_specs=placed,
        out_specs=(
            P(("grp", "row"), None, None),
            P(("grp", "row"), None, None),
            P(("grp", "row"), None, None),
            P(("grp", "row"), None),
        ),
        check_vma=False,
    )
```

time: 480 us -> 173 us (0.36)
  waiting for transfers between devices: 265 us -> 64.3 us
  blocking collectives: 79.9 us -> 0 us
  matrix products: 53.5 us -> 30.8 us
  starting transfers between devices: 36.7 us -> 58.5 us
  local copies, waits for them, and re-layouts: 28.1 us -> 8.02 us
  between operations: 14.1 us -> 1.81 us
  other arithmetic: 2.42 us -> 8.88 us
    reduce_scatter x2 -> x0, waiting for transfers between devices: 264 us -> none  [the longest x1 180 us: on_device(): lax.psum_scatter(jnp.stack(pieces_list, axis=1), 'row', scatter_dimension...]
    all_gather x1 -> x0, blocking collectives: 79.9 us -> none  [on_device(): lax.all_gather(merge_weight, 'row', axis=0, tiled=True)]
    ppermute x4 -> x44, waiting for transfers between devices: 0.01 us -> 64.3 us  [the longest x40 61.3 us: exchanged(): lax.ppermute(block, 'row', [(i, i ^ 1 << bit) for i in range(lax.axis_siz...]
    dot_general x33 -> x14, matrix products: 53.5 us -> 30.8 us  [dot_f32(): lax.dot_general(left, right, (((left_dim,), (right_dim,)), ((), ())), pre...]
    ppermute x4 -> x44, starting transfers between devices: 36.4 us -> 58.5 us  [the longest x40 47.6 us: exchanged(): lax.ppermute(block, 'row', [(i, i ^ 1 << bit) for i in range(lax.axis_siz...]
    another operation x1, local copies, waits for them, and re-layouts: 17.5 us -> 0.01 us  [on_device(): branch_kernel_gradient = jnp.stack(weight_gradient, axis=1) * scale]
    slice x6 -> x37, local copies, waits for them, and re-layouts: 8.6 us -> 2.85 us  [the longest x20 1.78 us: scatter_block(): other = lax.slice_in_dim(block, 1, 2, axis=axis).astype(dtype)]
    add x0 -> x21, other arithmetic: none -> 5.08 us  [the longest x16 4.91 us: scatter_block(): block = own + exchanged(other, bit).astype(jnp.float32)]
  transfers between devices with their start and end apart: 7 -> 44, of which waited for: 2 -> 20; matrix products, arithmetic and copies ran while one was open for 11% -> 22% of each run, Pallas kernels for 0% -> 0%
where the time goes in v1:
time: 173 us; the launch traced here: 172 us
  waiting for transfers between devices  64.3 us (37%)
  starting transfers between devices  58.5 us (34%)
  matrix products  30.8 us (18%)
  other arithmetic  8.88 us (5%)
  local copies, waits for them, and re-layouts  8.02 us (5%)
  between operations  1.81 us (1%)
    ppermute x40, waiting for transfers between devices, exchanged(): lax.ppermute(block, 'row', [(i, i ^ 1 << bit) for i in range(lax.axis_siz...  61.3 us
    ppermute x40, starting transfers between devices, exchanged(): lax.ppermute(block, 'row', [(i, i ^ 1 << bit) for i in range(lax.axis_siz...  47.6 us
    dot_general x14, matrix products, dot_f32(): lax.dot_general(left, right, (((left_dim,), (right_dim,)), ((), ())), pre...  30.8 us
    ppermute x4, starting transfers between devices, passed_along(): return lax.ppermute(block, 'row', route)  10.9 us
    add x16, other arithmetic, scatter_block(): block = own + exchanged(other, bit).astype(jnp.float32)  4.91 us
  transfers between devices with their start and end apart: 44, of which 20 were waited for; matrix products, arithmetic and copies ran while one was open for 22% of the time, Pallas kernels for 0%

profile of v1, /device:TPU:0, one launch (start us, length us, event | category | flops | bytes accessed | tf_op | source)
XLA Modules:
  0.0 172.3 jit_solution(11357216016409276621)
XLA Ops:
  2.1 3.8 %collective-permute-start.5 = (bf16[1,1,1,1,1,64,384]{6,5,4,3,2,1,0:T(8,128)(2,1)S(1)}, bf16[1,1,1,1,1,64,384]{6,5,4,3,2,1,0:T(8,128)(2,1)S(1)}, u32[]{:S(2)}, u32[]{:S(2)}) collective-permute-start(bf16[1,1,1,1,1,64,384]{6,5,4,3,2,1,0:T(8,128)(2,1)S(1)} %maximum_bitcast_fusion.1), channel_id=1, source_target_pairs={{0,16},{1,17},{2,18},{3,19},{4,20},{5,21},{6,22},{7,23},{8,24},{9,... | collective-permute-start | bytes 147464 | tf_op jit(solution)/shard_map/ppermute | solution.py:19
  5.9 3.0 %collective-permute-start = (bf16[1,1,1,1,1,64,512]{6,5,4,3,2,1,0:T(8,128)(2,1)S(1)}, bf16[1,1,1,1,1,64,512]{6,5,4,3,2,1,0:T(8,128)(2,1)S(1)}, u32[]{:S(2)}, u32[]{:S(2)}) collective-permute-start(bf16[1,1,1,1,1,64,512]{6,5,4,3,2,1,0:T(8,128)(2,1)S(1)} %maximum_bitcast_fusion), channel_id=1, source_target_pairs={{0,16},{1,17},{2,18},{3,19},{4,20},{5,21},{6,22},{7,23},{8,24},{9,... | collective-permute-start | bytes 196616 | tf_op jit(solution)/shard_map/ppermute | solution.py:19
  9.7 5.3 %fusion.12 = bf16[2048,384]{1,0:T(8,128)(2,1)S(1)} fusion(bf16[384,2048]{1,0:T(8,128)(2,1)S(1)} %bitcast.141, s32[2048]{0:T(1024)S(1)} %get-tuple-element.45, s32[2048]{0:T(1024)S(1)} %get-tuple-element.46, s32[]{:T(128)S(6)} %axis_index.12, s32[2048]{0:T(1024)S(1)} %get-tuple-element.44, s32[2048]{0:T(1024)S(1)} %get-tuple-element.47, ...), kind=kOutput, calls=%fused_computation.21 | convolution fusion | flops 3339452416 | bytes 3182596 | tf_op jit(solution)/shard_map/dot_general | solution.py:23
  35.1 3.2 %collective-permute-done.7 = bf16[1,2,2,1,1,64,384]{6,5,4,3,2,1,0:T(8,128)(2,1)S(1)} collective-permute-done((bf16[1,2,2,1,1,64,384]{6,5,4,3,2,1,0:T(8,128)(2,1)S(1)}, bf16[1,2,2,1,1,64,384]{6,5,4,3,2,1,0:T(8,128)(2,1)S(1)}, u32[]{:S(2)}, u32[]{:S(2)}) %collective-permute-start.7) | collective-permute-done | bytes 196640 | tf_op jit(solution)/shard_map/ppermute | solution.py:19
  39.9 3.5 %collective-permute-done.14 = bf16[1,2,1,2,2,64,384]{6,5,4,3,2,1,0:T(8,128)(2,1)S(1)} collective-permute-done((bf16[1,2,1,2,2,64,384]{6,5,4,3,2,1,0:T(8,128)(2,1)S(1)}, bf16[1,2,1,2,2,64,384]{6,5,4,3,2,1,0:T(8,128)(2,1)S(1)}, u32[]{:S(2)}, u32[]{:S(2)}) %collective-permute-start.14) | collective-permute-done | bytes 393248 | tf_op jit(solution)/shard_map/ppermute | solution.py:19
  43.6 2.6 %collective-permute-done.2 = bf16[1,2,1,1,2,64,512]{6,5,4,3,2,1,0:T(8,128)(2,1)S(1)} collective-permute-done((bf16[1,2,1,1,2,64,512]{6,5,4,3,2,1,0:T(8,128)(2,1)S(1)}, bf16[1,2,1,1,2,64,512]{6,5,4,3,2,1,0:T(8,128)(2,1)S(1)}, u32[]{:S(2)}, u32[]{:S(2)}) %collective-permute-start.2) | collective-permute-done | bytes 262176 | tf_op jit(solution)/shard_map/ppermute | solution.py:19
  47.2 10.8 %collective-permute-done.3 = bf16[1,2,2,1,2,64,512]{6,5,4,3,2,1,0:T(8,128)(2,1)S(1)} collective-permute-done((bf16[1,2,2,1,2,64,512]{6,5,4,3,2,1,0:T(8,128)(2,1)S(1)}, bf16[1,2,2,1,2,64,512]{6,5,4,3,2,1,0:T(8,128)(2,1)S(1)}, u32[]{:S(2)}, u32[]{:S(2)}) %collective-permute-start.3) | collective-permute-done | bytes 524320 | tf_op jit(solution)/shard_map/ppermute | solution.py:19
  62.3 4.3 %collective-permute-start.10 = (f32[2,192,128]{2,1,0:T(8,128)S(1)}, f32[2,192,128]{2,1,0:T(8,128)S(1)}, u32[]{:S(2)}, u32[]{:S(2)}) collective-permute-start(f32[2,192,128]{2,1,0:T(8,128)S(1)} %pad_add_fusion.1), channel_id=1, source_target_pairs={{0,9},{1,10},{2,11},{3,12},{4,13},{5,14},{6,15},{7,16},{8,17},{9,1... | collective-permute-start | bytes 589832 | tf_op jit(solution)/shard_map/ppermute | solution.py:15
  68.2 3.0 %collective-permute-done.10 = f32[2,192,128]{2,1,0:T(8,128)S(1)} collective-permute-done((f32[2,192,128]{2,1,0:T(8,128)S(1)}, f32[2,192,128]{2,1,0:T(8,128)S(1)}, u32[]{:S(2)}, u32[]{:S(2)}) %collective-permute-start.10) | collective-permute-done | bytes 196640 | tf_op jit(solution)/shard_map/ppermute | solution.py:15
  73.1 2.3 %fusion.19 = f32[256,256]{1,0:T(8,128)} fusion(bf16[384,256]{1,0:T(8,128)(2,1)} %copy-done.10, bf16[384,128]{1,0:T(8,128)(2,1)} %copy-done.12, bf16[384,128]{1,0:T(8,128)(2,1)} %copy-done.8, s32[256]{0:T(256)} %copy-done.25, s32[256]{0:T(256)} %copy-done.22, s32[]{:T(128)S(6)} %axis_index.12, s32[256]{0:T(256)} %copy-done.24, s32[256]{0:T(256)} %copy-done.23, ...), kind=kOutput, calls=%fused_computation.37 | convolution fusion | flops 102924288 | bytes 659972 | tf_op jit(solution)/shard_map/dot_general | solution.py:23
  76.4 3.8 %collective-permute-start.23 = (bf16[2,192,128]{2,1,0:T(8,128)(2,1)S(1)}, bf16[2,192,128]{2,1,0:T(8,128)(2,1)S(1)}, u32[]{:S(2)}, u32[]{:S(2)}) collective-permute-start(bf16[2,192,128]{2,1,0:T(8,128)(2,1)S(1)} %bitcast.151), channel_id=1, source_target_pairs={{0,9},{1,10},{2,11},{3,12},{4,13},{5,14},{6,15},{7,16},{8,17},{9,1... | collective-permute-start | bytes 294920 | tf_op jit(solution)/shard_map/ppermute | solution.py:15
  81.8 4.3 %fusion.43 = f32[384,2048]{1,0:T(8,128)} fusion(bf16[2048,512]{1,0:T(8,128)(2,1)} %bitcast.148, bf16[384,128]{1,0:T(8,128)(2,1)S(1)} %bitcast.162, bf16[384,128]{1,0:T(8,128)(2,1)S(1)} %get-tuple-element.17, bf16[384,128]{1,0:T(8,128)(2,1)S(1)} %bitcast.160, bf16[384,128]{1,0:T(8,128)(2,1)S(1)} %get-tuple-element.16), kind=kOutput, calls=%fused_computation.120 | convolution fusion | flops 806879232 | bytes 5636096 | tf_op jit(solution)/shard_map/dot_general | solution.py:23
  89.7 2.2 %collective-permute-start.39 = (f32[1,2,2,2,2,8,256]{6,5,4,3,2,1,0:T(8,128)S(1)}, f32[1,2,2,2,2,8,256]{6,5,4,3,2,1,0:T(8,128)S(1)}, u32[]{:S(2)}, u32[]{:S(2)}) collective-permute-start(f32[1,2,2,2,2,8,256]{6,5,4,3,2,1,0:T(8,128)S(1)} %bitcast.184), channel_id=1, source_target_pairs={{0,1},{1,0},{2,3},{3,2},{4,5},{5,4},{6,7},{7,6},{8,9},{9,8},{10,11... | collective-permute-start | bytes 393224 | tf_op jit(solution)/shard_map/ppermute | solution.py:19
  92.1 2.7 %fusion.38 = f32[384,2048]{1,0:T(8,128)} fusion(bf16[2048,384]{1,0:T(8,128)(2,1)S(1)} %bitcast.146, bf16[384,128]{1,0:T(8,128)(2,1)S(1)} %bitcast.158, bf16[384,128]{1,0:T(8,128)(2,1)S(1)} %bitcast.154, bf16[384,128]{1,0:T(8,128)(2,1)S(1)} %bitcast.156), kind=kOutput, calls=%fused_computation.109 | convolution fusion | flops 604864512 | bytes 5013504 | tf_op jit(solution)/shard_map/dot_general | solution.py:23
  103.7 3.4 %collective-permute-start.42 = (f32[1,2,1,1,1,8,256]{6,5,4,3,2,1,0:T(8,128)S(1)}, f32[1,2,1,1,1,8,256]{6,5,4,3,2,1,0:T(8,128)S(1)}, u32[]{:S(2)}, u32[]{:S(2)}) collective-permute-start(f32[1,2,1,1,1,8,256]{6,5,4,3,2,1,0:T(8,128)S(1)} %slice.463), channel_id=1, source_target_pairs={{0,8},{1,9},{2,10},{3,11},{4,12},{5,13},{6,14},{7,15},{8,0},{9,1},... | collective-permute-start | bytes 49160 | tf_op jit(solution)/shard_map/ppermute | solution.py:19
  109.9 5.5 %collective-permute-start.43 = (f32[1,1,1,1,1,8,256]{6,5,4,3,2,1,0:T(8,128)S(1)}, f32[1,1,1,1,1,8,256]{6,5,4,3,2,1,0:T(8,128)S(1)}, u32[]{:S(2)}, u32[]{:S(2)}) collective-permute-start(f32[1,1,1,1,1,8,256]{6,5,4,3,2,1,0:T(8,128)S(1)} %slice.465), channel_id=1, source_target_pairs={{0,16},{1,17},{2,18},{3,19},{4,20},{5,21},{6,22},{7,23},{8,24},{9,... | collective-permute-start | bytes 24584 | tf_op jit(solution)/shard_map/ppermute | solution.py:19
  115.4 8.5 %convolution_convert_fusion = bf16[384,2048]{1,0:T(8,128)(2,1)} fusion(f32[384,2048]{1,0:T(8,128)} %fusion.43, f32[384,2048]{1,0:T(8,128)} %fusion.38, bf16[2048,384]{1,0:T(8,128)(2,1)S(1)} %bitcast.150, bf16[384,128]{1,0:T(8,128)(2,1)S(1)} %bitcast.181, bf16[384,128]{1,0:T(8,128)(2,1)S(1)} %bitcast.165, bf16[384,128]{1,0:T(8,128)(2,1)S(1)} %bitcast.179, ...), kind=kOutput, calls=%fused_computation.22 | convolution fusion | flops 3942481920 | bytes 9768964 | tf_op jit(solution)/shard_map/dot_general | solution.py:23
  131.1 7.0 %collective-permute-done.30 = bf16[1,2,2,2,1,64,384]{6,5,4,3,2,1,0:T(8,128)(2,1)S(1)} collective-permute-done((bf16[1,2,2,2,1,64,384]{6,5,4,3,2,1,0:T(8,128)(2,1)S(1)}, bf16[1,2,2,2,1,64,384]{6,5,4,3,2,1,0:T(8,128)(2,1)S(1)}, u32[]{:S(2)}, u32[]{:S(2)}) %collective-permute-start.30) | collective-permute-done | bytes 393248 | tf_op jit(solution)/shard_map/ppermute | solution.py:19
  141.4 7.1 %collective-permute-done.31 = bf16[1,2,2,1,1,64,384]{6,5,4,3,2,1,0:T(8,128)(2,1)S(1)} collective-permute-done((bf16[1,2,2,1,1,64,384]{6,5,4,3,2,1,0:T(8,128)(2,1)S(1)}, bf16[1,2,2,1,1,64,384]{6,5,4,3,2,1,0:T(8,128)(2,1)S(1)}, u32[]{:S(2)}, u32[]{:S(2)}) %collective-permute-start.31) | collective-permute-done | bytes 196640 | tf_op jit(solution)/shard_map/ppermute | solution.py:19
  151.4 2.7 %collective-permute-done.32 = bf16[1,2,1,1,1,64,384]{6,5,4,3,2,1,0:T(8,128)(2,1)S(1)} collective-permute-done((bf16[1,2,1,1,1,64,384]{6,5,4,3,2,1,0:T(8,128)(2,1)S(1)}, bf16[1,2,1,1,1,64,384]{6,5,4,3,2,1,0:T(8,128)(2,1)S(1)}, u32[]{:S(2)}, u32[]{:S(2)}) %collective-permute-start.32) | collective-permute-done | bytes 98336 | tf_op jit(solution)/shard_map/ppermute | solution.py:19
  155.1 2.2 %collective-permute-start.38 = (bf16[1,1,1,1,1,64,384]{6,5,4,3,2,1,0:T(8,128)(2,1)S(1)}, bf16[1,1,1,1,1,64,384]{6,5,4,3,2,1,0:T(8,128)(2,1)S(1)}, u32[]{:S(2)}, u32[]{:S(2)}) collective-permute-start(bf16[1,1,1,1,1,64,384]{6,5,4,3,2,1,0:T(8,128)(2,1)S(1)} %slice.573), channel_id=1, source_target_pairs={{0,16},{1,17},{2,18},{3,19},{4,20},{5,21},{6,22},{7,23},{8,24},{9,... | collective-permute-start | bytes 147464 | tf_op jit(solution)/shard_map/ppermute | solution.py:19
  157.2 3.7 %collective-permute-done.26 = bf16[1,2,1,1,2,64,512]{6,5,4,3,2,1,0:T(8,128)(2,1)S(1)} collective-permute-done((bf16[1,2,1,1,2,64,512]{6,5,4,3,2,1,0:T(8,128)(2,1)S(1)}, bf16[1,2,1,1,2,64,512]{6,5,4,3,2,1,0:T(8,128)(2,1)S(1)}, u32[]{:S(2)}, u32[]{:S(2)}) %collective-permute-start.26) | collective-permute-done | bytes 262176 | tf_op jit(solution)/shard_map/ppermute | solution.py:19
  162.6 3.5 %collective-permute-done.27 = bf16[1,2,1,1,1,64,512]{6,5,4,3,2,1,0:T(8,128)(2,1)S(1)} collective-permute-done((bf16[1,2,1,1,1,64,512]{6,5,4,3,2,1,0:T(8,128)(2,1)S(1)}, bf16[1,2,1,1,1,64,512]{6,5,4,3,2,1,0:T(8,128)(2,1)S(1)}, u32[]{:S(2)}, u32[]{:S(2)}) %collective-permute-start.27) | collective-permute-done | bytes 131104 | tf_op jit(solution)/shard_map/ppermute | solution.py:19
  166.3 5.1 %collective-permute-done.28 = bf16[1,1,1,1,1,64,512]{6,5,4,3,2,1,0:T(8,128)(2,1)S(1)} collective-permute-done((bf16[1,1,1,1,1,64,512]{6,5,4,3,2,1,0:T(8,128)(2,1)S(1)}, bf16[1,1,1,1,1,64,512]{6,5,4,3,2,1,0:T(8,128)(2,1)S(1)}, u32[]{:S(2)}, u32[]{:S(2)}) %collective-permute-start.28) | collective-permute-done | bytes 65568 | tf_op jit(solution)/shard_map/ppermute | solution.py:19
  (249 shorter events, 67.1 us)
Async XLA Ops:
  0.6 14.4 %collective-permute-start.17 = (bf16[1,1,1,1,1,8,256]{6,5,4,3,2,1,0:T(8,128)(2,1)}, bf16[1,1,1,1,1,8,256]{6,5,4,3,2,1,0:T(8,128)(2,1)S(1)}, u32[]{:S(2)}, u32[]{:S(2)}) collective-permute-start(bf16[1,1,1,1,1,8,256]{6,5,4,3,2,1,0:T(8,128)(2,1)} %bitcast.185), channel_id=1, source_target_pairs={{0,1},{1,0},{2,3},{3,2},{4,5},{5,4},{6,7},{7,6},{8,9},{9,8},{10,11... | collective-permute-start | bytes 12296 | tf_op jit(solution)/shard_map/ppermute | solution.py:19
  2.1 24.6 %collective-permute-start.5 = (bf16[1,1,1,1,1,64,384]{6,5,4,3,2,1,0:T(8,128)(2,1)S(1)}, bf16[1,1,1,1,1,64,384]{6,5,4,3,2,1,0:T(8,128)(2,1)S(1)}, u32[]{:S(2)}, u32[]{:S(2)}) collective-permute-start(bf16[1,1,1,1,1,64,384]{6,5,4,3,2,1,0:T(8,128)(2,1)S(1)} %maximum_bitcast_fusion.1), channel_id=1, source_target_pairs={{0,16},{1,17},{2,18},{3,19},{4,20},{5,21},{6,22},{7,23},{8,24},{9,... | collective-permute-start | bytes 147464 | tf_op jit(solution)/shard_map/ppermute | solution.py:19
  5.8 14.5 %collective-permute-start.11 = (bf16[1,1,1,1,1,64,384]{6,5,4,3,2,1,0:T(8,128)(2,1)S(1)}, bf16[1,1,1,1,1,64,384]{6,5,4,3,2,1,0:T(8,128)(2,1)S(1)}, u32[]{:S(2)}, u32[]{:S(2)}) collective-permute-start(bf16[1,1,1,1,1,64,384]{6,5,4,3,2,1,0:T(8,128)(2,1)S(1)} %maximum_bitcast_fusion.2), channel_id=1, source_target_pairs={{0,16},{1,17},{2,18},{3,19},{4,20},{5,21},{6,22},{7,23},{8,24},{9,... | collective-permute-start | bytes 147464 | tf_op jit(solution)/shard_map/ppermute | solution.py:19
  5.9 22.4 %collective-permute-start = (bf16[1,1,1,1,1,64,512]{6,5,4,3,2,1,0:T(8,128)(2,1)S(1)}, bf16[1,1,1,1,1,64,512]{6,5,4,3,2,1,0:T(8,128)(2,1)S(1)}, u32[]{:S(2)}, u32[]{:S(2)}) collective-permute-start(bf16[1,1,1,1,1,64,512]{6,5,4,3,2,1,0:T(8,128)(2,1)S(1)} %maximum_bitcast_fusion), channel_id=1, source_target_pairs={{0,16},{1,17},{2,18},{3,19},{4,20},{5,21},{6,22},{7,23},{8,24},{9,... | collective-permute-start | bytes 196616 | tf_op jit(solution)/shard_map/ppermute | solution.py:19
  22.6 12.1 %collective-permute-start.20 = (bf16[2,1,1,2,2,8,256]{6,5,4,3,2,1,0:T(8,128)(2,1)S(1)}, bf16[2,1,1,2,2,8,256]{6,5,4,3,2,1,0:T(8,128)(2,1)S(1)}, u32[]{:S(2)}, u32[]{:S(2)}) collective-permute-start(bf16[2,1,1,2,2,8,256]{6,5,4,3,2,1,0:T(8,128)(2,1)S(1)} %pad_maximum_fusion.31), channel_id=1, source_target_pairs={{0,8},{1,9},{2,10},{3,11},{4,12},{5,13},{6,14},{7,15},{8,0},{9,1},... | collective-permute-start | bytes 98312 | tf_op jit(solution)/shard_map/ppermute | solution.py:19
  31.0 12.4 %collective-permute-start.14 = (bf16[1,2,1,2,2,64,384]{6,5,4,3,2,1,0:T(8,128)(2,1)S(1)}, bf16[1,2,1,2,2,64,384]{6,5,4,3,2,1,0:T(8,128)(2,1)S(1)}, u32[]{:S(2)}, u32[]{:S(2)}) collective-permute-start(bf16[1,2,1,2,2,64,384]{6,5,4,3,2,1,0:T(8,128)(2,1)S(1)} %pad_maximum_fusion.8), channel_id=1, source_target_pairs={{0,8},{1,9},{2,10},{3,11},{4,12},{5,13},{6,14},{7,15},{8,0},{9,1},... | collective-permute-start | bytes 1179656 | tf_op jit(solution)/shard_map/ppermute | solution.py:19
  33.4 12.8 %collective-permute-start.2 = (bf16[1,2,1,1,2,64,512]{6,5,4,3,2,1,0:T(8,128)(2,1)S(1)}, bf16[1,2,1,1,2,64,512]{6,5,4,3,2,1,0:T(8,128)(2,1)S(1)}, u32[]{:S(2)}, u32[]{:S(2)}) collective-permute-start(bf16[1,2,1,1,2,64,512]{6,5,4,3,2,1,0:T(8,128)(2,1)S(1)} %pad_maximum_fusion.12), channel_id=1, source_target_pairs={{0,8},{1,9},{2,10},{3,11},{4,12},{5,13},{6,14},{7,15},{8,0},{9,1},... | collective-permute-start | bytes 786440 | tf_op jit(solution)/shard_map/ppermute | solution.py:19
  34.7 12.1 %collective-permute-start.21 = (bf16[2,1,2,2,2,8,256]{6,5,4,3,2,1,0:T(8,128)(2,1)S(1)}, bf16[2,1,2,2,2,8,256]{6,5,4,3,2,1,0:T(8,128)(2,1)S(1)}, u32[]{:S(2)}, u32[]{:S(2)}) collective-permute-start(bf16[2,1,2,2,2,8,256]{6,5,4,3,2,1,0:T(8,128)(2,1)S(1)} %pad_maximum_fusion.30), channel_id=1, source_target_pairs={{0,16},{1,17},{2,18},{3,19},{4,20},{5,21},{6,22},{7,23},{8,24},{9,... | collective-permute-start | bytes 196616 | tf_op jit(solution)/shard_map/ppermute | solution.py:19
  43.5 14.7 %collective-permute-start.15 = (bf16[1,2,2,2,2,64,384]{6,5,4,3,2,1,0:T(8,128)(2,1)S(1)}, bf16[1,2,2,2,2,64,384]{6,5,4,3,2,1,0:T(8,128)(2,1)S(1)}, u32[]{:S(2)}, u32[]{:S(2)}) collective-permute-start(bf16[1,2,2,2,2,64,384]{6,5,4,3,2,1,0:T(8,128)(2,1)S(1)} %pad_maximum_fusion.5), channel_id=1, source_target_pairs={{0,1},{1,0},{2,3},{3,2},{4,5},{5,4},{6,7},{7,6},{8,9},{9,8},{10,11... | collective-permute-start | bytes 2359304 | tf_op jit(solution)/shard_map/ppermute | solution.py:19
  46.2 11.8 %collective-permute-start.3 = (bf16[1,2,2,1,2,64,512]{6,5,4,3,2,1,0:T(8,128)(2,1)S(1)}, bf16[1,2,2,1,2,64,512]{6,5,4,3,2,1,0:T(8,128)(2,1)S(1)}, u32[]{:S(2)}, u32[]{:S(2)}) collective-permute-start(bf16[1,2,2,1,2,64,512]{6,5,4,3,2,1,0:T(8,128)(2,1)S(1)} %pad_maximum_fusion.6), channel_id=1, source_target_pairs={{0,4},{1,5},{2,6},{3,7},{4,0},{5,1},{6,2},{7,3},{8,12},{9,13},{10,... | collective-permute-start | bytes 1572872 | tf_op jit(solution)/shard_map/ppermute | solution.py:19
  47.1 13.8 %collective-permute-start.9 = (bf16[1,2,2,2,2,64,384]{6,5,4,3,2,1,0:T(8,128)(2,1)S(1)}, bf16[1,2,2,2,2,64,384]{6,5,4,3,2,1,0:T(8,128)(2,1)S(1)}, u32[]{:S(2)}, u32[]{:S(2)}) collective-permute-start(bf16[1,2,2,2,2,64,384]{6,5,4,3,2,1,0:T(8,128)(2,1)S(1)} %pad_maximum_fusion.4), channel_id=1, source_target_pairs={{0,1},{1,0},{2,3},{3,2},{4,5},{5,4},{6,7},{7,6},{8,9},{9,8},{10,11... | collective-permute-start | bytes 2359304 | tf_op jit(solution)/shard_map/ppermute | solution.py:19
  76.4 15.6 %collective-permute-start.23 = (bf16[2,192,128]{2,1,0:T(8,128)(2,1)S(1)}, bf16[2,192,128]{2,1,0:T(8,128)(2,1)S(1)}, u32[]{:S(2)}, u32[]{:S(2)}) collective-permute-start(bf16[2,192,128]{2,1,0:T(8,128)(2,1)S(1)} %bitcast.151), channel_id=1, source_target_pairs={{0,9},{1,10},{2,11},{3,12},{4,13},{5,14},{6,15},{7,16},{8,17},{9,1... | collective-permute-start | bytes 294920 | tf_op jit(solution)/shard_map/ppermute | solution.py:15
  80.2 21.6 %collective-permute-start.22 = (bf16[2,192,128]{2,1,0:T(8,128)(2,1)S(1)}, bf16[2,192,128]{2,1,0:T(8,128)(2,1)S(1)}, u32[]{:S(2)}, u32[]{:S(2)}) collective-permute-start(bf16[2,192,128]{2,1,0:T(8,128)(2,1)S(1)} %bitcast.152), channel_id=1, source_target_pairs={{9,0},{10,1},{11,2},{12,3},{13,4},{14,5},{15,6},{16,7},{17,8},{18,... | collective-permute-start | bytes 294920 | tf_op jit(solution)/shard_map/ppermute | solution.py:15
  92.0 37.3 %collective-permute-start.24 = (bf16[1,2,2,2,2,64,512]{6,5,4,3,2,1,0:T(8,128)(2,1)}, bf16[1,2,2,2,2,64,512]{6,5,4,3,2,1,0:T(8,128)(2,1)}, u32[]{:S(2)}, u32[]{:S(2)}) collective-permute-start(bf16[1,2,2,2,2,64,512]{6,5,4,3,2,1,0:T(8,128)(2,1)} %bitcast.45), channel_id=1, source_target_pairs={{0,1},{1,0},{2,3},{3,2},{4,5},{5,4},{6,7},{7,6},{8,9},{9,8},{10,11... | collective-permute-start | bytes 3145736 | tf_op jit(solution)/shard_map/ppermute | solution.py:19
  108.4 16.1 %collective-permute-start.29 = (bf16[1,2,2,2,2,64,384]{6,5,4,3,2,1,0:T(8,128)(2,1)S(1)}, bf16[1,2,2,2,2,64,384]{6,5,4,3,2,1,0:T(8,128)(2,1)}, u32[]{:S(2)}, u32[]{:S(2)}) collective-permute-start(bf16[1,2,2,2,2,64,384]{6,5,4,3,2,1,0:T(8,128)(2,1)S(1)} %bitcast.167), channel_id=1, source_target_pairs={{0,1},{1,0},{2,3},{3,2},{4,5},{5,4},{6,7},{7,6},{8,9},{9,8},{10,11... | collective-permute-start | bytes 2359304 | tf_op jit(solution)/shard_map/ppermute | solution.py:19
  109.9 16.9 %collective-permute-start.34 = (bf16[1,2,2,2,2,64,384]{6,5,4,3,2,1,0:T(8,128)(2,1)S(1)}, bf16[1,2,2,2,2,64,384]{6,5,4,3,2,1,0:T(8,128)(2,1)}, u32[]{:S(2)}, u32[]{:S(2)}) collective-permute-start(bf16[1,2,2,2,2,64,384]{6,5,4,3,2,1,0:T(8,128)(2,1)S(1)} %bitcast.166), channel_id=1, source_target_pairs={{0,1},{1,0},{2,3},{3,2},{4,5},{5,4},{6,7},{7,6},{8,9},{9,8},{10,11... | collective-permute-start | bytes 2359304 | tf_op jit(solution)/shard_map/ppermute | solution.py:19
  109.9 14.0 %collective-permute-start.43 = (f32[1,1,1,1,1,8,256]{6,5,4,3,2,1,0:T(8,128)S(1)}, f32[1,1,1,1,1,8,256]{6,5,4,3,2,1,0:T(8,128)S(1)}, u32[]{:S(2)}, u32[]{:S(2)}) collective-permute-start(f32[1,1,1,1,1,8,256]{6,5,4,3,2,1,0:T(8,128)S(1)} %slice.465), channel_id=1, source_target_pairs={{0,16},{1,17},{2,18},{3,19},{4,20},{5,21},{6,22},{7,23},{8,24},{9,... | collective-permute-start | bytes 24584 | tf_op jit(solution)/shard_map/ppermute | solution.py:19
  126.7 11.3 %collective-permute-start.30 = (bf16[1,2,2,2,1,64,384]{6,5,4,3,2,1,0:T(8,128)(2,1)S(1)}, bf16[1,2,2,2,1,64,384]{6,5,4,3,2,1,0:T(8,128)(2,1)S(1)}, u32[]{:S(2)}, u32[]{:S(2)}) collective-permute-start(bf16[1,2,2,2,1,64,384]{6,5,4,3,2,1,0:T(8,128)(2,1)S(1)} %slice.565), channel_id=1, source_target_pairs={{0,2},{1,3},{2,0},{3,1},{4,6},{5,7},{6,4},{7,5},{8,10},{9,11},{10,... | collective-permute-start | bytes 1179656 | tf_op jit(solution)/shard_map/ppermute | solution.py:19
  128.3 11.3 %collective-permute-start.35 = (bf16[1,2,1,2,2,64,384]{6,5,4,3,2,1,0:T(8,128)(2,1)S(1)}, bf16[1,2,1,2,2,64,384]{6,5,4,3,2,1,0:T(8,128)(2,1)S(1)}, u32[]{:S(2)}, u32[]{:S(2)}) collective-permute-start(bf16[1,2,1,2,2,64,384]{6,5,4,3,2,1,0:T(8,128)(2,1)S(1)} %slice.564), channel_id=1, source_target_pairs={{0,8},{1,9},{2,10},{3,11},{4,12},{5,13},{6,14},{7,15},{8,0},{9,1},... | collective-permute-start | bytes 1179656 | tf_op jit(solution)/shard_map/ppermute | solution.py:19
  131.0 19.7 %collective-permute-start.25 = (bf16[1,2,2,1,2,64,512]{6,5,4,3,2,1,0:T(8,128)(2,1)S(1)}, bf16[1,2,2,1,2,64,512]{6,5,4,3,2,1,0:T(8,128)(2,1)S(1)}, u32[]{:S(2)}, u32[]{:S(2)}) collective-permute-start(bf16[1,2,2,1,2,64,512]{6,5,4,3,2,1,0:T(8,128)(2,1)S(1)} %slice.563), channel_id=1, source_target_pairs={{0,4},{1,5},{2,6},{3,7},{4,0},{5,1},{6,2},{7,3},{8,12},{9,13},{10,... | collective-permute-start | bytes 1572872 | tf_op jit(solution)/shard_map/ppermute | solution.py:19
  138.2 10.4 %collective-permute-start.31 = (bf16[1,2,2,1,1,64,384]{6,5,4,3,2,1,0:T(8,128)(2,1)S(1)}, bf16[1,2,2,1,1,64,384]{6,5,4,3,2,1,0:T(8,128)(2,1)S(1)}, u32[]{:S(2)}, u32[]{:S(2)}) collective-permute-start(bf16[1,2,2,1,1,64,384]{6,5,4,3,2,1,0:T(8,128)(2,1)S(1)} %slice.568), channel_id=1, source_target_pairs={{0,4},{1,5},{2,6},{3,7},{4,0},{5,1},{6,2},{7,3},{8,12},{9,13},{10,... | collective-permute-start | bytes 589832 | tf_op jit(solution)/shard_map/ppermute | solution.py:19
  139.7 10.6 %collective-permute-start.36 = (bf16[1,2,1,2,1,64,384]{6,5,4,3,2,1,0:T(8,128)(2,1)S(1)}, bf16[1,2,1,2,1,64,384]{6,5,4,3,2,1,0:T(8,128)(2,1)S(1)}, u32[]{:S(2)}, u32[]{:S(2)}) collective-permute-start(bf16[1,2,1,2,1,64,384]{6,5,4,3,2,1,0:T(8,128)(2,1)S(1)} %slice.567), channel_id=1, source_target_pairs={{0,2},{1,3},{2,0},{3,1},{4,6},{5,7},{6,4},{7,5},{8,10},{9,11},{10,... | collective-permute-start | bytes 589832 | tf_op jit(solution)/shard_map/ppermute | solution.py:19
  150.9 10.1 %collective-permute-start.26 = (bf16[1,2,1,1,2,64,512]{6,5,4,3,2,1,0:T(8,128)(2,1)S(1)}, bf16[1,2,1,1,2,64,512]{6,5,4,3,2,1,0:T(8,128)(2,1)S(1)}, u32[]{:S(2)}, u32[]{:S(2)}) collective-permute-start(bf16[1,2,1,1,2,64,512]{6,5,4,3,2,1,0:T(8,128)(2,1)S(1)} %slice.566), channel_id=1, source_target_pairs={{0,8},{1,9},{2,10},{3,11},{4,12},{5,13},{6,14},{7,15},{8,0},{9,1},... | collective-permute-start | bytes 786440 | tf_op jit(solution)/shard_map/ppermute | solution.py:19
  155.1 11.2 %collective-permute-start.38 = (bf16[1,1,1,1,1,64,384]{6,5,4,3,2,1,0:T(8,128)(2,1)S(1)}, bf16[1,1,1,1,1,64,384]{6,5,4,3,2,1,0:T(8,128)(2,1)S(1)}, u32[]{:S(2)}, u32[]{:S(2)}) collective-permute-start(bf16[1,1,1,1,1,64,384]{6,5,4,3,2,1,0:T(8,128)(2,1)S(1)} %slice.573), channel_id=1, source_target_pairs={{0,16},{1,17},{2,18},{3,19},{4,20},{5,21},{6,22},{7,23},{8,24},{9,... | collective-permute-start | bytes 147464 | tf_op jit(solution)/shard_map/ppermute | solution.py:19
  (53 other events, 460.7 us)

commit v2 on v1

v2 whole, which is shorter than its diff:
```python
import functools
import math

import jax
import jax.numpy as jnp
from jax import lax
from jax.experimental import pallas as pl
from jax.experimental.pallas import tpu as pltpu
from jax.sharding import PartitionSpec as P

DILATION_RATE = 18
LANES = 128
PORTIONS = ((1, 2, 3), (7, 8, 9), (0, 4, 5, 6))


def passed_along(block, distance):
    devices = range(lax.axis_size("row"))
    route = [(i - distance, i) for i in devices if i - distance in devices]
    return lax.ppermute(block, "row", route)


def exchanged(block, bit):
    return lax.ppermute(block, "row", [(i, i ^ (1 << bit)) for i in range(lax.axis_size("row"))])


def dot_f32(left, right, left_dim, right_dim):
    return lax.dot_general(
        left, right, (((left_dim,), (right_dim,)), ((), ())), preferred_element_type=jnp.float32
    )


def bit_orders(bit_count):
    near = [b for b in (3, 2, 1) if b < bit_count]
    return [near[k:] + near[:k] for k in range(3)]


def axis_of(bit, bit_count):
    return bit_count - 1 - bit


def after(value, *others):
    return lax.optimization_barrier((value,) + others)[0]


def together(*values):
    return list(lax.optimization_barrier(values))


def gathered(blocks, crossed, bit_count):
    arrived = together(*[exchanged(b, bit) for b, bit in zip(blocks, crossed)])
    return [
        jnp.concatenate([b, a], axis=axis_of(bit, bit_count))
        for b, a, bit in zip(blocks, arrived, crossed)
    ]


def added(own, arrived, bit, bit_count):
    axis = axis_of(bit, bit_count)

    def half(k):
        parts = [lax.slice_in_dim(x, k, k + 1, axis=axis) for x in (own, arrived)]
        return parts[0] + parts[1].astype(jnp.float32)

    return half(0), half(1).astype(jnp.bfloat16)


def halves(block, bit, bit_count):
    axis = axis_of(bit, bit_count)
    return (
        lax.slice_in_dim(block, 0, 1, axis=axis),
        lax.slice_in_dim(block, 1, 2, axis=axis).astype(jnp.bfloat16),
    )


def relative_order(size, device_count, me):
    width = size // device_count
    target = lax.broadcasted_iota(jnp.int32, (size, size), 1)
    source = lax.broadcasted_iota(jnp.int32, (size, size), 0)
    half = device_count // 2
    block, inner = target // width, target % width
    device = (block % half) * 2 + block // half
    return (source == (device ^ me) * width + inner).astype(jnp.bfloat16)


def reorder_kernel(me_ref, x_ref, own_ref, other_ref):
    me = me_ref[0]
    chip, core = me // 2, me % 2
    lane = lax.broadcasted_iota(jnp.int32, (x_ref.shape[0], LANES), 1)
    low_lane = lane < LANES // 2

    def tile(block):
        start = pl.multiple_of((block ^ chip) * LANES, LANES)
        return x_ref[:, pl.ds(start, LANES)].astype(jnp.float32)

    for t in range(own_ref.shape[1] // LANES):
        first, second = tile(2 * t), tile(2 * t + 1)
        low = jnp.where(low_lane, first, pltpu.roll(second, LANES // 2, 1)).astype(jnp.bfloat16)
        high = jnp.where(low_lane, pltpu.roll(first, LANES // 2, 1), second).astype(jnp.bfloat16)
        columns = slice(t * LANES, (t + 1) * LANES)
        own_ref[:, columns] = jnp.where(core == 0, low, high)
        other_ref[:, columns] = jnp.where(core == 0, high, low)


def reordered(flat, me):
    pixels, channels = flat.shape
    half = jax.ShapeDtypeStruct((pixels, channels // 2), flat.dtype)
    return pl.pallas_call(
        reorder_kernel,
        out_shape=(half, half),
        in_specs=[
            pl.BlockSpec(memory_space=pltpu.SMEM),
            pl.BlockSpec(memory_space=pltpu.VMEM),
        ],
        out_specs=(pl.BlockSpec(memory_space=pltpu.VMEM),) * 2,
        cost_estimate=pl.CostEstimate(
            flops=8 * pixels * channels, bytes_accessed=4 * pixels * channels, transcendentals=0
        ),
        name="reorder",
    )(me.reshape(1), flat)


def kernel_rows_kernel(order, w_ref, out_ref):
    for place, k in enumerate(order):
        out_ref[:, place * LANES : (place + 1) * LANES] = w_ref[k]


def kernel_rows(weight, order):
    taps, rows, branch = weight.shape
    return pl.pallas_call(
        functools.partial(kernel_rows_kernel, order),
        out_shape=jax.ShapeDtypeStruct((rows, taps * branch), weight.dtype),
        in_specs=[pl.BlockSpec(memory_space=pltpu.VMEM)],
        out_specs=pl.BlockSpec(memory_space=pltpu.VMEM),
        cost_estimate=pl.CostEstimate(flops=0, bytes_accessed=4 * weight.size, transcendentals=0),
        name="kernel_rows",
    )(weight)


def input_gradient_kernel(portion_count, me_ref, *refs):
    core = me_ref[0] % 2
    out_ref = refs[-1]
    total = None
    for p in range(portion_count):
        gradient_ref = refs[p]
        first = portion_count + 4 * p
        rows = []
        for k in range(2):
            own, other = refs[first + 2 * k][...], refs[first + 2 * k + 1][...]
            rows += [jnp.where(core == 0, own, other), jnp.where(core == 0, other, own)]
        part = dot_f32(gradient_ref[...], jnp.concatenate(rows, axis=0), 1, 1)
        total = part if total is None else total + part
    out_ref[...] = total.astype(out_ref.dtype)


def input_gradient(gradients, own, other, me):
    pixels = gradients[0].shape[0]
    half = own[0].shape[0]
    rows = LANES // 2
    operands, specs = list(gradients), [
        pl.BlockSpec(g.shape, lambda t, me_ref: (0, 0)) for g in gradients
    ]
    for a, b in zip(own, other):
        for k in range(2):
            for w in (a, b):
                operands.append(w)
                specs.append(
                    pl.BlockSpec(
                        (rows, w.shape[1]),
                        lambda t, me_ref, k=k: ((2 * t + k) ^ (me_ref[0] // 2), 0),
                    )
                )
    columns = sum(g.shape[1] for g in gradients)
    return pl.pallas_call(
        functools.partial(input_gradient_kernel, len(gradients)),
        out_shape=jax.ShapeDtypeStruct((pixels, 2 * half), jnp.bfloat16),
        grid_spec=pltpu.PrefetchScalarGridSpec(
            num_scalar_prefetch=1,
            grid=(half // LANES,),
            in_specs=specs,
            out_specs=pl.BlockSpec((pixels, 2 * LANES), lambda t, me_ref: (0, t)),
        ),
        cost_estimate=pl.CostEstimate(
            flops=4 * pixels * columns * half,
            bytes_accessed=2 * (pixels * columns + 2 * half * columns + 2 * pixels * half),
            transcendentals=0,
        ),
        name="input_gradient",
    )(me.reshape(1), *operands)


def column_shifted(rows, shift):
    width = rows.shape[1]
    if shift == 0:
        return rows
    if shift > 0:
        return jnp.pad(rows[:, shift:], ((0, 0), (0, shift), (0, 0)))
    return jnp.pad(rows[:, : width + shift], ((0, 0), (-shift, 0), (0, 0)))


def on_device(
    features, branch_kernel_weight, branch_norm_bias, merge_weight, merge_bias, cotangent
):
    device_count = lax.axis_size("row")
    bit_count = device_count.bit_length() - 1
    me = lax.axis_index("row")
    rows, width, channels = features.shape
    taps, branch = branch_kernel_weight.shape[1:]
    own_channels = branch_kernel_weight.shape[0]
    joined_rows, merged_width = merge_weight.shape
    joined_width = joined_rows * device_count
    pixels = rows * width
    scale = 1.0 / math.sqrt(rows * device_count * width)
    device_step = DILATION_RATE // rows
    bits = (1,) * (bit_count - 1)
    orders = bit_orders(bit_count)
    far_bits = list(range(bit_count - 1, 3, -1))
    paired = 2 * own_channels == LANES
    portion_widths = [len(p) * branch for p in PORTIONS]

    def split(array, widths):
        starts = [sum(widths[:i]) for i in range(len(widths))]
        return [lax.slice_in_dim(array, s, s + w, axis=-1) for s, w in zip(starts, widths)]

    tap_order = [k for portion in PORTIONS for k in portion]
    weight = branch_kernel_weight.transpose(1, 0, 2)
    if branch == LANES and own_channels % 16 == 0:
        block = kernel_rows(weight, tap_order)
    else:
        block = jnp.concatenate([weight[k] for k in tap_order], axis=1)
    block, flat = together(block, features.reshape(pixels, channels))
    half_rows = channels // 2
    if paired:
        flat_own, flat_other = reordered(flat, me)
    else:
        to_relative = relative_order(channels, device_count, me)
        flat = dot_f32(flat, to_relative, 1, 0).astype(jnp.bfloat16)
        flat_own, flat_other = flat[:, :half_rows], flat[:, half_rows:]
    block = block.reshape(bits + block.shape)
    for bit in far_bits:
        (block,) = gathered([block], [bit], bit_count)
    flat_own, flat_other, merge_block = together(flat_own, flat_other, merge_weight)
    whole_merge = lax.all_to_all(
        jnp.broadcast_to(merge_block[None], (device_count,) + merge_block.shape), "row", 0, 0
    ).reshape(joined_width, merged_width)
    block, flat_own, flat_other = together(block, flat_own, flat_other)
    blocks = split(block, portion_widths)
    for step in range(len(orders[0])):
        if step == 1:
            *blocks, whole_merge = together(*blocks, whole_merge)
        else:
            blocks = together(*blocks)
        blocks = gathered(blocks, [o[step] for o in orders], bit_count)
    own_weight = [b.reshape(half_rows, b.shape[-1]) for b in blocks]

    def row_sum(parts):
        total = None
        for j, part in enumerate(parts):
            moved = column_shifted(part.reshape(rows, width, branch), (j - 1) * DILATION_RATE)
            total = moved if total is None else total + moved
        return total

    def by_tap(product):
        return split(product, [branch] * (product.shape[1] // branch))

    def product(own, other):
        return by_tap(dot_f32(flat_own, own, 1, 0) + dot_f32(flat_other, other, 1, 0))

    other_weight = [exchanged(w, 0) for w in own_weight[:2]]
    sums = [row_sum(product(a, b)) for a, b in zip(own_weight, other_weight)]
    own_weight[2], *sums = together(own_weight[2], *sums)
    other_weight.append(exchanged(own_weight[2], 0))
    centre = product(own_weight[2], other_weight[2])
    above = passed_along(sums[0], device_step)
    below = passed_along(sums[1], -device_step)
    z_dil = (row_sum(centre[1:]) + above + below).reshape(pixels, branch)
    act_one = jnp.maximum(centre[0] + branch_norm_bias[0], 0.0).astype(jnp.bfloat16)
    act_dil = jnp.maximum(z_dil + branch_norm_bias[1], 0.0).astype(jnp.bfloat16)
    joined = jnp.concatenate([act_one, act_dil], axis=1)
    merged = jnp.maximum(dot_f32(joined, whole_merge, 1, 0) + merge_bias, 0.0).astype(jnp.bfloat16)
    grad_out = jnp.where(
        merged > 0, cotangent.reshape(pixels, merged_width), jnp.zeros((), jnp.bfloat16)
    )
    back = dot_f32(grad_out, whole_merge, 1, 1)
    grad_one = jnp.where(act_one > 0, back[:, :branch], 0.0).astype(jnp.bfloat16)
    grad_dil = jnp.where(act_dil > 0, back[:, branch:], 0.0).astype(jnp.bfloat16)
    grad_map = grad_dil.reshape(rows, width, branch)
    halos = [passed_along(grad_map, -device_step), passed_along(grad_map, device_step)]

    def shifted_gradients(block):
        return [
            column_shifted(block, (1 - j) * DILATION_RATE).reshape(pixels, branch) for j in range(3)
        ]

    merge_total = dot_f32(joined, grad_out, 0, 0).astype(jnp.bfloat16)
    gradients = [None] * 3
    own_total, other_total = [None] * 3, [None] * 3
    for p in (2, 0, 1):
        parts = [grad_one] + shifted_gradients(grad_map) if p == 2 else shifted_gradients(halos[p])
        gradients[p] = jnp.concatenate(parts, axis=1)
        if p == 2:
            gradients[p], merge_total = together(gradients[p], merge_total)
            merge_parts = lax.all_to_all(
                merge_total.reshape(device_count, joined_rows, merged_width), "row", 0, 0
            )
        else:
            gradients[p] = lax.optimization_barrier(gradients[p])
        other_total[p] = dot_f32(flat_other, gradients[p], 0, 0).astype(jnp.bfloat16)
        own_total[p] = dot_f32(flat_own, gradients[p], 0, 0)
        if p == 2:
            *halos, own_total[2], other_total[2] = together(*halos, own_total[2], other_total[2])
    other_total = together(*other_total)
    arrived = together(*[exchanged(t, 0) for t in other_total])
    split_shape = (2,) * (bit_count - 1) + (own_channels, -1)
    totals = [
        added(t.reshape(split_shape), a.reshape(split_shape), o[-1], bit_count)
        for t, a, o in zip(own_total, arrived, orders)
    ]
    *sent, g0, g1, g2 = together(*[t[1] for t in totals], *gradients)
    if paired:
        input_grad = input_gradient([g0, g1, g2], own_weight, other_weight, me)
    else:
        input_total = sum(
            dot_f32(g, jnp.concatenate([a, b], axis=0), 1, 1)
            for g, a, b in zip((g0, g1, g2), own_weight, other_weight)
        ).astype(jnp.bfloat16)
        input_grad = dot_f32(input_total, to_relative, 1, 1).astype(jnp.bfloat16)
    for step in range(len(orders[0])):
        arrived = together(*[exchanged(t, o[-1 - step]) for t, o in zip(sent, orders)])
        if step == 0:
            *arrived, input_grad, merge_parts = together(*arrived, input_grad, merge_parts)
        own = [t[0] for t in totals]
        if step + 1 < len(orders[0]):
            totals = [
                added(t, a, o[-2 - step], bit_count) for t, a, o in zip(own, arrived, orders)
            ]
            sent = together(*[t[1] for t in totals])
        else:
            totals = [t + a.astype(jnp.float32) for t, a in zip(own, arrived)]
    grad_merge = jnp.sum(merge_parts.astype(jnp.float32), axis=0) * scale
    total = jnp.concatenate(totals, axis=-1)
    for bit in far_bits[::-1]:
        own, other = halves(total, bit, bit_count)
        total = own + exchanged(other, bit).astype(jnp.float32)
    weight_gradient = dict(
        zip([k for p in PORTIONS for k in p], by_tap(total.reshape(own_channels, -1)))
    )
    branch_kernel_gradient = jnp.stack([weight_gradient[k] for k in range(taps)], axis=1) * scale

    return (
        merged.reshape(rows, width, merged_width),
        input_grad.reshape(rows, width, channels),
        branch_kernel_gradient,
        grad_merge,
    )


def solution(mesh):
    placed = (
        P(("grp", "row"), None, None),
        P("row", None, None),
        P(),
        P("row", None),
        P(),
        P(("grp", "row"), None, None),
    )
    return jax.shard_map(
        on_device,
        mesh=mesh,
        in_specs=placed,
        out_specs=(
            P(("grp", "row"), None, None),
            P(("grp", "row"), None, None),
            P(("grp", "row"), None, None),
            P(("grp", "row"), None),
        ),
        check_vma=False,
    )
```

time: 173 us -> 139 us (0.80)
  matrix products: 30.8 us -> 9.76 us
  Pallas kernels: 0 us -> 13.8 us
  starting transfers between devices: 58.5 us -> 44.9 us
  waiting for transfers between devices: 64.3 us -> 56.5 us
  local copies, waits for them, and re-layouts: 8.02 us -> 3.71 us
    dot_general x14 -> x15, matrix products: 30.8 us -> 9.76 us  [dot_f32(): lax.dot_general(left, right, (((left_dim,), (right_dim,)), ((), ())), pre...]
    ppermute x40 -> x26, waiting for transfers between devices: 61.3 us -> 41.4 us  [exchanged(): lax.ppermute(block, 'row', [(i, i ^ 1 << bit) for i in range(lax.axis_siz...]
    ppermute x40 -> x26, starting transfers between devices: 47.6 us -> 29.8 us  [exchanged(): lax.ppermute(block, 'row', [(i, i ^ 1 << bit) for i in range(lax.axis_siz...]
    pallas_call x0 -> x3, Pallas kernels: none -> 13.8 us  [the longest x1 8.69 us: input_gradient(): pl.pallas_call(functools.partial(input_gradient_kernel, len(gradients)),...]
    all_to_all x0 -> x2, waiting for transfers between devices: none -> 8.1 us  [the longest x1 8.09 us: on_device(): lax.all_to_all(jnp.broadcast_to(merge_block[None], (device_count,) + merg...]
    all_to_all x0 -> x2, starting transfers between devices: none -> 6.19 us  [the longest x1 3.64 us: on_device(): lax.all_to_all(jnp.broadcast_to(merge_block[None], (device_count,) + merg...]
    ppermute x4, waiting for transfers between devices: 2.98 us -> 6.96 us  [passed_along(): return lax.ppermute(block, 'row', route)]
    slice x28 -> x5, local copies, waits for them, and re-layouts: 2.67 us -> 0.13 us  [the longest x4 0.11 us: split(): lax.slice_in_dim(array, s, s + w, axis=-1)]
  transfers between devices with their start and end apart: 44 -> 32, of which waited for: 20 -> 20; matrix products, arithmetic and copies ran while one was open for 22% -> 5% of each run, Pallas kernels for 0% -> 9%
where the time goes in v2:
time: 139 us; the launch traced here: 138 us
  waiting for transfers between devices  56.5 us (41%)
  starting transfers between devices  44.9 us (32%)
  Pallas kernels  13.8 us (10%)
  matrix products  9.76 us (7%)
  other arithmetic  8.28 us (6%)
  local copies, waits for them, and re-layouts  3.71 us (3%)
  between operations  1.42 us (1%)
    ppermute x26, waiting for transfers between devices, exchanged(): lax.ppermute(block, 'row', [(i, i ^ 1 << bit) for i in range(lax.axis_siz...  41.4 us
    ppermute x26, starting transfers between devices, exchanged(): lax.ppermute(block, 'row', [(i, i ^ 1 << bit) for i in range(lax.axis_siz...  29.8 us
    dot_general x15, matrix products, dot_f32(): lax.dot_general(left, right, (((left_dim,), (right_dim,)), ((), ())), pre...  9.76 us
    ppermute x4, starting transfers between devices, passed_along(): return lax.ppermute(block, 'row', route)  8.99 us
    pallas_call x1, Pallas kernels, input_gradient(): pl.pallas_call(functools.partial(input_gradient_kernel, len(gradients)),...  8.69 us
    all_to_all x1, waiting for transfers between devices, on_device(): lax.all_to_all(jnp.broadcast_to(merge_block[None], (device_count,) + merg...  8.09 us
    ppermute x4, waiting for transfers between devices, passed_along(): return lax.ppermute(block, 'row', route)  6.96 us
    all_to_all x1, starting transfers between devices, on_device(): lax.all_to_all(jnp.broadcast_to(merge_block[None], (device_count,) + merg...  3.64 us
  transfers between devices with their start and end apart: 32, of which 20 were waited for; matrix products, arithmetic and copies ran while one was open for 5% of the time, Pallas kernels for 9%

profile of v2, /device:TPU:0, one launch (start us, length us, event | category | flops | bytes accessed | tf_op | source)
XLA Modules:
  0.0 138.4 jit_solution(16793499527510373968)
XLA Ops:
  0.6 1.6 %kernel_rows.1 = bf16[64,1280]{1,0:T(8,128)(2,1)} custom-call(bf16[10,64,128]{2,1,0:T(8,128)(2,1)} %bitcast.163), custom_call_target="tpu_custom_call" | custom-call | bytes 327680 | tf_op jit(solution)/shard_map/kernel_rows/pallas_call | solution.py:129
  2.3 4.0 %collective-permute-start = (bf16[1,1,1,1,64,1280]{5,4,3,2,1,0:T(8,128)(2,1)}, bf16[1,1,1,1,64,1280]{5,4,3,2,1,0:T(8,128)(2,1)S(1)}, u32[]{:S(2)}, u32[]{:S(2)}) collective-permute-start(bf16[1,1,1,1,64,1280]{5,4,3,2,1,0:T(8,128)(2,1)} %bitcast.153), channel_id=1, source_target_pairs={{0,16},{1,17},{2,18},{3,19},{4,20},{5,21},{6,22},{7,23},{8,24},{9,... | collective-permute-start | bytes 491528 | tf_op jit(solution)/shard_map/ppermute | solution.py:23
  6.3 3.5 %reorder.1 = (bf16[384,1024]{1,0:T(8,128)(2,1)}, bf16[384,1024]{1,0:T(8,128)(2,1)}) custom-call(s32[1]{0:T(128)} %bitcast.3.me_ref, bf16[384,2048]{1,0:T(8,128)(2,1)} %bitcast.135), custom_call_target="tpu_custom_call" | custom-call | flops 6291456 | bytes 3145728 | tf_op jit(solution)/shard_map/reorder/pallas_call | solution.py:107
  9.8 4.5 %collective-permute-done = bf16[1,1,1,1,64,1280]{5,4,3,2,1,0:T(8,128)(2,1)S(1)} collective-permute-done((bf16[1,1,1,1,64,1280]{5,4,3,2,1,0:T(8,128)(2,1)}, bf16[1,1,1,1,64,1280]{5,4,3,2,1,0:T(8,128)(2,1)S(1)}, u32[]{:S(2)}, u32[]{:S(2)}) %collective-permute-start) | collective-permute-done | bytes 163872 | tf_op jit(solution)/shard_map/ppermute | solution.py:23
  18.9 3.6 %all-to-all-start = ((bf16[32,8,256]{2,1,0:T(8,128)(2,1)}), bf16[32,8,256]{2,1,0:T(8,128)(2,1)S(1)}, u32[]{:S(2)}, u32[]{:S(2)}) async-start(bf16[32,8,256]{2,1,0:T(8,128)(2,1)} %broadcast_in_dim.5), calls=%async_computation | async-start | bytes 262144 | tf_op jit(solution)/shard_map/all_to_all | solution.py:242
  22.7 8.1 %all-to-all-done = bf16[32,8,256]{2,1,0:T(8,128)(2,1)S(1)} async-done(((bf16[32,8,256]{2,1,0:T(8,128)(2,1)}), bf16[32,8,256]{2,1,0:T(8,128)(2,1)S(1)}, u32[]{:S(2)}, u32[]{:S(2)}) %all-to-all-start) | async-done | bytes 131104 | tf_op jit(solution)/shard_map/all_to_all | solution.py:242
  32.9 4.9 %collective-permute-done.4 = bf16[2,2,1,1,64,384]{5,4,3,2,1,0:T(8,128)(2,1)S(1)} collective-permute-done((bf16[2,2,1,1,64,384]{5,4,3,2,1,0:T(8,128)(2,1)S(1)}, bf16[2,2,1,1,64,384]{5,4,3,2,1,0:T(8,128)(2,1)S(1)}, u32[]{:S(2)}, u32[]{:S(2)}) %collective-permute-start.4) | collective-permute-done | bytes 196640 | tf_op jit(solution)/shard_map/ppermute | solution.py:23
  41.8 8.1 %collective-permute-done.7 = bf16[2,2,2,1,64,384]{5,4,3,2,1,0:T(8,128)(2,1)S(1)} collective-permute-done((bf16[2,2,2,1,64,384]{5,4,3,2,1,0:T(8,128)(2,1)S(1)}, bf16[2,2,2,1,64,384]{5,4,3,2,1,0:T(8,128)(2,1)S(1)}, u32[]{:S(2)}, u32[]{:S(2)}) %collective-permute-start.7) | collective-permute-done | bytes 393248 | tf_op jit(solution)/shard_map/ppermute | solution.py:23
  50.0 2.7 %collective-permute-done.9 = bf16[2,2,1,2,64,512]{5,4,3,2,1,0:T(8,128)(2,1)S(1)} collective-permute-done((bf16[2,2,1,2,64,512]{5,4,3,2,1,0:T(8,128)(2,1)S(1)}, bf16[2,2,1,2,64,512]{5,4,3,2,1,0:T(8,128)(2,1)S(1)}, u32[]{:S(2)}, u32[]{:S(2)}) %collective-permute-start.9) | collective-permute-done | bytes 524320 | tf_op jit(solution)/shard_map/ppermute | solution.py:23
  58.4 1.8 %collective-permute-start.13 = (f32[2,192,128]{2,1,0:T(8,128)S(1)}, f32[2,192,128]{2,1,0:T(8,128)S(1)}, u32[]{:S(2)}, u32[]{:S(2)}) collective-permute-start(f32[2,192,128]{2,1,0:T(8,128)S(1)} %get-tuple-element.103), channel_id=1, source_target_pairs={{0,9},{1,10},{2,11},{3,12},{4,13},{5,14},{6,15},{7,16},{8,17},{9,1... | collective-permute-start | bytes 589832 | tf_op jit(solution)/shard_map/ppermute | solution.py:19
  63.3 2.1 %collective-permute-done.13 = f32[2,192,128]{2,1,0:T(8,128)S(1)} collective-permute-done((f32[2,192,128]{2,1,0:T(8,128)S(1)}, f32[2,192,128]{2,1,0:T(8,128)S(1)}, u32[]{:S(2)}, u32[]{:S(2)}) %collective-permute-start.13) | collective-permute-done | bytes 196640 | tf_op jit(solution)/shard_map/ppermute | solution.py:19
  65.4 1.9 %collective-permute-done.14 = f32[2,192,128]{2,1,0:T(8,128)S(1)} collective-permute-done((f32[2,192,128]{2,1,0:T(8,128)S(1)}, f32[2,192,128]{2,1,0:T(8,128)S(1)}, u32[]{:S(2)}, u32[]{:S(2)}) %collective-permute-start.14) | collective-permute-done | bytes 196640 | tf_op jit(solution)/shard_map/ppermute | solution.py:19
  69.6 4.6 %collective-permute-start.16 = (bf16[2,192,128]{2,1,0:T(8,128)(2,1)S(1)}, bf16[2,192,128]{2,1,0:T(8,128)(2,1)S(1)}, u32[]{:S(2)}, u32[]{:S(2)}) collective-permute-start(bf16[2,192,128]{2,1,0:T(8,128)(2,1)S(1)} %bitcast.136), channel_id=1, source_target_pairs={{0,9},{1,10},{2,11},{3,12},{4,13},{5,14},{6,15},{7,16},{8,17},{9,1... | collective-permute-start | bytes 294920 | tf_op jit(solution)/shard_map/ppermute | solution.py:19
  77.1 3.0 %collective-permute-done.15 = bf16[2,192,128]{2,1,0:T(8,128)(2,1)S(1)} collective-permute-done((bf16[2,192,128]{2,1,0:T(8,128)(2,1)S(1)}, bf16[2,192,128]{2,1,0:T(8,128)(2,1)S(1)}, u32[]{:S(2)}, u32[]{:S(2)}) %collective-permute-start.15) | collective-permute-done | bytes 98336 | tf_op jit(solution)/shard_map/ppermute | solution.py:19
  81.8 1.7 %collective-permute-start.19 = (bf16[1024,512]{1,0:T(8,128)(2,1)S(1)}, bf16[1024,512]{1,0:T(8,128)(2,1)S(1)}, u32[]{:S(2)}, u32[]{:S(2)}) collective-permute-start(bf16[1024,512]{1,0:T(8,128)(2,1)S(1)} %convolution_convert_fusion), channel_id=1, source_target_pairs={{0,1},{1,0},{2,3},{3,2},{4,5},{5,4},{6,7},{7,6},{8,9},{9,8},{10,11... | collective-permute-start | bytes 3145736 | tf_op jit(solution)/shard_map/ppermute | solution.py:23
  90.3 6.7 %collective-permute-start.20 = (bf16[2,2,2,1,64,384]{5,4,3,2,1,0:T(8,128)(2,1)}, bf16[2,2,2,1,64,384]{5,4,3,2,1,0:T(8,128)(2,1)}, u32[]{:S(2)}, u32[]{:S(2)}) collective-permute-start(bf16[2,2,2,1,64,384]{5,4,3,2,1,0:T(8,128)(2,1)} %get-tuple-element.117), channel_id=1, source_target_pairs={{0,2},{1,3},{2,0},{3,1},{4,6},{5,7},{6,4},{7,5},{8,10},{9,11},{10,... | collective-permute-start | bytes 1179656 | tf_op jit(solution)/shard_map/ppermute | solution.py:23
  97.0 2.6 %all-to-all-start.1 = ((bf16[32,8,256]{2,1,0:T(8,128)(2,1)}), bf16[32,8,256]{2,1,0:T(8,128)(2,1)S(1)}, u32[]{:S(2)}, u32[]{:S(2)}) async-start(bf16[32,8,256]{2,1,0:T(8,128)(2,1)} %bitcast.37), calls=%async_computation.1 | async-start | bytes 262144 | tf_op jit(solution)/shard_map/all_to_all | solution.py:302
  99.5 8.7 %input_gradient.1 = bf16[384,2048]{1,0:T(8,128)(2,1)} custom-call(s32[1]{0:T(128)} %bitcast.3.me_ref, bf16[384,384]{1,0:T(8,128)(2,1)} %copy-done.9, bf16[384,384]{1,0:T(8,128)(2,1)} %copy-done.10, bf16[384,512]{1,0:T(8,128)(2,1)} %copy-done.8, bf16[1024,384]{1,0:T(8,128)(2,1)} %bitcast.129, bf16[1024,384]{1,0:T(8,128)(2,1)} %copy-done.6, ...), custom_call_target="tpu_custom_call" | custom-call | flops 2013265920 | bytes 7798784 | tf_op jit(solution)/shard_map/input_gradient/pallas_call | solution.py:173
  108.2 1.6 %collective-permute-done.21 = bf16[2,1,2,2,64,384]{5,4,3,2,1,0:T(8,128)(2,1)} collective-permute-done((bf16[2,1,2,2,64,384]{5,4,3,2,1,0:T(8,128)(2,1)}, bf16[2,1,2,2,64,384]{5,4,3,2,1,0:T(8,128)(2,1)}, u32[]{:S(2)}, u32[]{:S(2)}) %collective-permute-start.21) | collective-permute-done | bytes 393248 | tf_op jit(solution)/shard_map/ppermute | solution.py:23
  116.4 3.9 %collective-permute-done.23 = bf16[2,2,1,1,64,384]{5,4,3,2,1,0:T(8,128)(2,1)S(1)} collective-permute-done((bf16[2,2,1,1,64,384]{5,4,3,2,1,0:T(8,128)(2,1)S(1)}, bf16[2,2,1,1,64,384]{5,4,3,2,1,0:T(8,128)(2,1)S(1)}, u32[]{:S(2)}, u32[]{:S(2)}) %collective-permute-start.23) | collective-permute-done | bytes 196640 | tf_op jit(solution)/shard_map/ppermute | solution.py:23
  123.2 1.7 %collective-permute-start.26 = (bf16[2,1,1,1,64,384]{5,4,3,2,1,0:T(8,128)(2,1)S(1)}, bf16[2,1,1,1,64,384]{5,4,3,2,1,0:T(8,128)(2,1)S(1)}, u32[]{:S(2)}, u32[]{:S(2)}) collective-permute-start(bf16[2,1,1,1,64,384]{5,4,3,2,1,0:T(8,128)(2,1)S(1)} %fusion.13), channel_id=1, source_target_pairs={{0,8},{1,9},{2,10},{3,11},{4,12},{5,13},{6,14},{7,15},{8,0},{9,1},... | collective-permute-start | bytes 294920 | tf_op jit(solution)/shard_map/ppermute | solution.py:23
  125.2 2.6 %collective-permute-done.26 = bf16[2,1,1,1,64,384]{5,4,3,2,1,0:T(8,128)(2,1)S(1)} collective-permute-done((bf16[2,1,1,1,64,384]{5,4,3,2,1,0:T(8,128)(2,1)S(1)}, bf16[2,1,1,1,64,384]{5,4,3,2,1,0:T(8,128)(2,1)S(1)}, u32[]{:S(2)}, u32[]{:S(2)}) %collective-permute-start.26) | collective-permute-done | bytes 98336 | tf_op jit(solution)/shard_map/ppermute | solution.py:23
  127.8 1.7 %collective-permute-done.27 = bf16[2,1,1,1,64,384]{5,4,3,2,1,0:T(8,128)(2,1)S(1)} collective-permute-done((bf16[2,1,1,1,64,384]{5,4,3,2,1,0:T(8,128)(2,1)S(1)}, bf16[2,1,1,1,64,384]{5,4,3,2,1,0:T(8,128)(2,1)S(1)}, u32[]{:S(2)}, u32[]{:S(2)}) %collective-permute-start.27) | collective-permute-done | bytes 98336 | tf_op jit(solution)/shard_map/ppermute | solution.py:23
  131.4 6.1 %collective-permute-done.29 = bf16[1,1,1,1,64,1280]{5,4,3,2,1,0:T(8,128)(2,1)S(1)} collective-permute-done((bf16[1,1,1,1,64,1280]{5,4,3,2,1,0:T(8,128)(2,1)S(1)}, bf16[1,1,1,1,64,1280]{5,4,3,2,1,0:T(8,128)(2,1)S(1)}, u32[]{:S(2)}, u32[]{:S(2)}) %collective-permute-start.29) | collective-permute-done | bytes 163872 | tf_op jit(solution)/shard_map/ppermute | solution.py:23
  (157 shorter events, 45.5 us)
Async XLA Ops:
  2.3 12.0 %collective-permute-start = (bf16[1,1,1,1,64,1280]{5,4,3,2,1,0:T(8,128)(2,1)}, bf16[1,1,1,1,64,1280]{5,4,3,2,1,0:T(8,128)(2,1)S(1)}, u32[]{:S(2)}, u32[]{:S(2)}) collective-permute-start(bf16[1,1,1,1,64,1280]{5,4,3,2,1,0:T(8,128)(2,1)} %bitcast.153), channel_id=1, source_target_pairs={{0,16},{1,17},{2,18},{3,19},{4,20},{5,21},{6,22},{7,23},{8,24},{9,... | collective-permute-start | bytes 491528 | tf_op jit(solution)/shard_map/ppermute | solution.py:23
  14.4 8.2 %collective-permute-start.3 = (bf16[2,1,1,1,64,512]{5,4,3,2,1,0:T(8,128)(2,1)S(1)}, bf16[2,1,1,1,64,512]{5,4,3,2,1,0:T(8,128)(2,1)S(1)}, u32[]{:S(2)}, u32[]{:S(2)}) collective-permute-start(bf16[2,1,1,1,64,512]{5,4,3,2,1,0:T(8,128)(2,1)S(1)} %slice.234), channel_id=1, source_target_pairs={{0,2},{1,3},{2,0},{3,1},{4,6},{5,7},{6,4},{7,5},{8,10},{9,11},{10,... | collective-permute-start | bytes 393224 | tf_op jit(solution)/shard_map/ppermute | solution.py:23
  15.9 6.6 %collective-permute-start.1 = (bf16[2,1,1,1,64,384]{5,4,3,2,1,0:T(8,128)(2,1)S(1)}, bf16[2,1,1,1,64,384]{5,4,3,2,1,0:T(8,128)(2,1)S(1)}, u32[]{:S(2)}, u32[]{:S(2)}) collective-permute-start(bf16[2,1,1,1,64,384]{5,4,3,2,1,0:T(8,128)(2,1)S(1)} %get-tuple-element.82), channel_id=1, source_target_pairs={{0,8},{1,9},{2,10},{3,11},{4,12},{5,13},{6,14},{7,15},{8,0},{9,1},... | collective-permute-start | bytes 294920 | tf_op jit(solution)/shard_map/ppermute | solution.py:23
  18.9 11.9 %all-to-all-start = ((bf16[32,8,256]{2,1,0:T(8,128)(2,1)}), bf16[32,8,256]{2,1,0:T(8,128)(2,1)S(1)}, u32[]{:S(2)}, u32[]{:S(2)}) async-start(bf16[32,8,256]{2,1,0:T(8,128)(2,1)} %broadcast_in_dim.5), calls=%async_computation | async-start | bytes 262144 | tf_op jit(solution)/shard_map/all_to_all | solution.py:242
  30.8 8.4 %collective-permute-start.6 = (bf16[2,1,1,2,64,512]{5,4,3,2,1,0:T(8,128)(2,1)S(1)}, bf16[2,1,1,2,64,512]{5,4,3,2,1,0:T(8,128)(2,1)S(1)}, u32[]{:S(2)}, u32[]{:S(2)}) collective-permute-start(bf16[2,1,1,2,64,512]{5,4,3,2,1,0:T(8,128)(2,1)S(1)} %pad_maximum_fusion.11), channel_id=1, source_target_pairs={{0,8},{1,9},{2,10},{3,11},{4,12},{5,13},{6,14},{7,15},{8,0},{9,1},... | collective-permute-start | bytes 786440 | tf_op jit(solution)/shard_map/ppermute | solution.py:23
  31.4 6.4 %collective-permute-start.4 = (bf16[2,2,1,1,64,384]{5,4,3,2,1,0:T(8,128)(2,1)S(1)}, bf16[2,2,1,1,64,384]{5,4,3,2,1,0:T(8,128)(2,1)S(1)}, u32[]{:S(2)}, u32[]{:S(2)}) collective-permute-start(bf16[2,2,1,1,64,384]{5,4,3,2,1,0:T(8,128)(2,1)S(1)} %pad_maximum_fusion.12), channel_id=1, source_target_pairs={{0,4},{1,5},{2,6},{3,7},{4,0},{5,1},{6,2},{7,3},{8,12},{9,13},{10,... | collective-permute-start | bytes 589832 | tf_op jit(solution)/shard_map/ppermute | solution.py:23
  32.1 6.2 %collective-permute-start.5 = (bf16[2,1,2,1,64,384]{5,4,3,2,1,0:T(8,128)(2,1)S(1)}, bf16[2,1,2,1,64,384]{5,4,3,2,1,0:T(8,128)(2,1)S(1)}, u32[]{:S(2)}, u32[]{:S(2)}) collective-permute-start(bf16[2,1,2,1,64,384]{5,4,3,2,1,0:T(8,128)(2,1)S(1)} %pad_maximum_fusion.13), channel_id=1, source_target_pairs={{0,2},{1,3},{2,0},{3,1},{4,6},{5,7},{6,4},{7,5},{8,10},{9,11},{10,... | collective-permute-start | bytes 589832 | tf_op jit(solution)/shard_map/ppermute | solution.py:23
  39.3 13.3 %collective-permute-start.9 = (bf16[2,2,1,2,64,512]{5,4,3,2,1,0:T(8,128)(2,1)S(1)}, bf16[2,2,1,2,64,512]{5,4,3,2,1,0:T(8,128)(2,1)S(1)}, u32[]{:S(2)}, u32[]{:S(2)}) collective-permute-start(bf16[2,2,1,2,64,512]{5,4,3,2,1,0:T(8,128)(2,1)S(1)} %pad_maximum_fusion.4), channel_id=1, source_target_pairs={{0,4},{1,5},{2,6},{3,7},{4,0},{5,1},{6,2},{7,3},{8,12},{9,13},{10,... | collective-permute-start | bytes 1572872 | tf_op jit(solution)/shard_map/ppermute | solution.py:23
  39.8 10.1 %collective-permute-start.7 = (bf16[2,2,2,1,64,384]{5,4,3,2,1,0:T(8,128)(2,1)S(1)}, bf16[2,2,2,1,64,384]{5,4,3,2,1,0:T(8,128)(2,1)S(1)}, u32[]{:S(2)}, u32[]{:S(2)}) collective-permute-start(bf16[2,2,2,1,64,384]{5,4,3,2,1,0:T(8,128)(2,1)S(1)} %pad_maximum_fusion.5), channel_id=1, source_target_pairs={{0,2},{1,3},{2,0},{3,1},{4,6},{5,7},{6,4},{7,5},{8,10},{9,11},{10,... | collective-permute-start | bytes 1179656 | tf_op jit(solution)/shard_map/ppermute | solution.py:23
  40.5 9.5 %collective-permute-start.8 = (bf16[2,1,2,2,64,384]{5,4,3,2,1,0:T(8,128)(2,1)S(1)}, bf16[2,1,2,2,64,384]{5,4,3,2,1,0:T(8,128)(2,1)S(1)}, u32[]{:S(2)}, u32[]{:S(2)}) collective-permute-start(bf16[2,1,2,2,64,384]{5,4,3,2,1,0:T(8,128)(2,1)S(1)} %pad_maximum_fusion.6), channel_id=1, source_target_pairs={{0,8},{1,9},{2,10},{3,11},{4,12},{5,13},{6,14},{7,15},{8,0},{9,1},... | collective-permute-start | bytes 1179656 | tf_op jit(solution)/shard_map/ppermute | solution.py:23
  58.4 6.9 %collective-permute-start.13 = (f32[2,192,128]{2,1,0:T(8,128)S(1)}, f32[2,192,128]{2,1,0:T(8,128)S(1)}, u32[]{:S(2)}, u32[]{:S(2)}) collective-permute-start(f32[2,192,128]{2,1,0:T(8,128)S(1)} %get-tuple-element.103), channel_id=1, source_target_pairs={{0,9},{1,10},{2,11},{3,12},{4,13},{5,14},{6,15},{7,16},{8,17},{9,1... | collective-permute-start | bytes 589832 | tf_op jit(solution)/shard_map/ppermute | solution.py:19
  60.3 7.0 %collective-permute-start.14 = (f32[2,192,128]{2,1,0:T(8,128)S(1)}, f32[2,192,128]{2,1,0:T(8,128)S(1)}, u32[]{:S(2)}, u32[]{:S(2)}) collective-permute-start(f32[2,192,128]{2,1,0:T(8,128)S(1)} %get-tuple-element.104), channel_id=1, source_target_pairs={{9,0},{10,1},{11,2},{12,3},{13,4},{14,5},{15,6},{16,7},{17,8},{18,... | collective-permute-start | bytes 589832 | tf_op jit(solution)/shard_map/ppermute | solution.py:19
  69.6 7.5 %collective-permute-start.16 = (bf16[2,192,128]{2,1,0:T(8,128)(2,1)S(1)}, bf16[2,192,128]{2,1,0:T(8,128)(2,1)S(1)}, u32[]{:S(2)}, u32[]{:S(2)}) collective-permute-start(bf16[2,192,128]{2,1,0:T(8,128)(2,1)S(1)} %bitcast.136), channel_id=1, source_target_pairs={{0,9},{1,10},{2,11},{3,12},{4,13},{5,14},{6,15},{7,16},{8,17},{9,1... | collective-permute-start | bytes 294920 | tf_op jit(solution)/shard_map/ppermute | solution.py:19
  74.1 5.9 %collective-permute-start.15 = (bf16[2,192,128]{2,1,0:T(8,128)(2,1)S(1)}, bf16[2,192,128]{2,1,0:T(8,128)(2,1)S(1)}, u32[]{:S(2)}, u32[]{:S(2)}) collective-permute-start(bf16[2,192,128]{2,1,0:T(8,128)(2,1)S(1)} %bitcast.137), channel_id=1, source_target_pairs={{9,0},{10,1},{11,2},{12,3},{13,4},{14,5},{15,6},{16,7},{17,8},{18,... | collective-permute-start | bytes 294920 | tf_op jit(solution)/shard_map/ppermute | solution.py:19
  81.8 6.2 %collective-permute-start.19 = (bf16[1024,512]{1,0:T(8,128)(2,1)S(1)}, bf16[1024,512]{1,0:T(8,128)(2,1)S(1)}, u32[]{:S(2)}, u32[]{:S(2)}) collective-permute-start(bf16[1024,512]{1,0:T(8,128)(2,1)S(1)} %convolution_convert_fusion), channel_id=1, source_target_pairs={{0,1},{1,0},{2,3},{3,2},{4,5},{5,4},{6,7},{7,6},{8,9},{9,8},{10,11... | collective-permute-start | bytes 3145736 | tf_op jit(solution)/shard_map/ppermute | solution.py:23
  90.3 19.6 %collective-permute-start.22 = (bf16[2,2,1,2,64,512]{5,4,3,2,1,0:T(8,128)(2,1)S(1)}, bf16[2,2,1,2,64,512]{5,4,3,2,1,0:T(8,128)(2,1)}, u32[]{:S(2)}, u32[]{:S(2)}) collective-permute-start(bf16[2,2,1,2,64,512]{5,4,3,2,1,0:T(8,128)(2,1)S(1)} %get-tuple-element.119), channel_id=1, source_target_pairs={{0,4},{1,5},{2,6},{3,7},{4,0},{5,1},{6,2},{7,3},{8,12},{9,13},{10,... | collective-permute-start | bytes 1572872 | tf_op jit(solution)/shard_map/ppermute | solution.py:23
  90.3 17.9 %collective-permute-start.20 = (bf16[2,2,2,1,64,384]{5,4,3,2,1,0:T(8,128)(2,1)}, bf16[2,2,2,1,64,384]{5,4,3,2,1,0:T(8,128)(2,1)}, u32[]{:S(2)}, u32[]{:S(2)}) collective-permute-start(bf16[2,2,2,1,64,384]{5,4,3,2,1,0:T(8,128)(2,1)} %get-tuple-element.117), channel_id=1, source_target_pairs={{0,2},{1,3},{2,0},{3,1},{4,6},{5,7},{6,4},{7,5},{8,10},{9,11},{10,... | collective-permute-start | bytes 1179656 | tf_op jit(solution)/shard_map/ppermute | solution.py:23
  96.9 12.9 %collective-permute-start.21 = (bf16[2,1,2,2,64,384]{5,4,3,2,1,0:T(8,128)(2,1)}, bf16[2,1,2,2,64,384]{5,4,3,2,1,0:T(8,128)(2,1)}, u32[]{:S(2)}, u32[]{:S(2)}) collective-permute-start(bf16[2,1,2,2,64,384]{5,4,3,2,1,0:T(8,128)(2,1)} %get-tuple-element.118), channel_id=1, source_target_pairs={{0,8},{1,9},{2,10},{3,11},{4,12},{5,13},{6,14},{7,15},{8,0},{9,1},... | collective-permute-start | bytes 1179656 | tf_op jit(solution)/shard_map/ppermute | solution.py:23
  97.0 12.9 %all-to-all-start.1 = ((bf16[32,8,256]{2,1,0:T(8,128)(2,1)}), bf16[32,8,256]{2,1,0:T(8,128)(2,1)S(1)}, u32[]{:S(2)}, u32[]{:S(2)}) async-start(bf16[32,8,256]{2,1,0:T(8,128)(2,1)} %bitcast.37), calls=%async_computation.1 | async-start | bytes 262144 | tf_op jit(solution)/shard_map/all_to_all | solution.py:302
  113.3 8.4 %collective-permute-start.25 = (bf16[2,1,1,2,64,512]{5,4,3,2,1,0:T(8,128)(2,1)S(1)}, bf16[2,1,1,2,64,512]{5,4,3,2,1,0:T(8,128)(2,1)S(1)}, u32[]{:S(2)}, u32[]{:S(2)}) collective-permute-start(bf16[2,1,1,2,64,512]{5,4,3,2,1,0:T(8,128)(2,1)S(1)} %get-tuple-element.133), channel_id=1, source_target_pairs={{0,8},{1,9},{2,10},{3,11},{4,12},{5,13},{6,14},{7,15},{8,0},{9,1},... | collective-permute-start | bytes 786440 | tf_op jit(solution)/shard_map/ppermute | solution.py:23
  113.8 6.6 %collective-permute-start.23 = (bf16[2,2,1,1,64,384]{5,4,3,2,1,0:T(8,128)(2,1)S(1)}, bf16[2,2,1,1,64,384]{5,4,3,2,1,0:T(8,128)(2,1)S(1)}, u32[]{:S(2)}, u32[]{:S(2)}) collective-permute-start(bf16[2,2,1,1,64,384]{5,4,3,2,1,0:T(8,128)(2,1)S(1)} %get-tuple-element.131), channel_id=1, source_target_pairs={{0,4},{1,5},{2,6},{3,7},{4,0},{5,1},{6,2},{7,3},{8,12},{9,13},{10,... | collective-permute-start | bytes 589832 | tf_op jit(solution)/shard_map/ppermute | solution.py:23
  115.0 6.4 %collective-permute-start.24 = (bf16[2,1,2,1,64,384]{5,4,3,2,1,0:T(8,128)(2,1)S(1)}, bf16[2,1,2,1,64,384]{5,4,3,2,1,0:T(8,128)(2,1)S(1)}, u32[]{:S(2)}, u32[]{:S(2)}) collective-permute-start(bf16[2,1,2,1,64,384]{5,4,3,2,1,0:T(8,128)(2,1)S(1)} %get-tuple-element.132), channel_id=1, source_target_pairs={{0,2},{1,3},{2,0},{3,1},{4,6},{5,7},{6,4},{7,5},{8,10},{9,11},{10,... | collective-permute-start | bytes 589832 | tf_op jit(solution)/shard_map/ppermute | solution.py:23
  121.7 7.7 %collective-permute-start.28 = (bf16[2,1,1,1,64,512]{5,4,3,2,1,0:T(8,128)(2,1)S(1)}, bf16[2,1,1,1,64,512]{5,4,3,2,1,0:T(8,128)(2,1)S(1)}, u32[]{:S(2)}, u32[]{:S(2)}) collective-permute-start(bf16[2,1,1,1,64,512]{5,4,3,2,1,0:T(8,128)(2,1)S(1)} %fusion.10), channel_id=1, source_target_pairs={{0,2},{1,3},{2,0},{3,1},{4,6},{5,7},{6,4},{7,5},{8,10},{9,11},{10,... | collective-permute-start | bytes 393224 | tf_op jit(solution)/shard_map/ppermute | solution.py:23
  129.7 7.8 %collective-permute-start.29 = (bf16[1,1,1,1,64,1280]{5,4,3,2,1,0:T(8,128)(2,1)S(1)}, bf16[1,1,1,1,64,1280]{5,4,3,2,1,0:T(8,128)(2,1)S(1)}, u32[]{:S(2)}, u32[]{:S(2)}) collective-permute-start(bf16[1,1,1,1,64,1280]{5,4,3,2,1,0:T(8,128)(2,1)S(1)} %slice.472), channel_id=1, source_target_pairs={{0,16},{1,17},{2,18},{3,19},{4,20},{5,21},{6,22},{7,23},{8,24},{9,... | collective-permute-start | bytes 491528 | tf_op jit(solution)/shard_map/ppermute | solution.py:23
  (24 other events, 97.3 us)

commit v3 on v2

--- a/solution.py
+++ b/solution.py
@@ -115,6 +115,7 @@
         cost_estimate=pl.CostEstimate(
             flops=8 * pixels * channels, bytes_accessed=4 * pixels * channels, transcendentals=0
         ),
+        compiler_params=pltpu.CompilerParams(vmem_limit_bytes=12 << 20),
         name="reorder",
     )(me.reshape(1), flat)
 
@@ -132,60 +133,171 @@
         in_specs=[pl.BlockSpec(memory_space=pltpu.VMEM)],
         out_specs=pl.BlockSpec(memory_space=pltpu.VMEM),
         cost_estimate=pl.CostEstimate(flops=0, bytes_accessed=4 * weight.size, transcendentals=0),
+        compiler_params=pltpu.CompilerParams(vmem_limit_bytes=4 << 20),
         name="kernel_rows",
     )(weight)
 
 
 def input_gradient_kernel(portion_count, me_ref, *refs):
-    core = me_ref[0] % 2
+    me = me_ref[0]
+    chip, core = me // 2, me % 2
+    gradients = refs[:portion_count]
+    own, other = refs[portion_count : 2 * portion_count], refs[2 * portion_count : -1]
     out_ref = refs[-1]
-    total = None
-    for p in range(portion_count):
-        gradient_ref = refs[p]
-        first = portion_count + 4 * p
-        rows = []
-        for k in range(2):
-            own, other = refs[first + 2 * k][...], refs[first + 2 * k + 1][...]
-            rows += [jnp.where(core == 0, own, other), jnp.where(core == 0, other, own)]
-        part = dot_f32(gradient_ref[...], jnp.concatenate(rows, axis=0), 1, 1)
-        total = part if total is None else total + part
-    out_ref[...] = total.astype(out_ref.dtype)
+    rows = LANES // 2
+
+    def step(t, carry):
+        total = None
+        for p in range(portion_count):
+            taken = []
+            for k in range(2):
+                at = pl.ds(pl.multiple_of(((2 * t + k) ^ chip) * rows, rows), rows)
+                a, b = own[p][at, :], other[p][at, :]
+                taken += [jnp.where(core == 0, a, b), jnp.where(core == 0, b, a)]
+            part = dot_f32(gradients[p][...], jnp.concatenate(taken, axis=0), 1, 1)
+            total = part if total is None else total + part
+        columns = pl.ds(pl.multiple_of(t * 2 * LANES, 2 * LANES), 2 * LANES)
+        out_ref[:, columns] = total.astype(out_ref.dtype)
+        return carry
+
+    lax.fori_loop(0, out_ref.shape[1] // (2 * LANES), step, 0, unroll=True)
 
 
 def input_gradient(gradients, own, other, me):
     pixels = gradients[0].shape[0]
     half = own[0].shape[0]
-    rows = LANES // 2
-    operands, specs = list(gradients), [
-        pl.BlockSpec(g.shape, lambda t, me_ref: (0, 0)) for g in gradients
-    ]
-    for a, b in zip(own, other):
-        for k in range(2):
-            for w in (a, b):
-                operands.append(w)
-                specs.append(
-                    pl.BlockSpec(
-                        (rows, w.shape[1]),
-                        lambda t, me_ref, k=k: ((2 * t + k) ^ (me_ref[0] // 2), 0),
-                    )
-                )
+    operands = [pltpu.with_memory_space_constraint(x, pltpu.VMEM) for x in (*gradients, *own, *other)]
     columns = sum(g.shape[1] for g in gradients)
     return pl.pallas_call(
         functools.partial(input_gradient_kernel, len(gradients)),
         out_shape=jax.ShapeDtypeStruct((pixels, 2 * half), jnp.bfloat16),
-        grid_spec=pltpu.PrefetchScalarGridSpec(
-            num_scalar_prefetch=1,
-            grid=(half // LANES,),
-            in_specs=specs,
-            out_specs=pl.BlockSpec((pixels, 2 * LANES), lambda t, me_ref: (0, t)),
-        ),
+        in_specs=[pl.BlockSpec(memory_space=pltpu.SMEM)]
+        + [pl.BlockSpec(memory_space=pltpu.VMEM)] * len(operands),
+        out_specs=pl.BlockSpec(memory_space=pltpu.VMEM),
         cost_estimate=pl.CostEstimate(
             flops=4 * pixels * columns * half,
             bytes_accessed=2 * (pixels * columns + 2 * half * columns + 2 * pixels * half),
             transcendentals=0,
         ),
+        compiler_params=pltpu.CompilerParams(vmem_limit_bytes=16 << 20),
         name="input_gradient",
     )(me.reshape(1), *operands)
+
+
+def moved_rows(block, width, shift):
+    if shift == 0:
+        return block
+    size = block.shape[0]
+    column = lax.broadcasted_iota(jnp.int32, block.shape, 0) % width + shift
+    inside = (column >= 0) & (column < width)
+    return jnp.where(inside, pltpu.roll(block, (-shift) % size, 0), 0.0)
+
+
+def head_kernel(
+    width, centre_ref, above_ref, below_ref, bias_ref, merge_ref, merge_bias_ref, cotangent_ref,
+    merged_ref, dilated_ref, gradient_ref, joined_ref, grad_out_ref,
+):
+    branch = above_ref.shape[1]
+    z_dil = above_ref[...] + below_ref[...]
+    for j in range(3):
+        part = centre_ref[:, (1 + j) * branch : (2 + j) * branch]
+        z_dil = z_dil + moved_rows(part, width, (j - 1) * DILATION_RATE)
+    act_one = jnp.maximum(centre_ref[:, :branch] + bias_ref[0:1, :], 0.0).astype(jnp.bfloat16)
+    act_dil = jnp.maximum(z_dil + bias_ref[1:2, :], 0.0).astype(jnp.bfloat16)
+    joined = jnp.concatenate([act_one, act_dil], axis=1)
+    joined_ref[...] = joined
+    merged = jnp.maximum(dot_f32(joined, merge_ref[...], 1, 0) + merge_bias_ref[...], 0.0)
+    merged = merged.astype(jnp.bfloat16)
+    merged_ref[...] = merged
+    cotangent = cotangent_ref[...].astype(jnp.float32)
+    grad_out = jnp.where(merged.astype(jnp.float32) > 0, cotangent, 0.0).astype(jnp.bfloat16)
+    grad_out_ref[...] = grad_out
+    back = dot_f32(grad_out, merge_ref[...], 1, 1)
+    kept = jnp.where(joined.astype(jnp.float32) > 0, back, 0.0).astype(jnp.bfloat16)
+    dilated = kept[:, branch:]
+    dilated_ref[...] = dilated
+    gradient_ref[:, :branch] = kept[:, :branch]
+    for j in range(3):
+        moved = moved_rows(dilated.astype(jnp.float32), width, (1 - j) * DILATION_RATE)
+        gradient_ref[:, (1 + j) * branch : (2 + j) * branch] = moved.astype(jnp.bfloat16)
+
+
+def head(width, centre, above, below, bias, whole_merge, merge_bias, cotangent):
+    pixels, branch = above.shape
+    merged_width = whole_merge.shape[1]
+    widths = (merged_width, branch, 4 * branch, 2 * branch, merged_width)
+    operands = (centre, above, below, bias, whole_merge, merge_bias.reshape(1, -1), cotangent)
+    return pl.pallas_call(
+        functools.partial(head_kernel, width),
+        out_shape=[jax.ShapeDtypeStruct((pixels, w), jnp.bfloat16) for w in widths],
+        in_specs=[pl.BlockSpec(memory_space=pltpu.VMEM)] * len(operands),
+        out_specs=[pl.BlockSpec(memory_space=pltpu.VMEM)] * len(widths),
+        cost_estimate=pl.CostEstimate(
+            flops=8 * pixels * branch * merged_width,
+            bytes_accessed=8 * pixels * (6 * branch + merged_width),
+            transcendentals=0,
+        ),
+        compiler_params=pltpu.CompilerParams(vmem_limit_bytes=12 << 20),
+        name="head",
+    )(*operands)
+
+
+def shift_kernel(width, first_ref, second_ref, first_out_ref, second_out_ref):
+    branch = first_ref.shape[1]
+    for ref, out_ref in ((first_ref, first_out_ref), (second_ref, second_out_ref)):
+        block = ref[...].astype(jnp.float32)
+        for j in range(3):
+            moved = moved_rows(block, width, (1 - j) * DILATION_RATE)
+            out_ref[:, j * branch : (j + 1) * branch] = moved.astype(jnp.bfloat16)
+
+
+def shifted(width, first, second):
+    pixels, branch = first.shape
+    out = jax.ShapeDtypeStruct((pixels, 3 * branch), jnp.bfloat16)
+    return pl.pallas_call(
+        functools.partial(shift_kernel, width),
+        out_shape=(out, out),
+        in_specs=[pl.BlockSpec(memory_space=pltpu.VMEM)] * 2,
+        out_specs=(pl.BlockSpec(memory_space=pltpu.VMEM),) * 2,
+        cost_estimate=pl.CostEstimate(
+            flops=0, bytes_accessed=16 * pixels * branch, transcendentals=0
+        ),
+        compiler_params=pltpu.CompilerParams(vmem_limit_bytes=8 << 20),
+        name="shift",
+    )(first, second)
+
+
+def merge_gradient_kernel(me_ref, joined_ref, grad_out_ref, own_ref, other_ref, total_ref):
+    me = me_ref[0]
+    total_ref[...] = dot_f32(joined_ref[...], grad_out_ref[...], 0, 0)
+    half = own_ref.shape[0]
+    group = 8
+    for k in range(half // group):
+        here = slice(k * group, (k + 1) * group)
+        device = (2 * k) ^ me
+        own_ref[here, :] = total_ref[pl.ds(pl.multiple_of(device * group, group), group), :]
+        device = (2 * k + 1) ^ me
+        other_ref[here, :] = total_ref[pl.ds(pl.multiple_of(device * group, group), group), :]
+
+
+def merge_gradient(joined, grad_out, me):
+    pixels, width = joined.shape
+    half = jax.ShapeDtypeStruct((width // 2, grad_out.shape[1]), jnp.float32)
+    return pl.pallas_call(
+        merge_gradient_kernel,
+        out_shape=(half, half),
+        in_specs=[pl.BlockSpec(memory_space=pltpu.SMEM)]
+        + [pl.BlockSpec(memory_space=pltpu.VMEM)] * 2,
+        out_specs=(pl.BlockSpec(memory_space=pltpu.VMEM),) * 2,
+        scratch_shapes=[pltpu.VMEM((width, grad_out.shape[1]), jnp.float32)],
+        cost_estimate=pl.CostEstimate(
+            flops=2 * pixels * width * grad_out.shape[1],
+            bytes_accessed=8 * pixels * width,
+            transcendentals=0,
+        ),
+        compiler_params=pltpu.CompilerParams(vmem_limit_bytes=8 << 20),
+        name="merge_gradient",
+    )(me.reshape(1), joined, grad_out)
 
 
 def column_shifted(rows, shift):
@@ -214,7 +326,7 @@
     bits = (1,) * (bit_count - 1)
     orders = bit_orders(bit_count)
     far_bits = list(range(bit_count - 1, 3, -1))
-    paired = 2 * own_channels == LANES
+    paired = 2 * own_channels == LANES and joined_rows == 8 and branch == LANES
     portion_widths = [len(p) * branch for p in PORTIONS]
 
     def split(array, widths):
@@ -227,7 +339,7 @@
         block = kernel_rows(weight, tap_order)
     else:
         block = jnp.concatenate([weight[k] for k in tap_order], axis=1)
-    block, flat = together(block, features.reshape(pixels, channels))
+    block, flat, me = together(block, features.reshape(pixels, channels), me)
     half_rows = channels // 2
     if paired:
         flat_own, flat_other = reordered(flat, me)
@@ -236,20 +348,16 @@
         flat = dot_f32(flat, to_relative, 1, 0).astype(jnp.bfloat16)
         flat_own, flat_other = flat[:, :half_rows], flat[:, half_rows:]
     block = block.reshape(bits + block.shape)
+    merge_block = merge_weight.reshape(bits + merge_weight.shape)
     for bit in far_bits:
-        (block,) = gathered([block], [bit], bit_count)
-    flat_own, flat_other, merge_block = together(flat_own, flat_other, merge_weight)
-    whole_merge = lax.all_to_all(
-        jnp.broadcast_to(merge_block[None], (device_count,) + merge_block.shape), "row", 0, 0
-    ).reshape(joined_width, merged_width)
+        block, merge_block = gathered([block, merge_block], [bit, bit], bit_count)
     block, flat_own, flat_other = together(block, flat_own, flat_other)
     blocks = split(block, portion_widths)
+    blocks.append(merge_block)
+    crossing = orders + [orders[0]]
     for step in range(len(orders[0])):
-        if step == 1:
-            *blocks, whole_merge = together(*blocks, whole_merge)
-        else:
-            blocks = together(*blocks)
-        blocks = gathered(blocks, [o[step] for o in orders], bit_count)
+        blocks = gathered(together(*blocks), [o[step] for o in crossing], bit_count)
+    own_merge = blocks.pop().reshape(joined_width // 2, merged_width)
     own_weight = [b.reshape(half_rows, b.shape[-1]) for b in blocks]
 
     def row_sum(parts):
@@ -267,54 +375,82 @@
 
     other_weight = [exchanged(w, 0) for w in own_weight[:2]]
     sums = [row_sum(product(a, b)) for a, b in zip(own_weight, other_weight)]
-    own_weight[2], *sums = together(own_weight[2], *sums)
+    merge_to_relative = relative_order(joined_width, device_count, me)
+    own_weight[2], own_merge, *sums = together(own_weight[2], own_merge, *sums)
+    whole_merge = dot_f32(
+        merge_to_relative, jnp.concatenate([own_merge, exchanged(own_merge, 0)], axis=0), 1, 0
+    ).astype(jnp.bfloat16)
     other_weight.append(exchanged(own_weight[2], 0))
-    centre = product(own_weight[2], other_weight[2])
-    above = passed_along(sums[0], device_step)
-    below = passed_along(sums[1], -device_step)
-    z_dil = (row_sum(centre[1:]) + above + below).reshape(pixels, branch)
-    act_one = jnp.maximum(centre[0] + branch_norm_bias[0], 0.0).astype(jnp.bfloat16)
-    act_dil = jnp.maximum(z_dil + branch_norm_bias[1], 0.0).astype(jnp.bfloat16)
-    joined = jnp.concatenate([act_one, act_dil], axis=1)
-    merged = jnp.maximum(dot_f32(joined, whole_merge, 1, 0) + merge_bias, 0.0).astype(jnp.bfloat16)
-    grad_out = jnp.where(
-        merged > 0, cotangent.reshape(pixels, merged_width), jnp.zeros((), jnp.bfloat16)
-    )
-    back = dot_f32(grad_out, whole_merge, 1, 1)
-    grad_one = jnp.where(act_one > 0, back[:, :branch], 0.0).astype(jnp.bfloat16)
-    grad_dil = jnp.where(act_dil > 0, back[:, branch:], 0.0).astype(jnp.bfloat16)
-    grad_map = grad_dil.reshape(rows, width, branch)
-    halos = [passed_along(grad_map, -device_step), passed_along(grad_map, device_step)]
+    centre = dot_f32(flat_own, own_weight[2], 1, 0) + dot_f32(flat_other, other_weight[2], 1, 0)
+    above = passed_along(sums[0], device_step).reshape(pixels, branch)
+    below = passed_along(sums[1], -device_step).reshape(pixels, branch)
+    flat_cotangent = cotangent.reshape(pixels, merged_width)
+    if paired:
+        merged, grad_dil, centre_gradient, joined, grad_out = head(
+            width, centre, above, below, branch_norm_bias, whole_merge, merge_bias, flat_cotangent
+        )
+    else:
+        centre = by_tap(centre)
+        z_dil = row_sum(centre[1:]).reshape(pixels, branch) + above + below
+        act_one = jnp.maximum(centre[0] + branch_norm_bias[0], 0.0).astype(jnp.bfloat16)
+        act_dil = jnp.maximum(z_dil + branch_norm_bias[1], 0.0).astype(jnp.bfloat16)
+        joined = jnp.concatenate([act_one, act_dil], axis=1)
+        merged = jnp.maximum(dot_f32(joined, whole_merge, 1, 0) + merge_bias, 0.0)
+        merged = merged.astype(jnp.bfloat16)
+        grad_out = jnp.where(merged > 0, flat_cotangent, jnp.zeros((), jnp.bfloat16))
+        back = dot_f32(grad_out, whole_merge, 1, 1)
+        kept = jnp.where(joined > 0, back, 0.0).astype(jnp.bfloat16)
+        grad_dil = kept[:, branch:]
+        centre_gradient = None
 
     def shifted_gradients(block):
-        return [
-            column_shifted(block, (1 - j) * DILATION_RATE).reshape(pixels, branch) for j in range(3)
-        ]
-
-    merge_total = dot_f32(joined, grad_out, 0, 0).astype(jnp.bfloat16)
-    gradients = [None] * 3
+        block = block.reshape(rows, width, branch)
+        parts = [column_shifted(block, (1 - j) * DILATION_RATE) for j in range(3)]
+        return [part.reshape(pixels, branch) for part in parts]
+
+    if not paired:
+        centre_gradient = jnp.concatenate([kept[:, :branch]] + shifted_gradients(grad_dil), axis=1)
+    halos = [passed_along(grad_dil, -device_step), passed_along(grad_dil, device_step)]
+    if paired:
+        own_merge, other_merge = merge_gradient(joined, grad_out, me)
+    else:
+        joined_relative = dot_f32(joined, merge_to_relative, 1, 0).astype(jnp.bfloat16)
+        merge_total = dot_f32(joined_relative, grad_out, 0, 0)
+        own_merge = merge_total[: joined_width // 2]
+        other_merge = merge_total[joined_width // 2 :]
+    merge_arrived = exchanged(other_merge, 0)
+
+    centre_gradient, own_merge = together(centre_gradient, own_merge)
     own_total, other_total = [None] * 3, [None] * 3
-    for p in (2, 0, 1):
-        parts = [grad_one] + shifted_gradients(grad_map) if p == 2 else shifted_gradients(halos[p])
-        gradients[p] = jnp.concatenate(parts, axis=1)
-        if p == 2:
-            gradients[p], merge_total = together(gradients[p], merge_total)
-            merge_parts = lax.all_to_all(
-                merge_total.reshape(device_count, joined_rows, merged_width), "row", 0, 0
-            )
-        else:
-            gradients[p] = lax.optimization_barrier(gradients[p])
+    other_total[2] = dot_f32(flat_other, centre_gradient, 0, 0).astype(jnp.bfloat16)
+    own_total[2] = dot_f32(flat_own, centre_gradient, 0, 0)
+    *halos, own_total[2], other_total[2] = together(*halos, own_total[2], other_total[2])
+    if paired:
+        gradients = [*shifted(width, *halos), centre_gradient]
+    else:
+        gradients = [jnp.concatenate(shifted_gradients(h), axis=1) for h in halos]
+        gradients = together(*gradients) + [centre_gradient]
+    for p in range(2):
         other_total[p] = dot_f32(flat_other, gradients[p], 0, 0).astype(jnp.bfloat16)
         own_total[p] = dot_f32(flat_own, gradients[p], 0, 0)
-        if p == 2:
-            *halos, own_total[2], other_total[2] = together(*halos, own_total[2], other_total[2])
-    other_total = together(*other_total)
-    arrived = together(*[exchanged(t, 0) for t in other_total])
-    split_shape = (2,) * (bit_count - 1) + (own_channels, -1)
-    totals = [
-        added(t.reshape(split_shape), a.reshape(split_shape), o[-1], bit_count)
-        for t, a, o in zip(own_total, arrived, orders)
+    merge_total = own_merge + merge_arrived.astype(jnp.float32)
+    merge_total = merge_total.reshape((2,) * (bit_count - 1) + (joined_rows, merged_width))
+    merge_parts = halves(merge_total, far_bits[0], bit_count) if far_bits else None
+    sending = list(other_total) + ([merge_parts[1]] if far_bits else [])
+    arrived = [
+        exchanged(t, b) for t, b in zip(together(*sending), [0, 0, 0] + far_bits[:1])
     ]
+    arrived = together(*arrived)
+    if far_bits:
+        merge_total = merge_parts[0] + arrived.pop().astype(jnp.float32)
+    for bit in far_bits[1:]:
+        own, other = halves(merge_total, bit, bit_count)
+        merge_total = own + exchanged(other, bit).astype(jnp.float32)
+    totals = []
+    for own, a, o in zip(own_total, arrived, orders):
+        shape = (2,) * (bit_count - 1) + (own.shape[0] // (device_count // 2), own.shape[1])
+        totals.append(added(own.reshape(shape), a.reshape(shape), o[-1], bit_count))
+    totals.append(halves(merge_total, crossing[3][-1], bit_count))
     *sent, g0, g1, g2 = together(*[t[1] for t in totals], *gradients)
     if paired:
         input_grad = input_gradient([g0, g1, g2], own_weight, other_weight, me)
@@ -325,19 +461,19 @@
         ).astype(jnp.bfloat16)
         input_grad = dot_f32(input_total, to_relative, 1, 1).astype(jnp.bfloat16)
     for step in range(len(orders[0])):
-        arrived = together(*[exchanged(t, o[-1 - step]) for t, o in zip(sent, orders)])
+        arrived = together(*[exchanged(t, o[-1 - step]) for t, o in zip(sent, crossing)])
         if step == 0:
-            *arrived, input_grad, merge_parts = together(*arrived, input_grad, merge_parts)
+            *arrived, input_grad = together(*arrived, input_grad)
         own = [t[0] for t in totals]
         if step + 1 < len(orders[0]):
             totals = [
-                added(t, a, o[-2 - step], bit_count) for t, a, o in zip(own, arrived, orders)
+                added(t, a, o[-2 - step], bit_count) for t, a, o in zip(own, arrived, crossing)
             ]
             sent = together(*[t[1] for t in totals])
         else:
             totals = [t + a.astype(jnp.float32) for t, a in zip(own, arrived)]
-    grad_merge = jnp.sum(merge_parts.astype(jnp.float32), axis=0) * scale
-    total = jnp.concatenate(totals, axis=-1)
+    grad_merge = totals[3].reshape(joined_rows, merged_width) * scale
+    total = jnp.concatenate(totals[:3], axis=-1)
     for bit in far_bits[::-1]:
         own, other = halves(total, bit, bit_count)
         total = own + exchanged(other, bit).astype(jnp.float32)

time: 139 us -> 122 us (0.88)
  Pallas kernels: 13.8 us -> 6.51 us
  waiting for transfers between devices: 56.5 us -> 49.5 us
  starting transfers between devices: 44.9 us -> 50.2 us
  other arithmetic: 8.28 us -> 3.38 us
  matrix products: 9.76 us -> 7.98 us
    ppermute x26 -> x36, starting transfers between devices: 29.8 us -> 38.9 us  [exchanged(): lax.ppermute(block, 'row', [(i, i ^ 1 << bit) for i in range(lax.axis_siz...]
    all_to_all x2 -> x0, waiting for transfers between devices: 8.1 us -> none  [the longest x1 8.09 us: on_device(): lax.all_to_all(jnp.broadcast_to(merge_block[None], (device_count,) + merg...]
    all_to_all x2 -> x0, starting transfers between devices: 6.19 us -> none  [the longest x1 3.64 us: on_device(): lax.all_to_all(jnp.broadcast_to(merge_block[None], (device_count,) + merg...]
    pallas_call x1, Pallas kernels: 8.69 us -> 3.8 us  [input_gradient(): pl.pallas_call(functools.partial(input_gradient_kernel, len(gradients)),...]
    add x4 -> x5, other arithmetic: 3.39 us -> 0.8 us  [half(): return parts[0] + parts[1].astype(jnp.float32)]
    pallas_call x1, Pallas kernels: 3.54 us -> 0.95 us  [reordered(): pl.pallas_call(reorder_kernel, out_shape=(half, half), in_specs=[pl.Block...]
    ppermute x4, starting transfers between devices: 8.99 us -> 11.4 us  [passed_along(): return lax.ppermute(block, 'row', route)]
    convert_element_type x5 -> x6, other arithmetic: 2.36 us -> 0.34 us  [added(): return (half(0), half(1).astype(jnp.bfloat16))]
  transfers between devices with their start and end apart: 32 -> 40, of which waited for: 20 -> 18; matrix products, arithmetic and copies ran while one was open for 5% -> 7% of each run, Pallas kernels for 9% -> 4%
where the time goes in v3:
time: 122 us
  starting transfers between devices  50.2 us (41%)
  waiting for transfers between devices  49.5 us (41%)
  matrix products  7.98 us (7%)
  Pallas kernels  6.51 us (5%)
  other arithmetic  3.38 us (3%)
  local copies, waits for them, and re-layouts  2.6 us (2%)
  between operations  1.3 us (1%)
    ppermute x36, waiting for transfers between devices, exchanged(): lax.ppermute(block, 'row', [(i, i ^ 1 << bit) for i in range(lax.axis_siz...  41.1 us
    ppermute x36, starting transfers between devices, exchanged(): lax.ppermute(block, 'row', [(i, i ^ 1 << bit) for i in range(lax.axis_siz...  38.9 us
    ppermute x4, starting transfers between devices, passed_along(): return lax.ppermute(block, 'row', route)  11.4 us
    ppermute x4, waiting for transfers between devices, passed_along(): return lax.ppermute(block, 'row', route)  8.37 us
    dot_general x13, matrix products, dot_f32(): lax.dot_general(left, right, (((left_dim,), (right_dim,)), ((), ())), pre...  7.98 us
    pallas_call x1, Pallas kernels, input_gradient(): pl.pallas_call(functools.partial(input_gradient_kernel, len(gradients)),...  3.8 us
  transfers between devices with their start and end apart: 40, of which 18 were waited for; matrix products, arithmetic and copies ran while one was open for 7% of the time, Pallas kernels for 4%

profile of v3, /device:TPU:0, one launch (start us, length us, event | category | flops | bytes accessed | tf_op | source)
XLA Modules:
  0.0 121.5 jit_solution(4722911022658353649)
XLA Ops:
  1.6 4.1 %collective-permute-start = (bf16[1,1,1,1,64,1280]{5,4,3,2,1,0:T(8,128)(2,1)S(1)}, bf16[1,1,1,1,64,1280]{5,4,3,2,1,0:T(8,128)(2,1)S(1)}, u32[]{:S(2)}, u32[]{:S(2)}) collective-permute-start(bf16[1,1,1,1,64,1280]{5,4,3,2,1,0:T(8,128)(2,1)S(1)} %bitcast.107), channel_id=1, source_target_pairs={{0,16},{1,17},{2,18},{3,19},{4,20},{5,21},{6,22},{7,23},{8,24},{9,... | collective-permute-start | bytes 491528 | tf_op jit(solution)/shard_map/ppermute | solution.py:23
  8.1 5.4 %collective-permute-done.1 = bf16[1,1,1,1,8,256]{5,4,3,2,1,0:T(8,128)(2,1)S(1)} collective-permute-done((bf16[1,1,1,1,8,256]{5,4,3,2,1,0:T(8,128)(2,1)}, bf16[1,1,1,1,8,256]{5,4,3,2,1,0:T(8,128)(2,1)S(1)}, u32[]{:S(2)}, u32[]{:S(2)}) %collective-permute-start.1) | collective-permute-done | bytes 4128 | tf_op jit(solution)/shard_map/ppermute | solution.py:23
  13.7 1.6 %collective-permute-start.4 = (bf16[2,1,1,1,64,512]{5,4,3,2,1,0:T(8,128)(2,1)S(1)}, bf16[2,1,1,1,64,512]{5,4,3,2,1,0:T(8,128)(2,1)S(1)}, u32[]{:S(2)}, u32[]{:S(2)}) collective-permute-start(bf16[2,1,1,1,64,512]{5,4,3,2,1,0:T(8,128)(2,1)S(1)} %slice.228), channel_id=1, source_target_pairs={{0,2},{1,3},{2,0},{3,1},{4,6},{5,7},{6,4},{7,5},{8,10},{9,11},{10,... | collective-permute-start | bytes 393224 | tf_op jit(solution)/shard_map/ppermute | solution.py:23
  16.0 1.5 %collective-permute-start.3 = (bf16[2,1,1,1,64,384]{5,4,3,2,1,0:T(8,128)(2,1)S(1)}, bf16[2,1,1,1,64,384]{5,4,3,2,1,0:T(8,128)(2,1)S(1)}, u32[]{:S(2)}, u32[]{:S(2)}) collective-permute-start(bf16[2,1,1,1,64,384]{5,4,3,2,1,0:T(8,128)(2,1)S(1)} %get-tuple-element.107), channel_id=1, source_target_pairs={{0,4},{1,5},{2,6},{3,7},{4,0},{5,1},{6,2},{7,3},{8,12},{9,13},{10,... | collective-permute-start | bytes 294920 | tf_op jit(solution)/shard_map/ppermute | solution.py:23
  18.8 2.3 %collective-permute-done.5 = bf16[2,1,1,1,8,256]{5,4,3,2,1,0:T(8,128)(2,1)S(1)} collective-permute-done((bf16[2,1,1,1,8,256]{5,4,3,2,1,0:T(8,128)(2,1)S(1)}, bf16[2,1,1,1,8,256]{5,4,3,2,1,0:T(8,128)(2,1)S(1)}, u32[]{:S(2)}, u32[]{:S(2)}) %collective-permute-start.5) | collective-permute-done | bytes 8224 | tf_op jit(solution)/shard_map/ppermute | solution.py:23
  25.2 3.4 %collective-permute-done.9 = bf16[2,2,1,1,8,256]{5,4,3,2,1,0:T(8,128)(2,1)S(1)} collective-permute-done((bf16[2,2,1,1,8,256]{5,4,3,2,1,0:T(8,128)(2,1)S(1)}, bf16[2,2,1,1,8,256]{5,4,3,2,1,0:T(8,128)(2,1)S(1)}, u32[]{:S(2)}, u32[]{:S(2)}) %collective-permute-start.9) | collective-permute-done | bytes 16416 | tf_op jit(solution)/shard_map/ppermute | solution.py:23
  31.9 1.5 %collective-permute-start.13 = (bf16[2,2,2,1,8,256]{5,4,3,2,1,0:T(8,128)(2,1)S(1)}, bf16[2,2,2,1,8,256]{5,4,3,2,1,0:T(8,128)(2,1)S(1)}, u32[]{:S(2)}, u32[]{:S(2)}) collective-permute-start(bf16[2,2,2,1,8,256]{5,4,3,2,1,0:T(8,128)(2,1)S(1)} %pad_maximum_fusion.12), channel_id=1, source_target_pairs={{0,2},{1,3},{2,0},{3,1},{4,6},{5,7},{6,4},{7,5},{8,10},{9,11},{10,... | collective-permute-start | bytes 98312 | tf_op jit(solution)/shard_map/ppermute | solution.py:23
  33.4 5.6 %collective-permute-done.13 = bf16[2,2,2,1,8,256]{5,4,3,2,1,0:T(8,128)(2,1)S(1)} collective-permute-done((bf16[2,2,2,1,8,256]{5,4,3,2,1,0:T(8,128)(2,1)S(1)}, bf16[2,2,2,1,8,256]{5,4,3,2,1,0:T(8,128)(2,1)S(1)}, u32[]{:S(2)}, u32[]{:S(2)}) %collective-permute-start.13) | collective-permute-done | bytes 32800 | tf_op jit(solution)/shard_map/ppermute | solution.py:23
  45.4 3.1 %collective-permute-start.17 = (f32[2,192,128]{2,1,0:T(8,128)S(1)}, f32[2,192,128]{2,1,0:T(8,128)S(1)}, u32[]{:S(2)}, u32[]{:S(2)}) collective-permute-start(f32[2,192,128]{2,1,0:T(8,128)S(1)} %get-tuple-element.132), channel_id=1, source_target_pairs={{0,9},{1,10},{2,11},{3,12},{4,13},{5,14},{6,15},{7,16},{8,17},{9,1... | collective-permute-start | bytes 589832 | tf_op jit(solution)/shard_map/ppermute | solution.py:19
  50.7 2.8 %collective-permute-done.17 = f32[2,192,128]{2,1,0:T(8,128)S(1)} collective-permute-done((f32[2,192,128]{2,1,0:T(8,128)S(1)}, f32[2,192,128]{2,1,0:T(8,128)S(1)}, u32[]{:S(2)}, u32[]{:S(2)}) %collective-permute-start.17) | collective-permute-done | bytes 196640 | tf_op jit(solution)/shard_map/ppermute | solution.py:19
  53.5 3.0 %collective-permute-done.18 = f32[2,192,128]{2,1,0:T(8,128)S(1)} collective-permute-done((f32[2,192,128]{2,1,0:T(8,128)S(1)}, f32[2,192,128]{2,1,0:T(8,128)S(1)}, u32[]{:S(2)}, u32[]{:S(2)}) %collective-permute-start.18) | collective-permute-done | bytes 196640 | tf_op jit(solution)/shard_map/ppermute | solution.py:19
  57.6 5.5 %collective-permute-start.21 = (bf16[384,128]{1,0:T(8,128)(2,1)S(1)}, bf16[384,128]{1,0:T(8,128)(2,1)S(1)}, u32[]{:S(2)}, u32[]{:S(2)}) collective-permute-start(bf16[384,128]{1,0:T(8,128)(2,1)S(1)} %get-tuple-element.136), channel_id=1, source_target_pairs={{0,9},{1,10},{2,11},{3,12},{4,13},{5,14},{6,15},{7,16},{8,17},{9,1... | collective-permute-start | bytes 294920 | tf_op jit(solution)/shard_map/ppermute | solution.py:19
  66.5 2.6 %collective-permute-done.20.first_ref = bf16[384,128]{1,0:T(8,128)(2,1)S(1)} collective-permute-done((bf16[384,128]{1,0:T(8,128)(2,1)S(1)}, bf16[384,128]{1,0:T(8,128)(2,1)S(1)}, u32[]{:S(2)}, u32[]{:S(2)}) %collective-permute-start.20) | collective-permute-done | bytes 98336 | tf_op jit(solution)/shard_map/ppermute | solution.py:19
  70.9 1.5 %collective-permute-start.25 = (bf16[1024,512]{1,0:T(8,128)(2,1)S(1)}, bf16[1024,512]{1,0:T(8,128)(2,1)S(1)}, u32[]{:S(2)}, u32[]{:S(2)}) collective-permute-start(bf16[1024,512]{1,0:T(8,128)(2,1)S(1)} %convolution_convert_fusion), channel_id=1, source_target_pairs={{0,1},{1,0},{2,3},{3,2},{4,5},{5,4},{6,7},{7,6},{8,9},{9,8},{10,11... | collective-permute-start | bytes 3145736 | tf_op jit(solution)/shard_map/ppermute | solution.py:23
  73.6 3.8 %collective-permute-start.26 = (bf16[1,2,2,2,8,256]{5,4,3,2,1,0:T(8,128)(2,1)S(1)}, bf16[1,2,2,2,8,256]{5,4,3,2,1,0:T(8,128)(2,1)S(1)}, u32[]{:S(2)}, u32[]{:S(2)}) collective-permute-start(bf16[1,2,2,2,8,256]{5,4,3,2,1,0:T(8,128)(2,1)S(1)} %bitcast.130), channel_id=1, source_target_pairs={{0,16},{1,17},{2,18},{3,19},{4,20},{5,21},{6,22},{7,23},{8,24},{9,... | collective-permute-start | bytes 98312 | tf_op jit(solution)/shard_map/ppermute | solution.py:23
  80.2 5.9 %collective-permute-start.27 = (bf16[2,2,2,1,64,384]{5,4,3,2,1,0:T(8,128)(2,1)S(1)}, bf16[2,2,2,1,64,384]{5,4,3,2,1,0:T(8,128)(2,1)S(1)}, u32[]{:S(2)}, u32[]{:S(2)}) collective-permute-start(bf16[2,2,2,1,64,384]{5,4,3,2,1,0:T(8,128)(2,1)S(1)} %get-tuple-element.158), channel_id=1, source_target_pairs={{0,2},{1,3},{2,0},{3,1},{4,6},{5,7},{6,4},{7,5},{8,10},{9,11},{10,... | collective-permute-start | bytes 1179656 | tf_op jit(solution)/shard_map/ppermute | solution.py:23
  86.1 3.8 %input_gradient.1 = bf16[384,2048]{1,0:T(8,128)(2,1)} custom-call(s32[1]{0:T(128)} %bitcast.4.me_ref, bf16[384,384]{1,0:T(8,128)(2,1)S(1)} %get-tuple-element.166.refs_0_, bf16[384,384]{1,0:T(8,128)(2,1)S(1)} %get-tuple-element.167.refs_1_, bf16[384,512]{1,0:T(8,128)(2,1)S(1)} %get-tuple-element.168.refs_2_, bf16[1024,384]{1,0:T(8,128)(2,1)S(1)} %bitcast.102, ...), custom_call_target="tpu_custom_call" | custom-call | flops 2013265920 | bytes 7798784 | tf_op jit(solution)/shard_map/input_gradient/pallas_call | solution.py:171
  89.9 4.7 %collective-permute-done.30 = bf16[1,2,2,1,8,256]{5,4,3,2,1,0:T(8,128)(2,1)S(1)} collective-permute-done((bf16[1,2,2,1,8,256]{5,4,3,2,1,0:T(8,128)(2,1)S(1)}, bf16[1,2,2,1,8,256]{5,4,3,2,1,0:T(8,128)(2,1)S(1)}, u32[]{:S(2)}, u32[]{:S(2)}) %collective-permute-start.30) | collective-permute-done | bytes 16416 | tf_op jit(solution)/shard_map/ppermute | solution.py:23
  96.8 2.8 %collective-permute-start.32 = (bf16[2,1,2,1,64,384]{5,4,3,2,1,0:T(8,128)(2,1)S(1)}, bf16[2,1,2,1,64,384]{5,4,3,2,1,0:T(8,128)(2,1)S(1)}, u32[]{:S(2)}, u32[]{:S(2)}) collective-permute-start(bf16[2,1,2,1,64,384]{5,4,3,2,1,0:T(8,128)(2,1)S(1)} %get-tuple-element.175), channel_id=1, source_target_pairs={{0,2},{1,3},{2,0},{3,1},{4,6},{5,7},{6,4},{7,5},{8,10},{9,11},{10,... | collective-permute-start | bytes 589832 | tf_op jit(solution)/shard_map/ppermute | solution.py:23
  99.9 3.4 %collective-permute-done.34 = bf16[1,2,1,1,8,256]{5,4,3,2,1,0:T(8,128)(2,1)S(1)} collective-permute-done((bf16[1,2,1,1,8,256]{5,4,3,2,1,0:T(8,128)(2,1)S(1)}, bf16[1,2,1,1,8,256]{5,4,3,2,1,0:T(8,128)(2,1)S(1)}, u32[]{:S(2)}, u32[]{:S(2)}) %collective-permute-start.34) | collective-permute-done | bytes 8224 | tf_op jit(solution)/shard_map/ppermute | solution.py:23
  103.4 2.1 %collective-permute-start.37 = (bf16[2,1,1,1,64,512]{5,4,3,2,1,0:T(8,128)(2,1)S(1)}, bf16[2,1,1,1,64,512]{5,4,3,2,1,0:T(8,128)(2,1)S(1)}, u32[]{:S(2)}, u32[]{:S(2)}) collective-permute-start(bf16[2,1,1,1,64,512]{5,4,3,2,1,0:T(8,128)(2,1)S(1)} %fusion.17), channel_id=1, source_target_pairs={{0,2},{1,3},{2,0},{3,1},{4,6},{5,7},{6,4},{7,5},{8,10},{9,11},{10,... | collective-permute-start | bytes 393224 | tf_op jit(solution)/shard_map/ppermute | solution.py:23
  105.5 2.2 %collective-permute-start.35 = (bf16[2,1,1,1,64,384]{5,4,3,2,1,0:T(8,128)(2,1)S(1)}, bf16[2,1,1,1,64,384]{5,4,3,2,1,0:T(8,128)(2,1)S(1)}, u32[]{:S(2)}, u32[]{:S(2)}) collective-permute-start(bf16[2,1,1,1,64,384]{5,4,3,2,1,0:T(8,128)(2,1)S(1)} %fusion.22), channel_id=1, source_target_pairs={{0,8},{1,9},{2,10},{3,11},{4,12},{5,13},{6,14},{7,15},{8,0},{9,1},... | collective-permute-start | bytes 294920 | tf_op jit(solution)/shard_map/ppermute | solution.py:23
  108.1 3.2 %collective-permute-done.38 = bf16[1,1,1,1,8,256]{5,4,3,2,1,0:T(8,128)(2,1)S(1)} collective-permute-done((bf16[1,1,1,1,8,256]{5,4,3,2,1,0:T(8,128)(2,1)S(1)}, bf16[1,1,1,1,8,256]{5,4,3,2,1,0:T(8,128)(2,1)S(1)}, u32[]{:S(2)}, u32[]{:S(2)}) %collective-permute-start.38) | collective-permute-done | bytes 4128 | tf_op jit(solution)/shard_map/ppermute | solution.py:23
  113.2 7.4 %collective-permute-done.39 = bf16[1,1,1,1,64,1280]{5,4,3,2,1,0:T(8,128)(2,1)S(1)} collective-permute-done((bf16[1,1,1,1,64,1280]{5,4,3,2,1,0:T(8,128)(2,1)S(1)}, bf16[1,1,1,1,64,1280]{5,4,3,2,1,0:T(8,128)(2,1)S(1)}, u32[]{:S(2)}, u32[]{:S(2)}) %collective-permute-start.39) | collective-permute-done | bytes 163872 | tf_op jit(solution)/shard_map/ppermute | solution.py:23
  (147 shorter events, 37.1 us)
Async XLA Ops:
  1.6 12.0 %collective-permute-start = (bf16[1,1,1,1,64,1280]{5,4,3,2,1,0:T(8,128)(2,1)S(1)}, bf16[1,1,1,1,64,1280]{5,4,3,2,1,0:T(8,128)(2,1)S(1)}, u32[]{:S(2)}, u32[]{:S(2)}) collective-permute-start(bf16[1,1,1,1,64,1280]{5,4,3,2,1,0:T(8,128)(2,1)S(1)} %bitcast.107), channel_id=1, source_target_pairs={{0,16},{1,17},{2,18},{3,19},{4,20},{5,21},{6,22},{7,23},{8,24},{9,... | collective-permute-start | bytes 491528 | tf_op jit(solution)/shard_map/ppermute | solution.py:23
  5.7 7.9 %collective-permute-start.1 = (bf16[1,1,1,1,8,256]{5,4,3,2,1,0:T(8,128)(2,1)}, bf16[1,1,1,1,8,256]{5,4,3,2,1,0:T(8,128)(2,1)S(1)}, u32[]{:S(2)}, u32[]{:S(2)}) collective-permute-start(bf16[1,1,1,1,8,256]{5,4,3,2,1,0:T(8,128)(2,1)} %bitcast.131), channel_id=1, source_target_pairs={{0,16},{1,17},{2,18},{3,19},{4,20},{5,21},{6,22},{7,23},{8,24},{9,... | collective-permute-start | bytes 12296 | tf_op jit(solution)/shard_map/ppermute | solution.py:23
  13.7 7.5 %collective-permute-start.4 = (bf16[2,1,1,1,64,512]{5,4,3,2,1,0:T(8,128)(2,1)S(1)}, bf16[2,1,1,1,64,512]{5,4,3,2,1,0:T(8,128)(2,1)S(1)}, u32[]{:S(2)}, u32[]{:S(2)}) collective-permute-start(bf16[2,1,1,1,64,512]{5,4,3,2,1,0:T(8,128)(2,1)S(1)} %slice.228), channel_id=1, source_target_pairs={{0,2},{1,3},{2,0},{3,1},{4,6},{5,7},{6,4},{7,5},{8,10},{9,11},{10,... | collective-permute-start | bytes 393224 | tf_op jit(solution)/shard_map/ppermute | solution.py:23
  21.3 8.0 %collective-permute-start.8 = (bf16[2,1,1,2,64,512]{5,4,3,2,1,0:T(8,128)(2,1)S(1)}, bf16[2,1,1,2,64,512]{5,4,3,2,1,0:T(8,128)(2,1)S(1)}, u32[]{:S(2)}, u32[]{:S(2)}) collective-permute-start(bf16[2,1,1,2,64,512]{5,4,3,2,1,0:T(8,128)(2,1)S(1)} %pad_maximum_fusion.8), channel_id=1, source_target_pairs={{0,8},{1,9},{2,10},{3,11},{4,12},{5,13},{6,14},{7,15},{8,0},{9,1},... | collective-permute-start | bytes 786440 | tf_op jit(solution)/shard_map/ppermute | solution.py:23
  22.7 5.9 %collective-permute-start.6 = (bf16[2,2,1,1,64,384]{5,4,3,2,1,0:T(8,128)(2,1)S(1)}, bf16[2,2,1,1,64,384]{5,4,3,2,1,0:T(8,128)(2,1)S(1)}, u32[]{:S(2)}, u32[]{:S(2)}) collective-permute-start(bf16[2,2,1,1,64,384]{5,4,3,2,1,0:T(8,128)(2,1)S(1)} %pad_maximum_fusion.9), channel_id=1, source_target_pairs={{0,4},{1,5},{2,6},{3,7},{4,0},{5,1},{6,2},{7,3},{8,12},{9,13},{10,... | collective-permute-start | bytes 589832 | tf_op jit(solution)/shard_map/ppermute | solution.py:23
  29.5 10.3 %collective-permute-start.12 = (bf16[2,2,1,2,64,512]{5,4,3,2,1,0:T(8,128)(2,1)S(1)}, bf16[2,2,1,2,64,512]{5,4,3,2,1,0:T(8,128)(2,1)S(1)}, u32[]{:S(2)}, u32[]{:S(2)}) collective-permute-start(bf16[2,2,1,2,64,512]{5,4,3,2,1,0:T(8,128)(2,1)S(1)} %pad_maximum_fusion.4), channel_id=1, source_target_pairs={{0,4},{1,5},{2,6},{3,7},{4,0},{5,1},{6,2},{7,3},{8,12},{9,13},{10,... | collective-permute-start | bytes 1572872 | tf_op jit(solution)/shard_map/ppermute | solution.py:23
  30.8 8.1 %collective-permute-start.10 = (bf16[2,2,2,1,64,384]{5,4,3,2,1,0:T(8,128)(2,1)S(1)}, bf16[2,2,2,1,64,384]{5,4,3,2,1,0:T(8,128)(2,1)S(1)}, u32[]{:S(2)}, u32[]{:S(2)}) collective-permute-start(bf16[2,2,2,1,64,384]{5,4,3,2,1,0:T(8,128)(2,1)S(1)} %pad_maximum_fusion.5), channel_id=1, source_target_pairs={{0,2},{1,3},{2,0},{3,1},{4,6},{5,7},{6,4},{7,5},{8,10},{9,11},{10,... | collective-permute-start | bytes 1179656 | tf_op jit(solution)/shard_map/ppermute | solution.py:23
  31.2 7.8 %collective-permute-start.11 = (bf16[2,1,2,2,64,384]{5,4,3,2,1,0:T(8,128)(2,1)S(1)}, bf16[2,1,2,2,64,384]{5,4,3,2,1,0:T(8,128)(2,1)S(1)}, u32[]{:S(2)}, u32[]{:S(2)}) collective-permute-start(bf16[2,1,2,2,64,384]{5,4,3,2,1,0:T(8,128)(2,1)S(1)} %pad_maximum_fusion.6), channel_id=1, source_target_pairs={{0,8},{1,9},{2,10},{3,11},{4,12},{5,13},{6,14},{7,15},{8,0},{9,1},... | collective-permute-start | bytes 1179656 | tf_op jit(solution)/shard_map/ppermute | solution.py:23
  31.9 7.1 %collective-permute-start.13 = (bf16[2,2,2,1,8,256]{5,4,3,2,1,0:T(8,128)(2,1)S(1)}, bf16[2,2,2,1,8,256]{5,4,3,2,1,0:T(8,128)(2,1)S(1)}, u32[]{:S(2)}, u32[]{:S(2)}) collective-permute-start(bf16[2,2,2,1,8,256]{5,4,3,2,1,0:T(8,128)(2,1)S(1)} %pad_maximum_fusion.12), channel_id=1, source_target_pairs={{0,2},{1,3},{2,0},{3,1},{4,6},{5,7},{6,4},{7,5},{8,10},{9,11},{10,... | collective-permute-start | bytes 98312 | tf_op jit(solution)/shard_map/ppermute | solution.py:23
  45.4 8.1 %collective-permute-start.17 = (f32[2,192,128]{2,1,0:T(8,128)S(1)}, f32[2,192,128]{2,1,0:T(8,128)S(1)}, u32[]{:S(2)}, u32[]{:S(2)}) collective-permute-start(f32[2,192,128]{2,1,0:T(8,128)S(1)} %get-tuple-element.132), channel_id=1, source_target_pairs={{0,9},{1,10},{2,11},{3,12},{4,13},{5,14},{6,15},{7,16},{8,17},{9,1... | collective-permute-start | bytes 589832 | tf_op jit(solution)/shard_map/ppermute | solution.py:19
  48.6 8.0 %collective-permute-start.18 = (f32[2,192,128]{2,1,0:T(8,128)S(1)}, f32[2,192,128]{2,1,0:T(8,128)S(1)}, u32[]{:S(2)}, u32[]{:S(2)}) collective-permute-start(f32[2,192,128]{2,1,0:T(8,128)S(1)} %get-tuple-element.133), channel_id=1, source_target_pairs={{9,0},{10,1},{11,2},{12,3},{13,4},{14,5},{15,6},{16,7},{17,8},{18,... | collective-permute-start | bytes 589832 | tf_op jit(solution)/shard_map/ppermute | solution.py:19
  57.6 8.9 %collective-permute-start.21 = (bf16[384,128]{1,0:T(8,128)(2,1)S(1)}, bf16[384,128]{1,0:T(8,128)(2,1)S(1)}, u32[]{:S(2)}, u32[]{:S(2)}) collective-permute-start(bf16[384,128]{1,0:T(8,128)(2,1)S(1)} %get-tuple-element.136), channel_id=1, source_target_pairs={{0,9},{1,10},{2,11},{3,12},{4,13},{5,14},{6,15},{7,16},{8,17},{9,1... | collective-permute-start | bytes 294920 | tf_op jit(solution)/shard_map/ppermute | solution.py:19
  70.9 8.4 %collective-permute-start.25 = (bf16[1024,512]{1,0:T(8,128)(2,1)S(1)}, bf16[1024,512]{1,0:T(8,128)(2,1)S(1)}, u32[]{:S(2)}, u32[]{:S(2)}) collective-permute-start(bf16[1024,512]{1,0:T(8,128)(2,1)S(1)} %convolution_convert_fusion), channel_id=1, source_target_pairs={{0,1},{1,0},{2,3},{3,2},{4,5},{5,4},{6,7},{7,6},{8,9},{9,8},{10,11... | collective-permute-start | bytes 3145736 | tf_op jit(solution)/shard_map/ppermute | solution.py:23
  72.4 7.0 %collective-permute-start.23 = (bf16[1024,384]{1,0:T(8,128)(2,1)S(1)}, bf16[1024,384]{1,0:T(8,128)(2,1)S(1)}, u32[]{:S(2)}, u32[]{:S(2)}) collective-permute-start(bf16[1024,384]{1,0:T(8,128)(2,1)S(1)} %convolution_convert_fusion.2), channel_id=1, source_target_pairs={{0,1},{1,0},{2,3},{3,2},{4,5},{5,4},{6,7},{7,6},{8,9},{9,8},{10,11... | collective-permute-start | bytes 2359304 | tf_op jit(solution)/shard_map/ppermute | solution.py:23
  72.4 6.9 %collective-permute-start.24 = (bf16[1024,384]{1,0:T(8,128)(2,1)S(1)}, bf16[1024,384]{1,0:T(8,128)(2,1)S(1)}, u32[]{:S(2)}, u32[]{:S(2)}) collective-permute-start(bf16[1024,384]{1,0:T(8,128)(2,1)S(1)} %convolution_convert_fusion.1), channel_id=1, source_target_pairs={{0,1},{1,0},{2,3},{3,2},{4,5},{5,4},{6,7},{7,6},{8,9},{9,8},{10,11... | collective-permute-start | bytes 2359304 | tf_op jit(solution)/shard_map/ppermute | solution.py:23
  80.1 15.6 %collective-permute-start.29 = (bf16[2,2,1,2,64,512]{5,4,3,2,1,0:T(8,128)(2,1)S(1)}, bf16[2,2,1,2,64,512]{5,4,3,2,1,0:T(8,128)(2,1)S(1)}, u32[]{:S(2)}, u32[]{:S(2)}) collective-permute-start(bf16[2,2,1,2,64,512]{5,4,3,2,1,0:T(8,128)(2,1)S(1)} %get-tuple-element.160), channel_id=1, source_target_pairs={{0,4},{1,5},{2,6},{3,7},{4,0},{5,1},{6,2},{7,3},{8,12},{9,13},{10,... | collective-permute-start | bytes 1572872 | tf_op jit(solution)/shard_map/ppermute | solution.py:23
  80.2 14.4 %collective-permute-start.27 = (bf16[2,2,2,1,64,384]{5,4,3,2,1,0:T(8,128)(2,1)S(1)}, bf16[2,2,2,1,64,384]{5,4,3,2,1,0:T(8,128)(2,1)S(1)}, u32[]{:S(2)}, u32[]{:S(2)}) collective-permute-start(bf16[2,2,2,1,64,384]{5,4,3,2,1,0:T(8,128)(2,1)S(1)} %get-tuple-element.158), channel_id=1, source_target_pairs={{0,2},{1,3},{2,0},{3,1},{4,6},{5,7},{6,4},{7,5},{8,10},{9,11},{10,... | collective-permute-start | bytes 1179656 | tf_op jit(solution)/shard_map/ppermute | solution.py:23
  86.1 9.6 %collective-permute-start.28 = (bf16[2,1,2,2,64,384]{5,4,3,2,1,0:T(8,128)(2,1)S(1)}, bf16[2,1,2,2,64,384]{5,4,3,2,1,0:T(8,128)(2,1)S(1)}, u32[]{:S(2)}, u32[]{:S(2)}) collective-permute-start(bf16[2,1,2,2,64,384]{5,4,3,2,1,0:T(8,128)(2,1)S(1)} %get-tuple-element.159), channel_id=1, source_target_pairs={{0,8},{1,9},{2,10},{3,11},{4,12},{5,13},{6,14},{7,15},{8,0},{9,1},... | collective-permute-start | bytes 1179656 | tf_op jit(solution)/shard_map/ppermute | solution.py:23
  86.1 8.5 %collective-permute-start.30 = (bf16[1,2,2,1,8,256]{5,4,3,2,1,0:T(8,128)(2,1)S(1)}, bf16[1,2,2,1,8,256]{5,4,3,2,1,0:T(8,128)(2,1)S(1)}, u32[]{:S(2)}, u32[]{:S(2)}) collective-permute-start(bf16[1,2,2,1,8,256]{5,4,3,2,1,0:T(8,128)(2,1)S(1)} %slice.468), channel_id=1, source_target_pairs={{0,2},{1,3},{2,0},{3,1},{4,6},{5,7},{6,4},{7,5},{8,10},{9,11},{10,... | collective-permute-start | bytes 49160 | tf_op jit(solution)/shard_map/ppermute | solution.py:23
  96.1 7.2 %collective-permute-start.33 = (bf16[2,1,1,2,64,512]{5,4,3,2,1,0:T(8,128)(2,1)S(1)}, bf16[2,1,1,2,64,512]{5,4,3,2,1,0:T(8,128)(2,1)S(1)}, u32[]{:S(2)}, u32[]{:S(2)}) collective-permute-start(bf16[2,1,1,2,64,512]{5,4,3,2,1,0:T(8,128)(2,1)S(1)} %get-tuple-element.176), channel_id=1, source_target_pairs={{0,8},{1,9},{2,10},{3,11},{4,12},{5,13},{6,14},{7,15},{8,0},{9,1},... | collective-permute-start | bytes 786440 | tf_op jit(solution)/shard_map/ppermute | solution.py:23
  96.4 6.8 %collective-permute-start.31 = (bf16[2,2,1,1,64,384]{5,4,3,2,1,0:T(8,128)(2,1)S(1)}, bf16[2,2,1,1,64,384]{5,4,3,2,1,0:T(8,128)(2,1)S(1)}, u32[]{:S(2)}, u32[]{:S(2)}) collective-permute-start(bf16[2,2,1,1,64,384]{5,4,3,2,1,0:T(8,128)(2,1)S(1)} %get-tuple-element.174), channel_id=1, source_target_pairs={{0,4},{1,5},{2,6},{3,7},{4,0},{5,1},{6,2},{7,3},{8,12},{9,13},{10,... | collective-permute-start | bytes 589832 | tf_op jit(solution)/shard_map/ppermute | solution.py:23
  96.8 6.5 %collective-permute-start.32 = (bf16[2,1,2,1,64,384]{5,4,3,2,1,0:T(8,128)(2,1)S(1)}, bf16[2,1,2,1,64,384]{5,4,3,2,1,0:T(8,128)(2,1)S(1)}, u32[]{:S(2)}, u32[]{:S(2)}) collective-permute-start(bf16[2,1,2,1,64,384]{5,4,3,2,1,0:T(8,128)(2,1)S(1)} %get-tuple-element.175), channel_id=1, source_target_pairs={{0,2},{1,3},{2,0},{3,1},{4,6},{5,7},{6,4},{7,5},{8,10},{9,11},{10,... | collective-permute-start | bytes 589832 | tf_op jit(solution)/shard_map/ppermute | solution.py:23
  103.4 9.0 %collective-permute-start.37 = (bf16[2,1,1,1,64,512]{5,4,3,2,1,0:T(8,128)(2,1)S(1)}, bf16[2,1,1,1,64,512]{5,4,3,2,1,0:T(8,128)(2,1)S(1)}, u32[]{:S(2)}, u32[]{:S(2)}) collective-permute-start(bf16[2,1,1,1,64,512]{5,4,3,2,1,0:T(8,128)(2,1)S(1)} %fusion.17), channel_id=1, source_target_pairs={{0,2},{1,3},{2,0},{3,1},{4,6},{5,7},{6,4},{7,5},{8,10},{9,11},{10,... | collective-permute-start | bytes 393224 | tf_op jit(solution)/shard_map/ppermute | solution.py:23
  112.6 8.0 %collective-permute-start.39 = (bf16[1,1,1,1,64,1280]{5,4,3,2,1,0:T(8,128)(2,1)S(1)}, bf16[1,1,1,1,64,1280]{5,4,3,2,1,0:T(8,128)(2,1)S(1)}, u32[]{:S(2)}, u32[]{:S(2)}) collective-permute-start(bf16[1,1,1,1,64,1280]{5,4,3,2,1,0:T(8,128)(2,1)S(1)} %slice.466), channel_id=1, source_target_pairs={{0,16},{1,17},{2,18},{3,19},{4,20},{5,21},{6,22},{7,23},{8,24},{9,... | collective-permute-start | bytes 491528 | tf_op jit(solution)/shard_map/ppermute | solution.py:23
  (22 other events, 109.5 us)

commit v4 on v3

--- a/solution.py
+++ b/solution.py
@@ -13,10 +13,10 @@
 PORTIONS = ((1, 2, 3), (7, 8, 9), (0, 4, 5, 6))
 
 
-def passed_along(block, distance):
-    devices = range(lax.axis_size("row"))
-    route = [(i - distance, i) for i in devices if i - distance in devices]
-    return lax.ppermute(block, "row", route)
+def swapped(block, distance, parity):
+    count = lax.axis_size("row")
+    pairs = [(i, i + distance) for i in range(count - distance) if i // distance % 2 == parity]
+    return lax.ppermute(block, "row", pairs + [(b, a) for a, b in pairs])
 
 
 def exchanged(block, bit):
@@ -118,24 +118,6 @@
         compiler_params=pltpu.CompilerParams(vmem_limit_bytes=12 << 20),
         name="reorder",
     )(me.reshape(1), flat)
-
-
-def kernel_rows_kernel(order, w_ref, out_ref):
-    for place, k in enumerate(order):
-        out_ref[:, place * LANES : (place + 1) * LANES] = w_ref[k]
-
-
-def kernel_rows(weight, order):
-    taps, rows, branch = weight.shape
-    return pl.pallas_call(
-        functools.partial(kernel_rows_kernel, order),
-        out_shape=jax.ShapeDtypeStruct((rows, taps * branch), weight.dtype),
-        in_specs=[pl.BlockSpec(memory_space=pltpu.VMEM)],
-        out_specs=pl.BlockSpec(memory_space=pltpu.VMEM),
-        cost_estimate=pl.CostEstimate(flops=0, bytes_accessed=4 * weight.size, transcendentals=0),
-        compiler_params=pltpu.CompilerParams(vmem_limit_bytes=4 << 20),
-        name="kernel_rows",
-    )(weight)
 
 
 def input_gradient_kernel(portion_count, me_ref, *refs):
@@ -242,29 +224,62 @@
     )(*operands)
 
 
-def shift_kernel(width, first_ref, second_ref, first_out_ref, second_out_ref):
+def is_upward(me, step):
+    return me // step % 2 == 0
+
+
+def halo_kernel(width, step, me_ref, first_ref, second_ref, first_out_ref, second_out_ref):
+    branch = first_out_ref.shape[1]
+    sums = []
+    for ref in (first_ref, second_ref):
+        total = None
+        for j in range(3):
+            part = ref[:, j * branch : (j + 1) * branch]
+            moved = moved_rows(part, width, (j - 1) * DILATION_RATE)
+            total = moved if total is None else total + moved
+        sums.append(total)
+    upward = is_upward(me_ref[0], step)
+    first_out_ref[...] = jnp.where(upward, sums[0], sums[1])
+    second_out_ref[...] = jnp.where(upward, sums[1], sums[0])
+
+
+def halo_sums(width, step, products, me):
+    pixels, taps = products[0].shape
+    out = jax.ShapeDtypeStruct((pixels, taps // 3), jnp.float32)
+    return halo_call(functools.partial(halo_kernel, width, step), "halo_sums", out, me, *products)
+
+
+def shift_kernel(width, step, me_ref, first_ref, second_ref, first_out_ref, second_out_ref):
     branch = first_ref.shape[1]
-    for ref, out_ref in ((first_ref, first_out_ref), (second_ref, second_out_ref)):
-        block = ref[...].astype(jnp.float32)
+    upward = is_upward(me_ref[0], step)
+    first, second = first_ref[...].astype(jnp.float32), second_ref[...].astype(jnp.float32)
+    pairs = ((first, second, first_out_ref), (second, first, second_out_ref))
+    for here, there, out_ref in pairs:
+        block = jnp.where(upward, here, there)
         for j in range(3):
             moved = moved_rows(block, width, (1 - j) * DILATION_RATE)
             out_ref[:, j * branch : (j + 1) * branch] = moved.astype(jnp.bfloat16)
 
 
-def shifted(width, first, second):
+def shifted(width, step, first, second, me):
     pixels, branch = first.shape
     out = jax.ShapeDtypeStruct((pixels, 3 * branch), jnp.bfloat16)
+    return halo_call(functools.partial(shift_kernel, width, step), "shift", out, me, first, second)
+
+
+def halo_call(kernel, name, out, me, first, second):
     return pl.pallas_call(
-        functools.partial(shift_kernel, width),
+        kernel,
         out_shape=(out, out),
-        in_specs=[pl.BlockSpec(memory_space=pltpu.VMEM)] * 2,
+        in_specs=[pl.BlockSpec(memory_space=pltpu.SMEM)]
+        + [pl.BlockSpec(memory_space=pltpu.VMEM)] * 2,
         out_specs=(pl.BlockSpec(memory_space=pltpu.VMEM),) * 2,
         cost_estimate=pl.CostEstimate(
-            flops=0, bytes_accessed=16 * pixels * branch, transcendentals=0
+            flops=0, bytes_accessed=8 * (first.size + out.size), transcendentals=0
         ),
         compiler_params=pltpu.CompilerParams(vmem_limit_bytes=8 << 20),
-        name="shift",
-    )(first, second)
+        name=name,
+    )(me.reshape(1), first, second)
 
 
 def merge_gradient_kernel(me_ref, joined_ref, grad_out_ref, own_ref, other_ref, total_ref):
@@ -300,6 +315,178 @@
     )(me.reshape(1), joined, grad_out)
 
 
+def layout(rows, merge_rows, merge_width):
+    shares = (0, 3 * rows // 8, 6 * rows // 8, rows)
+    tables = []
+    for p, portion in enumerate(PORTIONS):
+        table = [(k, 0, n * rows, rows) for n, k in enumerate(k for k in portion if k > 0)]
+        table.append((0, shares[p], 3 * rows, shares[p + 1] - shares[p]))
+        if p == 2:
+            first = 3 * rows + table[-1][3]
+            lanes = range(0, merge_width, LANES)
+            table += [(None, x, first + n * merge_rows, merge_rows) for n, x in enumerate(lanes)]
+        tables.append(table)
+    return tables
+
+
+def stack_rows(table):
+    return table[-1][2] + table[-1][3]
+
+
+def lanes_of(k):
+    for p, portion in enumerate(PORTIONS):
+        if k in portion:
+            at = portion.index(k) * LANES
+            return p, slice(at, at + LANES)
+
+
+def local_call(kernel, name, out_shape, operands, moved, grant):
+    return pl.pallas_call(
+        kernel,
+        out_shape=out_shape,
+        in_specs=[pl.BlockSpec(memory_space=pltpu.VMEM)] * len(operands),
+        out_specs=[pl.BlockSpec(memory_space=pltpu.VMEM)] * len(out_shape),
+        cost_estimate=pl.CostEstimate(flops=moved // 4, bytes_accessed=moved, transcendentals=0),
+        compiler_params=pltpu.CompilerParams(vmem_limit_bytes=grant << 20),
+        name=name,
+    )(*operands)
+
+
+def pack_kernel(tables, weight_ref, merge_ref, out_ref):
+    base = 0
+    for table in tables:
+        for k, there, here, count in table:
+            at = slice(base + here, base + here + count)
+            if k is None:
+                out_ref[at, :] = merge_ref[:, there : there + LANES]
+            else:
+                out_ref[at, :] = weight_ref[k, there : there + count, :]
+        base += stack_rows(table)
+
+
+def pack(weight, merge_weight, tables):
+    out = [jax.ShapeDtypeStruct((sum(map(stack_rows, tables)), LANES), weight.dtype)]
+    kernel = functools.partial(pack_kernel, tables)
+    return local_call(kernel, "pack", out, (weight, merge_weight), 4 * weight.size, 4)[0]
+
+
+def block_pair(target, inner):
+    low = target // inner * (2 * inner) + target % inner
+    return low, low + inner
+
+
+def unpack_kernel(tables, inners, *refs):
+    outs = refs[6:]
+
+    def step(target, carry):
+        for p, table in enumerate(tables):
+            for ref, block in zip(refs[2 * p : 2 * p + 2], block_pair(target, inners[p])):
+                for k, there, here, count in table:
+                    value = ref[target, here : here + count, :]
+                    if k is None:
+                        outs[3][block, :, there : there + LANES] = value
+                    else:
+                        q, lanes = lanes_of(k)
+                        outs[q][block, there : there + count, lanes] = value
+        return carry
+
+    lax.fori_loop(0, refs[0].shape[0], step, 0)
+
+
+def unpack(pairs, tables, inners, rows, merge_rows, merge_width):
+    blocks = 2 * pairs[0].shape[0]
+    shapes = [(blocks, rows, LANES * len(p)) for p in PORTIONS] + [(blocks, merge_rows, merge_width)]
+    out = [jax.ShapeDtypeStruct(x, jnp.bfloat16) for x in shapes]
+    kernel = functools.partial(unpack_kernel, tables, tuple(inners))
+    return local_call(kernel, "unpack", out, pairs, 4 * sum(x.size for x in pairs), 16)
+
+
+def first_fold_kernel(tables, inners, *refs):
+    owns, arriveds, keeps, sends = refs[:4], refs[4:8], refs[8:11], refs[11:]
+
+    def step(target, carry):
+        for p, table in enumerate(tables):
+            for half, block in enumerate(block_pair(target, inners[p])):
+                for k, there, here, count in table:
+                    if k is None:
+                        q, at = 3, (block, slice(None), slice(there, there + LANES))
+                    else:
+                        q, lanes = lanes_of(k)
+                        at = (block, slice(there, there + count), lanes)
+                    value = owns[q][at] + arriveds[q][at].astype(jnp.float32)
+                    out_ref = (keeps, sends)[half][p]
+                    out_ref[target, here : here + count, :] = value.astype(out_ref.dtype)
+        return carry
+
+    lax.fori_loop(0, keeps[0].shape[0], step, 0)
+
+
+def fold_kernel(inners, *refs):
+    owns, arriveds, keeps, sends = (refs[3 * k : 3 * k + 3] for k in range(4))
+
+    def step(target, carry):
+        for p in range(3):
+            for half, block in enumerate(block_pair(target, inners[p])):
+                value = owns[p][block] + arriveds[p][block].astype(jnp.float32)
+                out_ref = (keeps, sends)[half][p]
+                out_ref[target] = value.astype(out_ref.dtype)
+        return carry
+
+    lax.fori_loop(0, keeps[0].shape[0], step, 0)
+
+
+def fold(owns, arriveds, tables, inners):
+    shapes = [(owns[0].shape[0] // 2, stack_rows(table), LANES) for table in tables]
+    out = [jax.ShapeDtypeStruct(x, t) for t in (jnp.float32, jnp.bfloat16) for x in shapes]
+    if len(owns) == 4:
+        kernel = functools.partial(first_fold_kernel, tables, tuple(inners))
+    else:
+        kernel = functools.partial(fold_kernel, tuple(inners))
+    moved = 9 * sum(x.size for x in owns)
+    out = local_call(kernel, "fold", out, (*owns, *arriveds), moved, 20)
+    return out[:3], out[3:]
+
+
+def last_fold_kernel(*refs):
+    owns, arriveds = refs[:3], refs[3:6]
+    base = 0
+    for own, arrived in zip(owns, arriveds):
+        at = slice(base, base + own.shape[1])
+        base += own.shape[1]
+        refs[6][at, :] = own[0] + arrived[0].astype(jnp.float32)
+        refs[7][at, :] = (own[1] + arrived[1].astype(jnp.float32)).astype(jnp.bfloat16)
+
+
+def last_fold(owns, arriveds):
+    shape = (sum(x.shape[1] for x in owns), LANES)
+    out = [jax.ShapeDtypeStruct(shape, t) for t in (jnp.float32, jnp.bfloat16)]
+    moved = 9 * sum(x.size for x in owns)
+    return local_call(last_fold_kernel, "last_fold", out, (*owns, *arriveds), moved, 8)
+
+
+def scaled_kernel(tables, scale, keep_ref, arrived_ref, out_ref, out_merge_ref):
+    base = 0
+    for table in tables:
+        for k, there, here, count in table:
+            at = slice(base + here, base + here + count)
+            value = (keep_ref[at, :] + arrived_ref[at, :].astype(jnp.float32)) * scale
+            if k is None:
+                out_merge_ref[:, there : there + LANES] = value
+            else:
+                out_ref[k, there : there + count, :] = value
+        base += stack_rows(table)
+
+
+def scaled(keep, arrived, tables, scale, rows, merge_rows, merge_width):
+    taps = sum(map(len, PORTIONS))
+    out = [
+        jax.ShapeDtypeStruct((taps, rows, LANES), jnp.float32),
+        jax.ShapeDtypeStruct((merge_rows, merge_width), jnp.float32),
+    ]
+    kernel = functools.partial(scaled_kernel, tables, scale)
+    return local_call(kernel, "scaled", out, (keep, arrived), 10 * keep.size, 8)
+
+
 def column_shifted(rows, shift):
     width = rows.shape[1]
     if shift == 0:
@@ -326,7 +513,7 @@
     bits = (1,) * (bit_count - 1)
     orders = bit_orders(bit_count)
     far_bits = list(range(bit_count - 1, 3, -1))
-    paired = 2 * own_channels == LANES and joined_rows == 8 and branch == LANES
+    paired = 2 * own_channels == LANES and joined_rows == 8 and branch == LANES and bit_count == 5
     portion_widths = [len(p) * branch for p in PORTIONS]
 
     def split(array, widths):
@@ -335,30 +522,53 @@
 
     tap_order = [k for portion in PORTIONS for k in portion]
     weight = branch_kernel_weight.transpose(1, 0, 2)
-    if branch == LANES and own_channels % 16 == 0:
-        block = kernel_rows(weight, tap_order)
+    half_rows = channels // 2
+    crossing = orders + [orders[1]]
+    flat = features.reshape(pixels, channels)
+    if paired:
+        tables = layout(own_channels, joined_rows, merged_width)
+        block = pack(weight, merge_weight, tables)
+        block, flat, me = together(block, flat, me)
+        flat_own, flat_other = reordered(flat, me)
+        block = block.reshape(bits + block.shape)
+        (arrived,) = together(exchanged(block, far_bits[0]))
+        block, arrived, flat_own, flat_other = together(block, arrived, flat_own, flat_other)
+        blocks, base = [], 0
+        for table in tables:
+            parts = [
+                lax.slice_in_dim(x, base, base + stack_rows(table), axis=-2) for x in (block, arrived)
+            ]
+            blocks.append(jnp.concatenate(parts, axis=0))
+            base += stack_rows(table)
+        for step in range(len(orders[0]) - 1):
+            blocks = gathered(together(*blocks), [o[step] for o in orders], bit_count)
+        blocks = together(*blocks)
+        arrived = together(*[exchanged(b, o[-1]) for b, o in zip(blocks, orders)])
+        pairs = [
+            x.reshape((device_count // 4,) + x.shape[-2:])
+            for pair in zip(blocks, arrived)
+            for x in pair
+        ]
+        inners = [1 << (o[-1] - 1) for o in orders]
+        *own_weight, own_merge = unpack(
+            pairs, tables, inners, own_channels, joined_rows, merged_width
+        )
+        own_weight = [x.reshape(half_rows, x.shape[-1]) for x in own_weight]
     else:
         block = jnp.concatenate([weight[k] for k in tap_order], axis=1)
-    block, flat, me = together(block, features.reshape(pixels, channels), me)
-    half_rows = channels // 2
-    if paired:
-        flat_own, flat_other = reordered(flat, me)
-    else:
         to_relative = relative_order(channels, device_count, me)
         flat = dot_f32(flat, to_relative, 1, 0).astype(jnp.bfloat16)
         flat_own, flat_other = flat[:, :half_rows], flat[:, half_rows:]
-    block = block.reshape(bits + block.shape)
-    merge_block = merge_weight.reshape(bits + merge_weight.shape)
-    for bit in far_bits:
-        block, merge_block = gathered([block, merge_block], [bit, bit], bit_count)
-    block, flat_own, flat_other = together(block, flat_own, flat_other)
-    blocks = split(block, portion_widths)
-    blocks.append(merge_block)
-    crossing = orders + [orders[0]]
-    for step in range(len(orders[0])):
-        blocks = gathered(together(*blocks), [o[step] for o in crossing], bit_count)
-    own_merge = blocks.pop().reshape(joined_width // 2, merged_width)
-    own_weight = [b.reshape(half_rows, b.shape[-1]) for b in blocks]
+        block = block.reshape(bits + block.shape)
+        merge_block = merge_weight.reshape(bits + merge_weight.shape)
+        for bit in far_bits:
+            block, merge_block = gathered([block, merge_block], [bit, bit], bit_count)
+        blocks = split(block, portion_widths) + [merge_block]
+        for step in range(len(orders[0])):
+            blocks = gathered(together(*blocks), [o[step] for o in crossing], bit_count)
+        own_merge = blocks.pop()
+        own_weight = [b.reshape(half_rows, b.shape[-1]) for b in blocks]
+    own_merge = own_merge.reshape(joined_width // 2, merged_width)
 
     def row_sum(parts):
         total = None
@@ -370,11 +580,17 @@
     def by_tap(product):
         return split(product, [branch] * (product.shape[1] // branch))
 
-    def product(own, other):
-        return by_tap(dot_f32(flat_own, own, 1, 0) + dot_f32(flat_other, other, 1, 0))
-
     other_weight = [exchanged(w, 0) for w in own_weight[:2]]
-    sums = [row_sum(product(a, b)) for a, b in zip(own_weight, other_weight)]
+    sums = [
+        dot_f32(flat_own, a, 1, 0) + dot_f32(flat_other, b, 1, 0)
+        for a, b in zip(own_weight, other_weight)
+    ]
+    upward = is_upward(me, device_step)
+    if paired:
+        sums = halo_sums(width, device_step, sums, me)
+    else:
+        sums = [row_sum(by_tap(x)).reshape(pixels, branch) for x in sums]
+        sums = [jnp.where(upward, *sums), jnp.where(upward, *sums[::-1])]
     merge_to_relative = relative_order(joined_width, device_count, me)
     own_weight[2], own_merge, *sums = together(own_weight[2], own_merge, *sums)
     whole_merge = dot_f32(
@@ -382,8 +598,7 @@
     ).astype(jnp.bfloat16)
     other_weight.append(exchanged(own_weight[2], 0))
     centre = dot_f32(flat_own, own_weight[2], 1, 0) + dot_f32(flat_other, other_weight[2], 1, 0)
-    above = passed_along(sums[0], device_step).reshape(pixels, branch)
-    below = passed_along(sums[1], -device_step).reshape(pixels, branch)
+    above, below = swapped(sums[0], device_step, 0), swapped(sums[1], device_step, 1)
     flat_cotangent = cotangent.reshape(pixels, merged_width)
     if paired:
         merged, grad_dil, centre_gradient, joined, grad_out = head(
@@ -410,7 +625,7 @@
 
     if not paired:
         centre_gradient = jnp.concatenate([kept[:, :branch]] + shifted_gradients(grad_dil), axis=1)
-    halos = [passed_along(grad_dil, -device_step), passed_along(grad_dil, device_step)]
+    halos = [swapped(grad_dil, device_step, 0), swapped(grad_dil, device_step, 1)]
     if paired:
         own_merge, other_merge = merge_gradient(joined, grad_out, me)
     else:
@@ -426,61 +641,92 @@
     own_total[2] = dot_f32(flat_own, centre_gradient, 0, 0)
     *halos, own_total[2], other_total[2] = together(*halos, own_total[2], other_total[2])
     if paired:
-        gradients = [*shifted(width, *halos), centre_gradient]
+        gradients = [*shifted(width, device_step, *halos, me), centre_gradient]
     else:
+        halos = [jnp.where(upward, *halos), jnp.where(upward, *halos[::-1])]
         gradients = [jnp.concatenate(shifted_gradients(h), axis=1) for h in halos]
         gradients = together(*gradients) + [centre_gradient]
     for p in range(2):
         other_total[p] = dot_f32(flat_other, gradients[p], 0, 0).astype(jnp.bfloat16)
         own_total[p] = dot_f32(flat_own, gradients[p], 0, 0)
-    merge_total = own_merge + merge_arrived.astype(jnp.float32)
-    merge_total = merge_total.reshape((2,) * (bit_count - 1) + (joined_rows, merged_width))
-    merge_parts = halves(merge_total, far_bits[0], bit_count) if far_bits else None
-    sending = list(other_total) + ([merge_parts[1]] if far_bits else [])
-    arrived = [
-        exchanged(t, b) for t, b in zip(together(*sending), [0, 0, 0] + far_bits[:1])
-    ]
-    arrived = together(*arrived)
-    if far_bits:
-        merge_total = merge_parts[0] + arrived.pop().astype(jnp.float32)
-    for bit in far_bits[1:]:
-        own, other = halves(merge_total, bit, bit_count)
-        merge_total = own + exchanged(other, bit).astype(jnp.float32)
-    totals = []
-    for own, a, o in zip(own_total, arrived, orders):
-        shape = (2,) * (bit_count - 1) + (own.shape[0] // (device_count // 2), own.shape[1])
-        totals.append(added(own.reshape(shape), a.reshape(shape), o[-1], bit_count))
-    totals.append(halves(merge_total, crossing[3][-1], bit_count))
-    *sent, g0, g1, g2 = together(*[t[1] for t in totals], *gradients)
     if paired:
-        input_grad = input_gradient([g0, g1, g2], own_weight, other_weight, me)
+        sending = together(*other_total)
+        arrived = together(*[exchanged(t, 0) for t in sending])
+        own_blocks = device_count // 2
+        owns = [x.reshape(own_blocks, -1, x.shape[-1]) for x in (*own_total, own_merge)]
+        arrived = [x.reshape(own_blocks, -1, x.shape[-1]) for x in (*arrived, merge_arrived)]
+        left = [list(range(bit_count - 1, 0, -1)) for _ in orders]
+        for step in range(len(orders[0])):
+            bits_now = [o[-1 - step] for o in orders]
+            inners = [1 << (len(x) - 1 - x.index(b)) for x, b in zip(left, bits_now)]
+            owns, sent = fold(owns, arrived, tables, inners)
+            for x, b in zip(left, bits_now):
+                x.remove(b)
+            if step == 0:
+                *sent, g0, g1, g2 = together(*sent, *gradients)
+                input_grad = input_gradient([g0, g1, g2], own_weight, other_weight, me)
+            else:
+                sent = together(*sent)
+            arrived = together(*[exchanged(t, b) for t, b in zip(sent, bits_now)])
+            if step == 0:
+                *arrived, input_grad = together(*arrived, input_grad)
+        keep, sent = last_fold(owns, arrived)
+        branch_kernel_gradient, grad_merge = scaled(
+            keep,
+            exchanged(sent, far_bits[0]),
+            tables,
+            scale,
+            own_channels,
+            joined_rows,
+            merged_width,
+        )
+        branch_kernel_gradient = branch_kernel_gradient.transpose(1, 0, 2)
     else:
+        merge_total = own_merge + merge_arrived.astype(jnp.float32)
+        merge_total = merge_total.reshape((2,) * (bit_count - 1) + (joined_rows, merged_width))
+        merge_parts = halves(merge_total, far_bits[0], bit_count) if far_bits else None
+        sending = list(other_total) + ([merge_parts[1]] if far_bits else [])
+        arrived = [
+            exchanged(t, b) for t, b in zip(together(*sending), [0, 0, 0] + far_bits[:1])
+        ]
+        arrived = together(*arrived)
+        if far_bits:
+            merge_total = merge_parts[0] + arrived.pop().astype(jnp.float32)
+        for bit in far_bits[1:]:
+            own, other = halves(merge_total, bit, bit_count)
+            merge_total = own + exchanged(other, bit).astype(jnp.float32)
+        totals = []
+        for own, a, o in zip(own_total, arrived, orders):
+            shape = (2,) * (bit_count - 1) + (own.shape[0] // (device_count // 2), own.shape[1])
+            totals.append(added(own.reshape(shape), a.reshape(shape), o[-1], bit_count))
+        totals.append(halves(merge_total, crossing[3][-1], bit_count))
+        *sent, g0, g1, g2 = together(*[t[1] for t in totals], *gradients)
         input_total = sum(
             dot_f32(g, jnp.concatenate([a, b], axis=0), 1, 1)
             for g, a, b in zip((g0, g1, g2), own_weight, other_weight)
         ).astype(jnp.bfloat16)
         input_grad = dot_f32(input_total, to_relative, 1, 1).astype(jnp.bfloat16)
-    for step in range(len(orders[0])):
-        arrived = together(*[exchanged(t, o[-1 - step]) for t, o in zip(sent, crossing)])
-        if step == 0:
-            *arrived, input_grad = together(*arrived, input_grad)
-        own = [t[0] for t in totals]
-        if step + 1 < len(orders[0]):
-            totals = [
-                added(t, a, o[-2 - step], bit_count) for t, a, o in zip(own, arrived, crossing)
-            ]
-            sent = together(*[t[1] for t in totals])
-        else:
-            totals = [t + a.astype(jnp.float32) for t, a in zip(own, arrived)]
-    grad_merge = totals[3].reshape(joined_rows, merged_width) * scale
-    total = jnp.concatenate(totals[:3], axis=-1)
-    for bit in far_bits[::-1]:
-        own, other = halves(total, bit, bit_count)
-        total = own + exchanged(other, bit).astype(jnp.float32)
-    weight_gradient = dict(
-        zip([k for p in PORTIONS for k in p], by_tap(total.reshape(own_channels, -1)))
-    )
-    branch_kernel_gradient = jnp.stack([weight_gradient[k] for k in range(taps)], axis=1) * scale
+        for step in range(len(orders[0])):
+            arrived = together(*[exchanged(t, o[-1 - step]) for t, o in zip(sent, crossing)])
+            if step == 0:
+                *arrived, input_grad = together(*arrived, input_grad)
+            own = [t[0] for t in totals]
+            if step + 1 < len(orders[0]):
+                totals = [
+                    added(t, a, o[-2 - step], bit_count) for t, a, o in zip(own, arrived, crossing)
+                ]
+                sent = together(*[t[1] for t in totals])
+            else:
+                totals = [t + a.astype(jnp.float32) for t, a in zip(own, arrived)]
+        grad_merge = totals[3].reshape(joined_rows, merged_width) * scale
+        total = jnp.concatenate(totals[:3], axis=-1)
+        for bit in far_bits[::-1]:
+            own, other = halves(total, bit, bit_count)
+            total = own + exchanged(other, bit).astype(jnp.float32)
+        weight_gradient = dict(
+            zip([k for p in PORTIONS for k in p], by_tap(total.reshape(own_channels, -1)))
+        )
+        branch_kernel_gradient = jnp.stack([weight_gradient[k] for k in range(taps)], axis=1) * scale
 
     return (
         merged.reshape(rows, width, merged_width),

time: 122 us -> 117 us (0.959)
  starting transfers between devices: 50.2 us -> 44.9 us
  other arithmetic: 3.38 us -> 0.26 us
  Pallas kernels: 6.51 us -> 8.92 us
  waiting for transfers between devices: 49.5 us -> 51.2 us
    ppermute x36 -> x28, starting transfers between devices: 38.9 us -> 30.2 us  [exchanged(): lax.ppermute(block, 'row', [(i, i ^ 1 << bit) for i in range(lax.axis_siz...]
    ppermute x36 -> x28, waiting for transfers between devices: 41.1 us -> 48.2 us  [exchanged(): lax.ppermute(block, 'row', [(i, i ^ 1 << bit) for i in range(lax.axis_siz...]
    ppermute x4, waiting for transfers between devices: 8.37 us -> 2.95 us  [swapped(): return lax.ppermute(block, 'row', pairs + [(b, a) for a, b in pairs])]
    ppermute x4, starting transfers between devices: 11.4 us -> 14.8 us  [swapped(): return lax.ppermute(block, 'row', pairs + [(b, a) for a, b in pairs])]
    pallas_call x2 -> x9, Pallas kernels: 0.38 us -> 2.82 us  [the longest x7 2.2 us: local_call(): pl.pallas_call(kernel, out_shape=out_shape, in_specs=[pl.BlockSpec(memory...]
    mul x2 -> x0, other arithmetic: 1.36 us -> none  [the longest x1 0.76 us: on_device(): jnp.stack([weight_gradient[k] for k in range(taps)], axis=1) * scale]
    unnamed x21 -> x12, local copies, waits for them, and re-layouts: 2.38 us -> 3.02 us
  transfers between devices with their start and end apart: 40 -> 32, of which waited for: 18 -> 20; matrix products, arithmetic and copies ran while one was open for 7% -> 5% of each run, Pallas kernels for 4% -> 4%
where the time goes in v4:
time: 117 us
  waiting for transfers between devices  51.2 us (44%)
  starting transfers between devices  44.9 us (38%)
  Pallas kernels  8.92 us (8%)
  matrix products  7.86 us (7%)
  local copies, waits for them, and re-layouts  3.05 us (3%)
    ppermute x28, waiting for transfers between devices, exchanged(): lax.ppermute(block, 'row', [(i, i ^ 1 << bit) for i in range(lax.axis_siz...  48.2 us
    ppermute x28, starting transfers between devices, exchanged(): lax.ppermute(block, 'row', [(i, i ^ 1 << bit) for i in range(lax.axis_siz...  30.2 us
    ppermute x4, starting transfers between devices, swapped(): return lax.ppermute(block, 'row', pairs + [(b, a) for a, b in pairs])  14.8 us
    dot_general x13, matrix products, dot_f32(): lax.dot_general(left, right, (((left_dim,), (right_dim,)), ((), ())), pre...  7.86 us
    pallas_call x1, Pallas kernels, input_gradient(): pl.pallas_call(functools.partial(input_gradient_kernel, len(gradients)),...  3.78 us
    unnamed x12, local copies, waits for them, and re-layouts  3.02 us
    ppermute x4, waiting for transfers between devices, swapped(): return lax.ppermute(block, 'row', pairs + [(b, a) for a, b in pairs])  2.95 us
  transfers between devices with their start and end apart: 32, of which 20 were waited for; matrix products, arithmetic and copies ran while one was open for 5% of the time, Pallas kernels for 4%

profile of v4, /device:TPU:0, one launch (start us, length us, event | category | flops | bytes accessed | tf_op | source)
XLA Modules:
  0.0 117.2 jit_solution(5995391705318331955)
XLA Ops:
  2.3 4.1 %collective-permute-start = (bf16[1,1,1,1,656,128]{5,4,3,2,1,0:T(8,128)(2,1)S(1)}, bf16[1,1,1,1,656,128]{5,4,3,2,1,0:T(8,128)(2,1)S(1)}, u32[]{:S(2)}, u32[]{:S(2)}) collective-permute-start(bf16[1,1,1,1,656,128]{5,4,3,2,1,0:T(8,128)(2,1)S(1)} %bitcast.70), channel_id=1, source_target_pairs={{0,16},{1,17},{2,18},{3,19},{4,20},{5,21},{6,22},{7,23},{8,24},{9,... | collective-permute-start | bytes 503816 | tf_op jit(solution)/shard_map/ppermute | solution.py:23
  8.7 5.5 %collective-permute-done = bf16[1,1,1,1,656,128]{5,4,3,2,1,0:T(8,128)(2,1)S(1)} collective-permute-done((bf16[1,1,1,1,656,128]{5,4,3,2,1,0:T(8,128)(2,1)S(1)}, bf16[1,1,1,1,656,128]{5,4,3,2,1,0:T(8,128)(2,1)S(1)}, u32[]{:S(2)}, u32[]{:S(2)}) %collective-permute-start) | collective-permute-done | bytes 167968 | tf_op jit(solution)/shard_map/ppermute | solution.py:23
  14.3 1.6 %collective-permute-start.3 = (bf16[2,1,1,1,224,128]{5,4,3,2,1,0:T(8,128)(2,1)S(1)}, bf16[2,1,1,1,224,128]{5,4,3,2,1,0:T(8,128)(2,1)S(1)}, u32[]{:S(2)}, u32[]{:S(2)}) collective-permute-start(bf16[2,1,1,1,224,128]{5,4,3,2,1,0:T(8,128)(2,1)S(1)} %pad_maximum_fusion.6), channel_id=1, source_target_pairs={{0,2},{1,3},{2,0},{3,1},{4,6},{5,7},{6,4},{7,5},{8,10},{9,11},{10,... | collective-permute-start | bytes 344072 | tf_op jit(solution)/shard_map/ppermute | solution.py:23
  16.6 1.5 %collective-permute-start.2 = (bf16[2,1,1,1,216,128]{5,4,3,2,1,0:T(8,128)(2,1)S(1)}, bf16[2,1,1,1,216,128]{5,4,3,2,1,0:T(8,128)(2,1)S(1)}, u32[]{:S(2)}, u32[]{:S(2)}) collective-permute-start(bf16[2,1,1,1,216,128]{5,4,3,2,1,0:T(8,128)(2,1)S(1)} %pad_maximum_fusion.8), channel_id=1, source_target_pairs={{0,4},{1,5},{2,6},{3,7},{4,0},{5,1},{6,2},{7,3},{8,12},{9,13},{10,... | collective-permute-start | bytes 331784 | tf_op jit(solution)/shard_map/ppermute | solution.py:23
  18.1 2.6 %collective-permute-done.1 = bf16[2,1,1,1,216,128]{5,4,3,2,1,0:T(8,128)(2,1)S(1)} collective-permute-done((bf16[2,1,1,1,216,128]{5,4,3,2,1,0:T(8,128)(2,1)S(1)}, bf16[2,1,1,1,216,128]{5,4,3,2,1,0:T(8,128)(2,1)S(1)}, u32[]{:S(2)}, u32[]{:S(2)}) %collective-permute-start.1) | collective-permute-done | bytes 110624 | tf_op jit(solution)/shard_map/ppermute | solution.py:23
  24.9 3.9 %collective-permute-done.4 = bf16[2,2,1,1,216,128]{5,4,3,2,1,0:T(8,128)(2,1)S(1)} collective-permute-done((bf16[2,2,1,1,216,128]{5,4,3,2,1,0:T(8,128)(2,1)S(1)}, bf16[2,2,1,1,216,128]{5,4,3,2,1,0:T(8,128)(2,1)S(1)}, u32[]{:S(2)}, u32[]{:S(2)}) %collective-permute-start.4) | collective-permute-done | bytes 221216 | tf_op jit(solution)/shard_map/ppermute | solution.py:23
  28.8 2.2 %collective-permute-done.5 = bf16[2,1,2,1,216,128]{5,4,3,2,1,0:T(8,128)(2,1)S(1)} collective-permute-done((bf16[2,1,2,1,216,128]{5,4,3,2,1,0:T(8,128)(2,1)S(1)}, bf16[2,1,2,1,216,128]{5,4,3,2,1,0:T(8,128)(2,1)S(1)}, u32[]{:S(2)}, u32[]{:S(2)}) %collective-permute-start.5) | collective-permute-done | bytes 221216 | tf_op jit(solution)/shard_map/ppermute | solution.py:23
  32.3 7.5 %collective-permute-done.7 = bf16[2,2,2,1,216,128]{5,4,3,2,1,0:T(8,128)(2,1)S(1)} collective-permute-done((bf16[2,2,2,1,216,128]{5,4,3,2,1,0:T(8,128)(2,1)S(1)}, bf16[2,2,2,1,216,128]{5,4,3,2,1,0:T(8,128)(2,1)S(1)}, u32[]{:S(2)}, u32[]{:S(2)}) %collective-permute-start.7) | collective-permute-done | bytes 442400 | tf_op jit(solution)/shard_map/ppermute | solution.py:23
  41.1 1.8 %collective-permute-done.10.refs_6_ = bf16[1024,384]{1,0:T(8,128)(2,1)S(1)} collective-permute-done((bf16[1024,384]{1,0:T(8,128)(2,1)S(1)}, bf16[1024,384]{1,0:T(8,128)(2,1)S(1)}, u32[]{:S(2)}, u32[]{:S(2)}) %collective-permute-start.10) | collective-permute-done | bytes 786464 | tf_op jit(solution)/shard_map/ppermute | solution.py:23
  46.0 2.6 %collective-permute-start.13 = (f32[384,128]{1,0:T(8,128)S(1)}, f32[384,128]{1,0:T(8,128)S(1)}, u32[]{:S(2)}, u32[]{:S(2)}) collective-permute-start(f32[384,128]{1,0:T(8,128)S(1)} %get-tuple-element.143), channel_id=1, source_target_pairs={{0,9},{1,10},{2,11},{3,12},{4,13},{5,14},{6,15},{7,16},{8,17},{18,... | collective-permute-start | bytes 589832 | tf_op jit(solution)/shard_map/ppermute | solution.py:19
  50.8 2.6 %collective-permute-done.13.above_ref = f32[384,128]{1,0:T(8,128)S(1)} collective-permute-done((f32[384,128]{1,0:T(8,128)S(1)}, f32[384,128]{1,0:T(8,128)S(1)}, u32[]{:S(2)}, u32[]{:S(2)}) %collective-permute-start.13) | collective-permute-done | bytes 196640 | tf_op jit(solution)/shard_map/ppermute | solution.py:19
  55.2 10.8 %collective-permute-start.16 = (bf16[384,128]{1,0:T(8,128)(2,1)S(1)}, bf16[384,128]{1,0:T(8,128)(2,1)S(1)}, u32[]{:S(2)}, u32[]{:S(2)}) collective-permute-start(bf16[384,128]{1,0:T(8,128)(2,1)S(1)} %get-tuple-element.147), channel_id=1, source_target_pairs={{0,9},{1,10},{2,11},{3,12},{4,13},{5,14},{6,15},{7,16},{8,17},{18,... | collective-permute-start | bytes 294920 | tf_op jit(solution)/shard_map/ppermute | solution.py:19
  69.9 2.0 %collective-permute-start.20 = (bf16[1024,512]{1,0:T(8,128)(2,1)S(1)}, bf16[1024,512]{1,0:T(8,128)(2,1)S(1)}, u32[]{:S(2)}, u32[]{:S(2)}) collective-permute-start(bf16[1024,512]{1,0:T(8,128)(2,1)S(1)} %convolution_convert_fusion), channel_id=1, source_target_pairs={{0,1},{1,0},{2,3},{3,2},{4,5},{5,4},{6,7},{7,6},{8,9},{9,8},{10,11... | collective-permute-start | bytes 3145736 | tf_op jit(solution)/shard_map/ppermute | solution.py:23
  77.0 2.6 %collective-permute-start.24 = (bf16[8,224,128]{2,1,0:T(8,128)(2,1)S(1)}, bf16[8,224,128]{2,1,0:T(8,128)(2,1)S(1)}, u32[]{:S(2)}, u32[]{:S(2)}) collective-permute-start(bf16[8,224,128]{2,1,0:T(8,128)(2,1)S(1)} %get-tuple-element.172), channel_id=1, source_target_pairs={{0,4},{1,5},{2,6},{3,7},{4,0},{5,1},{6,2},{7,3},{8,12},{9,13},{10,... | collective-permute-start | bytes 1376264 | tf_op jit(solution)/shard_map/ppermute | solution.py:23
  79.6 2.1 %collective-permute-start.22 = (bf16[8,216,128]{2,1,0:T(8,128)(2,1)S(1)}, bf16[8,216,128]{2,1,0:T(8,128)(2,1)S(1)}, u32[]{:S(2)}, u32[]{:S(2)}) collective-permute-start(bf16[8,216,128]{2,1,0:T(8,128)(2,1)S(1)} %get-tuple-element.170), channel_id=1, source_target_pairs={{0,2},{1,3},{2,0},{3,1},{4,6},{5,7},{6,4},{7,5},{8,10},{9,11},{10,... | collective-permute-start | bytes 1327112 | tf_op jit(solution)/shard_map/ppermute | solution.py:23
  81.7 1.8 %collective-permute-start.23 = (bf16[8,216,128]{2,1,0:T(8,128)(2,1)S(1)}, bf16[8,216,128]{2,1,0:T(8,128)(2,1)S(1)}, u32[]{:S(2)}, u32[]{:S(2)}) collective-permute-start(bf16[8,216,128]{2,1,0:T(8,128)(2,1)S(1)} %get-tuple-element.171), channel_id=1, source_target_pairs={{0,8},{1,9},{2,10},{3,11},{4,12},{5,13},{6,14},{7,15},{8,0},{9,1},... | collective-permute-start | bytes 1327112 | tf_op jit(solution)/shard_map/ppermute | solution.py:23
  83.5 3.8 %input_gradient.1 = bf16[384,2048]{1,0:T(8,128)(2,1)} custom-call(s32[1]{0:T(128)} %bitcast.3.me_ref, bf16[384,384]{1,0:T(8,128)(2,1)S(1)} %get-tuple-element.176.refs_0_, bf16[384,384]{1,0:T(8,128)(2,1)S(1)} %get-tuple-element.177.refs_1_, bf16[384,512]{1,0:T(8,128)(2,1)S(1)} %get-tuple-element.178.refs_2_, bf16[1024,384]{1,0:T(8,128)(2,1)S(1)} %bitcast.59, ...), custom_call_target="tpu_custom_call" | custom-call | flops 2013265920 | bytes 7798784 | tf_op jit(solution)/shard_map/input_gradient/pallas_call | solution.py:153
  87.2 4.6 %collective-permute-done.22.refs_3_ = bf16[8,216,128]{2,1,0:T(8,128)(2,1)S(1)} collective-permute-done((bf16[8,216,128]{2,1,0:T(8,128)(2,1)S(1)}, bf16[8,216,128]{2,1,0:T(8,128)(2,1)S(1)}, u32[]{:S(2)}, u32[]{:S(2)}) %collective-permute-start.22) | collective-permute-done | bytes 442400 | tf_op jit(solution)/shard_map/ppermute | solution.py:23
  91.9 1.7 %collective-permute-done.23.refs_4_ = bf16[8,216,128]{2,1,0:T(8,128)(2,1)S(1)} collective-permute-done((bf16[8,216,128]{2,1,0:T(8,128)(2,1)S(1)}, bf16[8,216,128]{2,1,0:T(8,128)(2,1)S(1)}, u32[]{:S(2)}, u32[]{:S(2)}) %collective-permute-start.23) | collective-permute-done | bytes 442400 | tf_op jit(solution)/shard_map/ppermute | solution.py:23
  93.9 1.8 %collective-permute-start.27 = (bf16[4,224,128]{2,1,0:T(8,128)(2,1)S(1)}, bf16[4,224,128]{2,1,0:T(8,128)(2,1)S(1)}, u32[]{:S(2)}, u32[]{:S(2)}) collective-permute-start(bf16[4,224,128]{2,1,0:T(8,128)(2,1)S(1)} %get-tuple-element.194), channel_id=1, source_target_pairs={{0,8},{1,9},{2,10},{3,11},{4,12},{5,13},{6,14},{7,15},{8,0},{9,1},... | collective-permute-start | bytes 688136 | tf_op jit(solution)/shard_map/ppermute | solution.py:23
  96.6 5.1 %collective-permute-done.25.refs_3_ = bf16[4,216,128]{2,1,0:T(8,128)(2,1)S(1)} collective-permute-done((bf16[4,216,128]{2,1,0:T(8,128)(2,1)S(1)}, bf16[4,216,128]{2,1,0:T(8,128)(2,1)S(1)}, u32[]{:S(2)}, u32[]{:S(2)}) %collective-permute-start.25) | collective-permute-done | bytes 221216 | tf_op jit(solution)/shard_map/ppermute | solution.py:23
  104.6 3.3 %collective-permute-done.28.refs_3_ = bf16[2,216,128]{2,1,0:T(8,128)(2,1)S(1)} collective-permute-done((bf16[2,216,128]{2,1,0:T(8,128)(2,1)S(1)}, bf16[2,216,128]{2,1,0:T(8,128)(2,1)S(1)}, u32[]{:S(2)}, u32[]{:S(2)}) %collective-permute-start.28) | collective-permute-done | bytes 110624 | tf_op jit(solution)/shard_map/ppermute | solution.py:23
  108.3 2.5 %collective-permute-start.31 = (bf16[656,128]{1,0:T(8,128)(2,1)S(1)}, bf16[656,128]{1,0:T(8,128)(2,1)S(1)}, u32[]{:S(2)}, u32[]{:S(2)}) collective-permute-start(bf16[656,128]{1,0:T(8,128)(2,1)S(1)} %get-tuple-element.211), channel_id=1, source_target_pairs={{0,16},{1,17},{2,18},{3,19},{4,20},{5,21},{6,22},{7,23},{8,24},{9,... | collective-permute-start | bytes 503816 | tf_op jit(solution)/shard_map/ppermute | solution.py:23
  110.8 5.7 %collective-permute-done.31.arrived_ref = bf16[656,128]{1,0:T(8,128)(2,1)S(1)} collective-permute-done((bf16[656,128]{1,0:T(8,128)(2,1)S(1)}, bf16[656,128]{1,0:T(8,128)(2,1)S(1)}, u32[]{:S(2)}, u32[]{:S(2)}) %collective-permute-start.31) | collective-permute-done | bytes 167968 | tf_op jit(solution)/shard_map/ppermute | solution.py:23
  (93 shorter events, 32.5 us)
Async XLA Ops:
  2.3 12.0 %collective-permute-start = (bf16[1,1,1,1,656,128]{5,4,3,2,1,0:T(8,128)(2,1)S(1)}, bf16[1,1,1,1,656,128]{5,4,3,2,1,0:T(8,128)(2,1)S(1)}, u32[]{:S(2)}, u32[]{:S(2)}) collective-permute-start(bf16[1,1,1,1,656,128]{5,4,3,2,1,0:T(8,128)(2,1)S(1)} %bitcast.70), channel_id=1, source_target_pairs={{0,16},{1,17},{2,18},{3,19},{4,20},{5,21},{6,22},{7,23},{8,24},{9,... | collective-permute-start | bytes 503816 | tf_op jit(solution)/shard_map/ppermute | solution.py:23
  14.3 7.0 %collective-permute-start.3 = (bf16[2,1,1,1,224,128]{5,4,3,2,1,0:T(8,128)(2,1)S(1)}, bf16[2,1,1,1,224,128]{5,4,3,2,1,0:T(8,128)(2,1)S(1)}, u32[]{:S(2)}, u32[]{:S(2)}) collective-permute-start(bf16[2,1,1,1,224,128]{5,4,3,2,1,0:T(8,128)(2,1)S(1)} %pad_maximum_fusion.6), channel_id=1, source_target_pairs={{0,2},{1,3},{2,0},{3,1},{4,6},{5,7},{6,4},{7,5},{8,10},{9,11},{10,... | collective-permute-start | bytes 344072 | tf_op jit(solution)/shard_map/ppermute | solution.py:23
  16.0 4.7 %collective-permute-start.1 = (bf16[2,1,1,1,216,128]{5,4,3,2,1,0:T(8,128)(2,1)S(1)}, bf16[2,1,1,1,216,128]{5,4,3,2,1,0:T(8,128)(2,1)S(1)}, u32[]{:S(2)}, u32[]{:S(2)}) collective-permute-start(bf16[2,1,1,1,216,128]{5,4,3,2,1,0:T(8,128)(2,1)S(1)} %pad_maximum_fusion.7), channel_id=1, source_target_pairs={{0,8},{1,9},{2,10},{3,11},{4,12},{5,13},{6,14},{7,15},{8,0},{9,1},... | collective-permute-start | bytes 331784 | tf_op jit(solution)/shard_map/ppermute | solution.py:23
  16.6 4.7 %collective-permute-start.2 = (bf16[2,1,1,1,216,128]{5,4,3,2,1,0:T(8,128)(2,1)S(1)}, bf16[2,1,1,1,216,128]{5,4,3,2,1,0:T(8,128)(2,1)S(1)}, u32[]{:S(2)}, u32[]{:S(2)}) collective-permute-start(bf16[2,1,1,1,216,128]{5,4,3,2,1,0:T(8,128)(2,1)S(1)} %pad_maximum_fusion.8), channel_id=1, source_target_pairs={{0,4},{1,5},{2,6},{3,7},{4,0},{5,1},{6,2},{7,3},{8,12},{9,13},{10,... | collective-permute-start | bytes 331784 | tf_op jit(solution)/shard_map/ppermute | solution.py:23
  21.5 9.6 %collective-permute-start.6 = (bf16[2,1,1,2,224,128]{5,4,3,2,1,0:T(8,128)(2,1)S(1)}, bf16[2,1,1,2,224,128]{5,4,3,2,1,0:T(8,128)(2,1)S(1)}, u32[]{:S(2)}, u32[]{:S(2)}) collective-permute-start(bf16[2,1,1,2,224,128]{5,4,3,2,1,0:T(8,128)(2,1)S(1)} %pad_maximum_fusion.3), channel_id=1, source_target_pairs={{0,8},{1,9},{2,10},{3,11},{4,12},{5,13},{6,14},{7,15},{8,0},{9,1},... | collective-permute-start | bytes 688136 | tf_op jit(solution)/shard_map/ppermute | solution.py:23
  22.9 5.9 %collective-permute-start.4 = (bf16[2,2,1,1,216,128]{5,4,3,2,1,0:T(8,128)(2,1)S(1)}, bf16[2,2,1,1,216,128]{5,4,3,2,1,0:T(8,128)(2,1)S(1)}, u32[]{:S(2)}, u32[]{:S(2)}) collective-permute-start(bf16[2,2,1,1,216,128]{5,4,3,2,1,0:T(8,128)(2,1)S(1)} %pad_maximum_fusion.4), channel_id=1, source_target_pairs={{0,4},{1,5},{2,6},{3,7},{4,0},{5,1},{6,2},{7,3},{8,12},{9,13},{10,... | collective-permute-start | bytes 663560 | tf_op jit(solution)/shard_map/ppermute | solution.py:23
  24.4 6.6 %collective-permute-start.5 = (bf16[2,1,2,1,216,128]{5,4,3,2,1,0:T(8,128)(2,1)S(1)}, bf16[2,1,2,1,216,128]{5,4,3,2,1,0:T(8,128)(2,1)S(1)}, u32[]{:S(2)}, u32[]{:S(2)}) collective-permute-start(bf16[2,1,2,1,216,128]{5,4,3,2,1,0:T(8,128)(2,1)S(1)} %pad_maximum_fusion.5), channel_id=1, source_target_pairs={{0,2},{1,3},{2,0},{3,1},{4,6},{5,7},{6,4},{7,5},{8,10},{9,11},{10,... | collective-permute-start | bytes 663560 | tf_op jit(solution)/shard_map/ppermute | solution.py:23
  31.2 8.8 %collective-permute-start.9 = (bf16[2,2,1,2,224,128]{5,4,3,2,1,0:T(8,128)(2,1)S(1)}, bf16[2,2,1,2,224,128]{5,4,3,2,1,0:T(8,128)(2,1)S(1)}, u32[]{:S(2)}, u32[]{:S(2)}) collective-permute-start(bf16[2,2,1,2,224,128]{5,4,3,2,1,0:T(8,128)(2,1)S(1)} %pad_maximum_fusion), channel_id=1, source_target_pairs={{0,4},{1,5},{2,6},{3,7},{4,0},{5,1},{6,2},{7,3},{8,12},{9,13},{10,... | collective-permute-start | bytes 1376264 | tf_op jit(solution)/shard_map/ppermute | solution.py:23
  31.3 8.5 %collective-permute-start.7 = (bf16[2,2,2,1,216,128]{5,4,3,2,1,0:T(8,128)(2,1)S(1)}, bf16[2,2,2,1,216,128]{5,4,3,2,1,0:T(8,128)(2,1)S(1)}, u32[]{:S(2)}, u32[]{:S(2)}) collective-permute-start(bf16[2,2,2,1,216,128]{5,4,3,2,1,0:T(8,128)(2,1)S(1)} %pad_maximum_fusion.1), channel_id=1, source_target_pairs={{0,2},{1,3},{2,0},{3,1},{4,6},{5,7},{6,4},{7,5},{8,10},{9,11},{10,... | collective-permute-start | bytes 1327112 | tf_op jit(solution)/shard_map/ppermute | solution.py:23
  31.7 8.3 %collective-permute-start.8 = (bf16[2,1,2,2,216,128]{5,4,3,2,1,0:T(8,128)(2,1)S(1)}, bf16[2,1,2,2,216,128]{5,4,3,2,1,0:T(8,128)(2,1)S(1)}, u32[]{:S(2)}, u32[]{:S(2)}) collective-permute-start(bf16[2,1,2,2,216,128]{5,4,3,2,1,0:T(8,128)(2,1)S(1)} %pad_maximum_fusion.2), channel_id=1, source_target_pairs={{0,8},{1,9},{2,10},{3,11},{4,12},{5,13},{6,14},{7,15},{8,0},{9,1},... | collective-permute-start | bytes 1327112 | tf_op jit(solution)/shard_map/ppermute | solution.py:23
  46.0 7.4 %collective-permute-start.13 = (f32[384,128]{1,0:T(8,128)S(1)}, f32[384,128]{1,0:T(8,128)S(1)}, u32[]{:S(2)}, u32[]{:S(2)}) collective-permute-start(f32[384,128]{1,0:T(8,128)S(1)} %get-tuple-element.143), channel_id=1, source_target_pairs={{0,9},{1,10},{2,11},{3,12},{4,13},{5,14},{6,15},{7,16},{8,17},{18,... | collective-permute-start | bytes 589832 | tf_op jit(solution)/shard_map/ppermute | solution.py:19
  54.5 13.3 %collective-permute-start.17 = (bf16[384,128]{1,0:T(8,128)(2,1)S(1)}, bf16[384,128]{1,0:T(8,128)(2,1)S(1)}, u32[]{:S(2)}, u32[]{:S(2)}) collective-permute-start(bf16[384,128]{1,0:T(8,128)(2,1)S(1)} %get-tuple-element.147), channel_id=1, source_target_pairs={{9,18},{10,19},{11,20},{12,21},{13,22},{14,23},{15,24},{16,25},{17... | collective-permute-start | bytes 294920 | tf_op jit(solution)/shard_map/ppermute | solution.py:19
  55.2 12.9 %collective-permute-start.16 = (bf16[384,128]{1,0:T(8,128)(2,1)S(1)}, bf16[384,128]{1,0:T(8,128)(2,1)S(1)}, u32[]{:S(2)}, u32[]{:S(2)}) collective-permute-start(bf16[384,128]{1,0:T(8,128)(2,1)S(1)} %get-tuple-element.147), channel_id=1, source_target_pairs={{0,9},{1,10},{2,11},{3,12},{4,13},{5,14},{6,15},{7,16},{8,17},{18,... | collective-permute-start | bytes 294920 | tf_op jit(solution)/shard_map/ppermute | solution.py:19
  69.9 6.6 %collective-permute-start.20 = (bf16[1024,512]{1,0:T(8,128)(2,1)S(1)}, bf16[1024,512]{1,0:T(8,128)(2,1)S(1)}, u32[]{:S(2)}, u32[]{:S(2)}) collective-permute-start(bf16[1024,512]{1,0:T(8,128)(2,1)S(1)} %convolution_convert_fusion), channel_id=1, source_target_pairs={{0,1},{1,0},{2,3},{3,2},{4,5},{5,4},{6,7},{7,6},{8,9},{9,8},{10,11... | collective-permute-start | bytes 3145736 | tf_op jit(solution)/shard_map/ppermute | solution.py:23
  77.0 16.6 %collective-permute-start.24 = (bf16[8,224,128]{2,1,0:T(8,128)(2,1)S(1)}, bf16[8,224,128]{2,1,0:T(8,128)(2,1)S(1)}, u32[]{:S(2)}, u32[]{:S(2)}) collective-permute-start(bf16[8,224,128]{2,1,0:T(8,128)(2,1)S(1)} %get-tuple-element.172), channel_id=1, source_target_pairs={{0,4},{1,5},{2,6},{3,7},{4,0},{5,1},{6,2},{7,3},{8,12},{9,13},{10,... | collective-permute-start | bytes 1376264 | tf_op jit(solution)/shard_map/ppermute | solution.py:23
  79.6 12.3 %collective-permute-start.22 = (bf16[8,216,128]{2,1,0:T(8,128)(2,1)S(1)}, bf16[8,216,128]{2,1,0:T(8,128)(2,1)S(1)}, u32[]{:S(2)}, u32[]{:S(2)}) collective-permute-start(bf16[8,216,128]{2,1,0:T(8,128)(2,1)S(1)} %get-tuple-element.170), channel_id=1, source_target_pairs={{0,2},{1,3},{2,0},{3,1},{4,6},{5,7},{6,4},{7,5},{8,10},{9,11},{10,... | collective-permute-start | bytes 1327112 | tf_op jit(solution)/shard_map/ppermute | solution.py:23
  81.7 11.9 %collective-permute-start.23 = (bf16[8,216,128]{2,1,0:T(8,128)(2,1)S(1)}, bf16[8,216,128]{2,1,0:T(8,128)(2,1)S(1)}, u32[]{:S(2)}, u32[]{:S(2)}) collective-permute-start(bf16[8,216,128]{2,1,0:T(8,128)(2,1)S(1)} %get-tuple-element.171), channel_id=1, source_target_pairs={{0,8},{1,9},{2,10},{3,11},{4,12},{5,13},{6,14},{7,15},{8,0},{9,1},... | collective-permute-start | bytes 1327112 | tf_op jit(solution)/shard_map/ppermute | solution.py:23
  93.9 8.2 %collective-permute-start.27 = (bf16[4,224,128]{2,1,0:T(8,128)(2,1)S(1)}, bf16[4,224,128]{2,1,0:T(8,128)(2,1)S(1)}, u32[]{:S(2)}, u32[]{:S(2)}) collective-permute-start(bf16[4,224,128]{2,1,0:T(8,128)(2,1)S(1)} %get-tuple-element.194), channel_id=1, source_target_pairs={{0,8},{1,9},{2,10},{3,11},{4,12},{5,13},{6,14},{7,15},{8,0},{9,1},... | collective-permute-start | bytes 688136 | tf_op jit(solution)/shard_map/ppermute | solution.py:23
  95.7 6.0 %collective-permute-start.25 = (bf16[4,216,128]{2,1,0:T(8,128)(2,1)S(1)}, bf16[4,216,128]{2,1,0:T(8,128)(2,1)S(1)}, u32[]{:S(2)}, u32[]{:S(2)}) collective-permute-start(bf16[4,216,128]{2,1,0:T(8,128)(2,1)S(1)} %get-tuple-element.192), channel_id=1, source_target_pairs={{0,4},{1,5},{2,6},{3,7},{4,0},{5,1},{6,2},{7,3},{8,12},{9,13},{10,... | collective-permute-start | bytes 663560 | tf_op jit(solution)/shard_map/ppermute | solution.py:23
  96.0 6.0 %collective-permute-start.26 = (bf16[4,216,128]{2,1,0:T(8,128)(2,1)S(1)}, bf16[4,216,128]{2,1,0:T(8,128)(2,1)S(1)}, u32[]{:S(2)}, u32[]{:S(2)}) collective-permute-start(bf16[4,216,128]{2,1,0:T(8,128)(2,1)S(1)} %get-tuple-element.193), channel_id=1, source_target_pairs={{0,2},{1,3},{2,0},{3,1},{4,6},{5,7},{6,4},{7,5},{8,10},{9,11},{10,... | collective-permute-start | bytes 663560 | tf_op jit(solution)/shard_map/ppermute | solution.py:23
  102.2 6.0 %collective-permute-start.30 = (bf16[2,224,128]{2,1,0:T(8,128)(2,1)S(1)}, bf16[2,224,128]{2,1,0:T(8,128)(2,1)S(1)}, u32[]{:S(2)}, u32[]{:S(2)}) collective-permute-start(bf16[2,224,128]{2,1,0:T(8,128)(2,1)S(1)} %get-tuple-element.206), channel_id=1, source_target_pairs={{0,2},{1,3},{2,0},{3,1},{4,6},{5,7},{6,4},{7,5},{8,10},{9,11},{10,... | collective-permute-start | bytes 344072 | tf_op jit(solution)/shard_map/ppermute | solution.py:23
  103.1 4.7 %collective-permute-start.28 = (bf16[2,216,128]{2,1,0:T(8,128)(2,1)S(1)}, bf16[2,216,128]{2,1,0:T(8,128)(2,1)S(1)}, u32[]{:S(2)}, u32[]{:S(2)}) collective-permute-start(bf16[2,216,128]{2,1,0:T(8,128)(2,1)S(1)} %get-tuple-element.204), channel_id=1, source_target_pairs={{0,8},{1,9},{2,10},{3,11},{4,12},{5,13},{6,14},{7,15},{8,0},{9,1},... | collective-permute-start | bytes 331784 | tf_op jit(solution)/shard_map/ppermute | solution.py:23
  103.5 4.7 %collective-permute-start.29 = (bf16[2,216,128]{2,1,0:T(8,128)(2,1)S(1)}, bf16[2,216,128]{2,1,0:T(8,128)(2,1)S(1)}, u32[]{:S(2)}, u32[]{:S(2)}) collective-permute-start(bf16[2,216,128]{2,1,0:T(8,128)(2,1)S(1)} %get-tuple-element.205), channel_id=1, source_target_pairs={{0,4},{1,5},{2,6},{3,7},{4,0},{5,1},{6,2},{7,3},{8,12},{9,13},{10,... | collective-permute-start | bytes 331784 | tf_op jit(solution)/shard_map/ppermute | solution.py:23
  108.3 8.1 %collective-permute-start.31 = (bf16[656,128]{1,0:T(8,128)(2,1)S(1)}, bf16[656,128]{1,0:T(8,128)(2,1)S(1)}, u32[]{:S(2)}, u32[]{:S(2)}) collective-permute-start(bf16[656,128]{1,0:T(8,128)(2,1)S(1)} %get-tuple-element.211), channel_id=1, source_target_pairs={{0,16},{1,17},{2,18},{3,19},{4,20},{5,21},{6,22},{7,23},{8,24},{9,... | collective-permute-start | bytes 503816 | tf_op jit(solution)/shard_map/ppermute | solution.py:23
  (14 other events, 43.2 us)

commit v5 on v4

--- a/solution.py
+++ b/solution.py
@@ -249,9 +249,9 @@
     return halo_call(functools.partial(halo_kernel, width, step), "halo_sums", out, me, *products)
 
 
-def shift_kernel(width, step, me_ref, first_ref, second_ref, first_out_ref, second_out_ref):
+def shift_kernel(width, step, flip, me_ref, first_ref, second_ref, first_out_ref, second_out_ref):
     branch = first_ref.shape[1]
-    upward = is_upward(me_ref[0], step)
+    upward = is_upward(me_ref[0] ^ flip, step)
     first, second = first_ref[...].astype(jnp.float32), second_ref[...].astype(jnp.float32)
     pairs = ((first, second, first_out_ref), (second, first, second_out_ref))
     for here, there, out_ref in pairs:
@@ -261,10 +261,11 @@
             out_ref[:, j * branch : (j + 1) * branch] = moved.astype(jnp.bfloat16)
 
 
-def shifted(width, step, first, second, me):
+def shifted(width, step, first, second, me, flip=0):
     pixels, branch = first.shape
     out = jax.ShapeDtypeStruct((pixels, 3 * branch), jnp.bfloat16)
-    return halo_call(functools.partial(shift_kernel, width, step), "shift", out, me, first, second)
+    kernel = functools.partial(shift_kernel, width, step, flip)
+    return halo_call(kernel, "shift", out, me, first, second)
 
 
 def halo_call(kernel, name, out, me, first, second):
@@ -316,7 +317,7 @@
 
 
 def layout(rows, merge_rows, merge_width):
-    shares = (0, 3 * rows // 8, 6 * rows // 8, rows)
+    shares = (0, rows // 4, rows // 2, rows)
     tables = []
     for p, portion in enumerate(PORTIONS):
         table = [(k, 0, n * rows, rows) for n, k in enumerate(k for k in portion if k > 0)]
@@ -352,22 +353,34 @@
     )(*operands)
 
 
-def pack_kernel(tables, weight_ref, merge_ref, out_ref):
-    base = 0
+def pack_kernel(tables, weight_ref, merge_ref, out_ref, sems):
+    copies, base = [], 0
     for table in tables:
         for k, there, here, count in table:
-            at = slice(base + here, base + here + count)
             if k is None:
-                out_ref[at, :] = merge_ref[:, there : there + LANES]
+                source = merge_ref.at[:, pl.ds(there, LANES)]
             else:
-                out_ref[at, :] = weight_ref[k, there : there + count, :]
+                source = weight_ref.at[k, pl.ds(there, count), :]
+            target = out_ref.at[pl.ds(base + here, count), :]
+            copies.append(pltpu.make_async_copy(source, target, sems.at[len(copies)]))
         base += stack_rows(table)
+    for copy in copies:
+        copy.start()
+    for copy in copies:
+        copy.wait()
 
 
 def pack(weight, merge_weight, tables):
-    out = [jax.ShapeDtypeStruct((sum(map(stack_rows, tables)), LANES), weight.dtype)]
-    kernel = functools.partial(pack_kernel, tables)
-    return local_call(kernel, "pack", out, (weight, merge_weight), 4 * weight.size, 4)[0]
+    return pl.pallas_call(
+        functools.partial(pack_kernel, tables),
+        out_shape=jax.ShapeDtypeStruct((sum(map(stack_rows, tables)), LANES), weight.dtype),
+        in_specs=[pl.BlockSpec(memory_space=pltpu.HBM)] * 2,
+        out_specs=pl.BlockSpec(memory_space=pltpu.VMEM),
+        scratch_shapes=[pltpu.SemaphoreType.DMA((sum(map(len, tables)),))],
+        cost_estimate=pl.CostEstimate(flops=0, bytes_accessed=4 * weight.size, transcendentals=0),
+        compiler_params=pltpu.CompilerParams(vmem_limit_bytes=4 << 20),
+        name="pack",
+    )(*(pltpu.with_memory_space_constraint(x, pltpu.HBM) for x in (weight, merge_weight)))
 
 
 def block_pair(target, inner):
@@ -402,7 +415,7 @@
 
 
 def first_fold_kernel(tables, inners, *refs):
-    owns, arriveds, keeps, sends = refs[:4], refs[4:8], refs[8:11], refs[11:]
+    owns, arrived, keeps, sends = refs[:4], refs[4], refs[5:8], refs[8:]
 
     def step(target, carry):
         for p, table in enumerate(tables):
@@ -413,7 +426,9 @@
                     else:
                         q, lanes = lanes_of(k)
                         at = (block, slice(there, there + count), lanes)
-                    value = owns[q][at] + arriveds[q][at].astype(jnp.float32)
+                    value = owns[q][at]
+                    if k is None:
+                        value = value + arrived[at]
                     out_ref = (keeps, sends)[half][p]
                     out_ref[target, here : here + count, :] = value.astype(out_ref.dtype)
         return carry
@@ -581,10 +596,9 @@
         return split(product, [branch] * (product.shape[1] // branch))
 
     other_weight = [exchanged(w, 0) for w in own_weight[:2]]
-    sums = [
-        dot_f32(flat_own, a, 1, 0) + dot_f32(flat_other, b, 1, 0)
-        for a, b in zip(own_weight, other_weight)
-    ]
+    sums = [dot_f32(flat_own, w, 1, 0) for w in own_weight[:2]]
+    other_weight[0], *sums = together(other_weight[0], *sums)
+    sums = [x + dot_f32(flat_other, w, 1, 0) for x, w in zip(sums, other_weight)]
     upward = is_upward(me, device_step)
     if paired:
         sums = halo_sums(width, device_step, sums, me)
@@ -637,24 +651,32 @@
 
     centre_gradient, own_merge = together(centre_gradient, own_merge)
     own_total, other_total = [None] * 3, [None] * 3
-    other_total[2] = dot_f32(flat_other, centre_gradient, 0, 0).astype(jnp.bfloat16)
     own_total[2] = dot_f32(flat_own, centre_gradient, 0, 0)
-    *halos, own_total[2], other_total[2] = together(*halos, own_total[2], other_total[2])
     if paired:
+        flat_partner = exchanged(flat_other, 0)
+        partner_gradient = exchanged(centre_gradient, 0)
+        own_total[2] = own_total[2] + dot_f32(flat_partner, partner_gradient, 0, 0)
+        *halos, own_total[2] = together(*halos, own_total[2])
+        partner_halos = [exchanged(h, 0) for h in halos]
         gradients = [*shifted(width, device_step, *halos, me), centre_gradient]
+        own_total[:2] = [dot_f32(flat_own, g, 0, 0) for g in gradients[:2]]
+        *partner_halos, own_total[0], own_total[1] = together(*partner_halos, *own_total[:2])
+        partner_gradients = shifted(width, device_step, *partner_halos, me, 1)
+        for p in range(2):
+            own_total[p] = own_total[p] + dot_f32(flat_partner, partner_gradients[p], 0, 0)
     else:
+        other_total[2] = dot_f32(flat_other, centre_gradient, 0, 0).astype(jnp.bfloat16)
+        *halos, own_total[2], other_total[2] = together(*halos, own_total[2], other_total[2])
         halos = [jnp.where(upward, *halos), jnp.where(upward, *halos[::-1])]
         gradients = [jnp.concatenate(shifted_gradients(h), axis=1) for h in halos]
         gradients = together(*gradients) + [centre_gradient]
-    for p in range(2):
-        other_total[p] = dot_f32(flat_other, gradients[p], 0, 0).astype(jnp.bfloat16)
-        own_total[p] = dot_f32(flat_own, gradients[p], 0, 0)
+        for p in range(2):
+            other_total[p] = dot_f32(flat_other, gradients[p], 0, 0).astype(jnp.bfloat16)
+            own_total[p] = dot_f32(flat_own, gradients[p], 0, 0)
     if paired:
-        sending = together(*other_total)
-        arrived = together(*[exchanged(t, 0) for t in sending])
         own_blocks = device_count // 2
         owns = [x.reshape(own_blocks, -1, x.shape[-1]) for x in (*own_total, own_merge)]
-        arrived = [x.reshape(own_blocks, -1, x.shape[-1]) for x in (*arrived, merge_arrived)]
+        arrived = [merge_arrived.reshape(owns[3].shape)]
         left = [list(range(bit_count - 1, 0, -1)) for _ in orders]
         for step in range(len(orders[0])):
             bits_now = [o[-1 - step] for o in orders]

time: 117 us -> 116 us (level)
  waiting for transfers between devices: 51.2 us -> 46.3 us
  starting transfers between devices: 44.9 us -> 48.2 us
  local copies, waits for them, and re-layouts: 3.05 us -> 1.45 us
  Pallas kernels: 8.92 us -> 10.1 us
    ppermute x28 -> x29, waiting for transfers between devices: 48.2 us -> 42.9 us  [exchanged(): lax.ppermute(block, 'row', [(i, i ^ 1 << bit) for i in range(lax.axis_siz...]
    ppermute x28 -> x29, starting transfers between devices: 30.2 us -> 32.9 us  [exchanged(): lax.ppermute(block, 'row', [(i, i ^ 1 << bit) for i in range(lax.axis_siz...]
    unnamed x12 -> x8, local copies, waits for them, and re-layouts: 3.02 us -> 1.43 us
  transfers between devices with their start and end apart: 32 -> 33, of which waited for: 20 -> 19; matrix products, arithmetic and copies ran while one was open for 5% -> 7% of each run, Pallas kernels for 4% -> 6%
where the time goes in v5:
time: 116 us
  starting transfers between devices  48.2 us (42%)
  waiting for transfers between devices  46.3 us (40%)
  Pallas kernels  10.1 us (9%)
  matrix products  7.84 us (7%)
  local copies, waits for them, and re-layouts  1.45 us (1%)
    ppermute x29, waiting for transfers between devices, exchanged(): lax.ppermute(block, 'row', [(i, i ^ 1 << bit) for i in range(lax.axis_siz...  42.9 us
    ppermute x29, starting transfers between devices, exchanged(): lax.ppermute(block, 'row', [(i, i ^ 1 << bit) for i in range(lax.axis_siz...  32.9 us
    ppermute x4, starting transfers between devices, swapped(): return lax.ppermute(block, 'row', pairs + [(b, a) for a, b in pairs])  15.3 us
    dot_general x13, matrix products, dot_f32(): lax.dot_general(left, right, (((left_dim,), (right_dim,)), ((), ())), pre...  7.84 us
    pallas_call x1, Pallas kernels, input_gradient(): pl.pallas_call(functools.partial(input_gradient_kernel, len(gradients)),...  3.78 us
    ppermute x4, waiting for transfers between devices, swapped(): return lax.ppermute(block, 'row', pairs + [(b, a) for a, b in pairs])  3.37 us
  transfers between devices with their start and end apart: 33, of which 19 were waited for; matrix products, arithmetic and copies ran while one was open for 7% of the time, Pallas kernels for 6%

profile of v5, /device:TPU:0, one launch (start us, length us, event | category | flops | bytes accessed | tf_op | source)
XLA Modules:
  0.0 115.7 jit_solution(13844656159625740815)
XLA Ops:
  1.6 4.1 %collective-permute-start = (bf16[1,1,1,1,656,128]{5,4,3,2,1,0:T(8,128)(2,1)S(1)}, bf16[1,1,1,1,656,128]{5,4,3,2,1,0:T(8,128)(2,1)S(1)}, u32[]{:S(2)}, u32[]{:S(2)}) collective-permute-start(bf16[1,1,1,1,656,128]{5,4,3,2,1,0:T(8,128)(2,1)S(1)} %bitcast.64), channel_id=1, source_target_pairs={{0,16},{1,17},{2,18},{3,19},{4,20},{5,21},{6,22},{7,23},{8,24},{9,... | collective-permute-start | bytes 503816 | tf_op jit(solution)/shard_map/ppermute | solution.py:23
  8.1 5.5 %collective-permute-done = bf16[1,1,1,1,656,128]{5,4,3,2,1,0:T(8,128)(2,1)S(1)} collective-permute-done((bf16[1,1,1,1,656,128]{5,4,3,2,1,0:T(8,128)(2,1)S(1)}, bf16[1,1,1,1,656,128]{5,4,3,2,1,0:T(8,128)(2,1)S(1)}, u32[]{:S(2)}, u32[]{:S(2)}) %collective-permute-start) | collective-permute-done | bytes 167968 | tf_op jit(solution)/shard_map/ppermute | solution.py:23
  13.7 1.6 %collective-permute-start.3 = (bf16[2,1,1,1,240,128]{5,4,3,2,1,0:T(8,128)(2,1)S(1)}, bf16[2,1,1,1,240,128]{5,4,3,2,1,0:T(8,128)(2,1)S(1)}, u32[]{:S(2)}, u32[]{:S(2)}) collective-permute-start(bf16[2,1,1,1,240,128]{5,4,3,2,1,0:T(8,128)(2,1)S(1)} %pad_maximum_fusion.6), channel_id=1, source_target_pairs={{0,2},{1,3},{2,0},{3,1},{4,6},{5,7},{6,4},{7,5},{8,10},{9,11},{10,... | collective-permute-start | bytes 368648 | tf_op jit(solution)/shard_map/ppermute | solution.py:23
  16.0 1.5 %collective-permute-start.2 = (bf16[2,1,1,1,208,128]{5,4,3,2,1,0:T(8,128)(2,1)S(1)}, bf16[2,1,1,1,208,128]{5,4,3,2,1,0:T(8,128)(2,1)S(1)}, u32[]{:S(2)}, u32[]{:S(2)}) collective-permute-start(bf16[2,1,1,1,208,128]{5,4,3,2,1,0:T(8,128)(2,1)S(1)} %pad_maximum_fusion.8), channel_id=1, source_target_pairs={{0,4},{1,5},{2,6},{3,7},{4,0},{5,1},{6,2},{7,3},{8,12},{9,13},{10,... | collective-permute-start | bytes 319496 | tf_op jit(solution)/shard_map/ppermute | solution.py:23
  17.5 2.5 %collective-permute-done.1 = bf16[2,1,1,1,208,128]{5,4,3,2,1,0:T(8,128)(2,1)S(1)} collective-permute-done((bf16[2,1,1,1,208,128]{5,4,3,2,1,0:T(8,128)(2,1)S(1)}, bf16[2,1,1,1,208,128]{5,4,3,2,1,0:T(8,128)(2,1)S(1)}, u32[]{:S(2)}, u32[]{:S(2)}) %collective-permute-start.1) | collective-permute-done | bytes 106528 | tf_op jit(solution)/shard_map/ppermute | solution.py:23
  22.2 1.5 %collective-permute-start.4 = (bf16[2,2,1,1,208,128]{5,4,3,2,1,0:T(8,128)(2,1)S(1)}, bf16[2,2,1,1,208,128]{5,4,3,2,1,0:T(8,128)(2,1)S(1)}, u32[]{:S(2)}, u32[]{:S(2)}) collective-permute-start(bf16[2,2,1,1,208,128]{5,4,3,2,1,0:T(8,128)(2,1)S(1)} %pad_maximum_fusion.4), channel_id=1, source_target_pairs={{0,4},{1,5},{2,6},{3,7},{4,0},{5,1},{6,2},{7,3},{8,12},{9,13},{10,... | collective-permute-start | bytes 638984 | tf_op jit(solution)/shard_map/ppermute | solution.py:23
  24.3 3.8 %collective-permute-done.4 = bf16[2,2,1,1,208,128]{5,4,3,2,1,0:T(8,128)(2,1)S(1)} collective-permute-done((bf16[2,2,1,1,208,128]{5,4,3,2,1,0:T(8,128)(2,1)S(1)}, bf16[2,2,1,1,208,128]{5,4,3,2,1,0:T(8,128)(2,1)S(1)}, u32[]{:S(2)}, u32[]{:S(2)}) %collective-permute-start.4) | collective-permute-done | bytes 213024 | tf_op jit(solution)/shard_map/ppermute | solution.py:23
  28.1 2.0 %collective-permute-done.5 = bf16[2,1,2,1,208,128]{5,4,3,2,1,0:T(8,128)(2,1)S(1)} collective-permute-done((bf16[2,1,2,1,208,128]{5,4,3,2,1,0:T(8,128)(2,1)S(1)}, bf16[2,1,2,1,208,128]{5,4,3,2,1,0:T(8,128)(2,1)S(1)}, u32[]{:S(2)}, u32[]{:S(2)}) %collective-permute-start.5) | collective-permute-done | bytes 213024 | tf_op jit(solution)/shard_map/ppermute | solution.py:23
  31.5 7.2 %collective-permute-done.7 = bf16[2,2,2,1,208,128]{5,4,3,2,1,0:T(8,128)(2,1)S(1)} collective-permute-done((bf16[2,2,2,1,208,128]{5,4,3,2,1,0:T(8,128)(2,1)S(1)}, bf16[2,2,2,1,208,128]{5,4,3,2,1,0:T(8,128)(2,1)S(1)}, u32[]{:S(2)}, u32[]{:S(2)}) %collective-permute-start.7) | collective-permute-done | bytes 426016 | tf_op jit(solution)/shard_map/ppermute | solution.py:23
  44.7 3.5 %collective-permute-start.13 = (f32[384,128]{1,0:T(8,128)S(1)}, f32[384,128]{1,0:T(8,128)S(1)}, u32[]{:S(2)}, u32[]{:S(2)}) collective-permute-start(f32[384,128]{1,0:T(8,128)S(1)} %get-tuple-element.148), channel_id=1, source_target_pairs={{0,9},{1,10},{2,11},{3,12},{4,13},{5,14},{6,15},{7,16},{8,17},{18,... | collective-permute-start | bytes 589832 | tf_op jit(solution)/shard_map/ppermute | solution.py:19
  50.4 2.6 %collective-permute-done.13.above_ref = f32[384,128]{1,0:T(8,128)S(1)} collective-permute-done((f32[384,128]{1,0:T(8,128)S(1)}, f32[384,128]{1,0:T(8,128)S(1)}, u32[]{:S(2)}, u32[]{:S(2)}) %collective-permute-start.13) | collective-permute-done | bytes 196640 | tf_op jit(solution)/shard_map/ppermute | solution.py:19
  56.6 10.4 %collective-permute-start.16 = (bf16[384,128]{1,0:T(8,128)(2,1)S(1)}, bf16[384,128]{1,0:T(8,128)(2,1)S(1)}, u32[]{:S(2)}, u32[]{:S(2)}) collective-permute-start(bf16[384,128]{1,0:T(8,128)(2,1)S(1)} %get-tuple-element.152), channel_id=1, source_target_pairs={{0,9},{1,10},{2,11},{3,12},{4,13},{5,14},{6,15},{7,16},{8,17},{18,... | collective-permute-start | bytes 294920 | tf_op jit(solution)/shard_map/ppermute | solution.py:19
  74.1 1.9 %collective-permute-start.25 = (bf16[8,240,128]{2,1,0:T(8,128)(2,1)S(1)}, bf16[8,240,128]{2,1,0:T(8,128)(2,1)S(1)}, u32[]{:S(2)}, u32[]{:S(2)}) collective-permute-start(bf16[8,240,128]{2,1,0:T(8,128)(2,1)S(1)} %get-tuple-element.176), channel_id=1, source_target_pairs={{0,4},{1,5},{2,6},{3,7},{4,0},{5,1},{6,2},{7,3},{8,12},{9,13},{10,... | collective-permute-start | bytes 1474568 | tf_op jit(solution)/shard_map/ppermute | solution.py:23
  76.1 3.2 %collective-permute-start.23 = (bf16[8,208,128]{2,1,0:T(8,128)(2,1)S(1)}, bf16[8,208,128]{2,1,0:T(8,128)(2,1)S(1)}, u32[]{:S(2)}, u32[]{:S(2)}) collective-permute-start(bf16[8,208,128]{2,1,0:T(8,128)(2,1)S(1)} %get-tuple-element.174), channel_id=1, source_target_pairs={{0,2},{1,3},{2,0},{3,1},{4,6},{5,7},{6,4},{7,5},{8,10},{9,11},{10,... | collective-permute-start | bytes 1277960 | tf_op jit(solution)/shard_map/ppermute | solution.py:23
  79.2 1.8 %collective-permute-start.24 = (bf16[8,208,128]{2,1,0:T(8,128)(2,1)S(1)}, bf16[8,208,128]{2,1,0:T(8,128)(2,1)S(1)}, u32[]{:S(2)}, u32[]{:S(2)}) collective-permute-start(bf16[8,208,128]{2,1,0:T(8,128)(2,1)S(1)} %get-tuple-element.175), channel_id=1, source_target_pairs={{0,8},{1,9},{2,10},{3,11},{4,12},{5,13},{6,14},{7,15},{8,0},{9,1},... | collective-permute-start | bytes 1277960 | tf_op jit(solution)/shard_map/ppermute | solution.py:23
  81.0 3.8 %input_gradient.1 = bf16[384,2048]{1,0:T(8,128)(2,1)} custom-call(s32[1]{0:T(128)} %bitcast.3.me_ref, bf16[384,384]{1,0:T(8,128)(2,1)S(1)} %get-tuple-element.180.refs_0_, bf16[384,384]{1,0:T(8,128)(2,1)S(1)} %get-tuple-element.181.refs_1_, bf16[384,512]{1,0:T(8,128)(2,1)S(1)} %get-tuple-element.182.refs_2_, bf16[1024,384]{1,0:T(8,128)(2,1)S(1)} %bitcast.56, ...), custom_call_target="tpu_custom_call" | custom-call | flops 2013265920 | bytes 7798784 | tf_op jit(solution)/shard_map/input_gradient/pallas_call | solution.py:153
  84.8 4.1 %collective-permute-done.23.refs_3_ = bf16[8,208,128]{2,1,0:T(8,128)(2,1)S(1)} collective-permute-done((bf16[8,208,128]{2,1,0:T(8,128)(2,1)S(1)}, bf16[8,208,128]{2,1,0:T(8,128)(2,1)S(1)}, u32[]{:S(2)}, u32[]{:S(2)}) %collective-permute-start.23) | collective-permute-done | bytes 426016 | tf_op jit(solution)/shard_map/ppermute | solution.py:23
  88.9 2.0 %collective-permute-done.24.refs_4_ = bf16[8,208,128]{2,1,0:T(8,128)(2,1)S(1)} collective-permute-done((bf16[8,208,128]{2,1,0:T(8,128)(2,1)S(1)}, bf16[8,208,128]{2,1,0:T(8,128)(2,1)S(1)}, u32[]{:S(2)}, u32[]{:S(2)}) %collective-permute-start.24) | collective-permute-done | bytes 426016 | tf_op jit(solution)/shard_map/ppermute | solution.py:23
  91.2 1.8 %collective-permute-start.28 = (bf16[4,240,128]{2,1,0:T(8,128)(2,1)S(1)}, bf16[4,240,128]{2,1,0:T(8,128)(2,1)S(1)}, u32[]{:S(2)}, u32[]{:S(2)}) collective-permute-start(bf16[4,240,128]{2,1,0:T(8,128)(2,1)S(1)} %get-tuple-element.198), channel_id=1, source_target_pairs={{0,8},{1,9},{2,10},{3,11},{4,12},{5,13},{6,14},{7,15},{8,0},{9,1},... | collective-permute-start | bytes 737288 | tf_op jit(solution)/shard_map/ppermute | solution.py:23
  95.0 4.0 %collective-permute-done.26.refs_3_ = bf16[4,208,128]{2,1,0:T(8,128)(2,1)S(1)} collective-permute-done((bf16[4,208,128]{2,1,0:T(8,128)(2,1)S(1)}, bf16[4,208,128]{2,1,0:T(8,128)(2,1)S(1)}, u32[]{:S(2)}, u32[]{:S(2)}) %collective-permute-start.26) | collective-permute-done | bytes 213024 | tf_op jit(solution)/shard_map/ppermute | solution.py:23
  99.7 1.8 %collective-permute-start.31 = (bf16[2,240,128]{2,1,0:T(8,128)(2,1)S(1)}, bf16[2,240,128]{2,1,0:T(8,128)(2,1)S(1)}, u32[]{:S(2)}, u32[]{:S(2)}) collective-permute-start(bf16[2,240,128]{2,1,0:T(8,128)(2,1)S(1)} %get-tuple-element.210), channel_id=1, source_target_pairs={{0,2},{1,3},{2,0},{3,1},{4,6},{5,7},{6,4},{7,5},{8,10},{9,11},{10,... | collective-permute-start | bytes 368648 | tf_op jit(solution)/shard_map/ppermute | solution.py:23
  102.8 3.4 %collective-permute-done.29.refs_3_ = bf16[2,208,128]{2,1,0:T(8,128)(2,1)S(1)} collective-permute-done((bf16[2,208,128]{2,1,0:T(8,128)(2,1)S(1)}, bf16[2,208,128]{2,1,0:T(8,128)(2,1)S(1)}, u32[]{:S(2)}, u32[]{:S(2)}) %collective-permute-start.29) | collective-permute-done | bytes 106528 | tf_op jit(solution)/shard_map/ppermute | solution.py:23
  106.7 3.1 %collective-permute-start.32 = (bf16[656,128]{1,0:T(8,128)(2,1)S(1)}, bf16[656,128]{1,0:T(8,128)(2,1)S(1)}, u32[]{:S(2)}, u32[]{:S(2)}) collective-permute-start(bf16[656,128]{1,0:T(8,128)(2,1)S(1)} %get-tuple-element.215), channel_id=1, source_target_pairs={{0,16},{1,17},{2,18},{3,19},{4,20},{5,21},{6,22},{7,23},{8,24},{9,... | collective-permute-start | bytes 503816 | tf_op jit(solution)/shard_map/ppermute | solution.py:23
  109.8 5.1 %collective-permute-done.32.arrived_ref = bf16[656,128]{1,0:T(8,128)(2,1)S(1)} collective-permute-done((bf16[656,128]{1,0:T(8,128)(2,1)S(1)}, bf16[656,128]{1,0:T(8,128)(2,1)S(1)}, u32[]{:S(2)}, u32[]{:S(2)}) %collective-permute-start.32) | collective-permute-done | bytes 167968 | tf_op jit(solution)/shard_map/ppermute | solution.py:23
  (96 shorter events, 32.1 us)
Async XLA Ops:
  1.6 12.0 %collective-permute-start = (bf16[1,1,1,1,656,128]{5,4,3,2,1,0:T(8,128)(2,1)S(1)}, bf16[1,1,1,1,656,128]{5,4,3,2,1,0:T(8,128)(2,1)S(1)}, u32[]{:S(2)}, u32[]{:S(2)}) collective-permute-start(bf16[1,1,1,1,656,128]{5,4,3,2,1,0:T(8,128)(2,1)S(1)} %bitcast.64), channel_id=1, source_target_pairs={{0,16},{1,17},{2,18},{3,19},{4,20},{5,21},{6,22},{7,23},{8,24},{9,... | collective-permute-start | bytes 503816 | tf_op jit(solution)/shard_map/ppermute | solution.py:23
  13.7 7.0 %collective-permute-start.3 = (bf16[2,1,1,1,240,128]{5,4,3,2,1,0:T(8,128)(2,1)S(1)}, bf16[2,1,1,1,240,128]{5,4,3,2,1,0:T(8,128)(2,1)S(1)}, u32[]{:S(2)}, u32[]{:S(2)}) collective-permute-start(bf16[2,1,1,1,240,128]{5,4,3,2,1,0:T(8,128)(2,1)S(1)} %pad_maximum_fusion.6), channel_id=1, source_target_pairs={{0,2},{1,3},{2,0},{3,1},{4,6},{5,7},{6,4},{7,5},{8,10},{9,11},{10,... | collective-permute-start | bytes 368648 | tf_op jit(solution)/shard_map/ppermute | solution.py:23
  20.8 9.2 %collective-permute-start.6 = (bf16[2,1,1,2,240,128]{5,4,3,2,1,0:T(8,128)(2,1)S(1)}, bf16[2,1,1,2,240,128]{5,4,3,2,1,0:T(8,128)(2,1)S(1)}, u32[]{:S(2)}, u32[]{:S(2)}) collective-permute-start(bf16[2,1,1,2,240,128]{5,4,3,2,1,0:T(8,128)(2,1)S(1)} %pad_maximum_fusion.3), channel_id=1, source_target_pairs={{0,8},{1,9},{2,10},{3,11},{4,12},{5,13},{6,14},{7,15},{8,0},{9,1},... | collective-permute-start | bytes 737288 | tf_op jit(solution)/shard_map/ppermute | solution.py:23
  22.2 5.8 %collective-permute-start.4 = (bf16[2,2,1,1,208,128]{5,4,3,2,1,0:T(8,128)(2,1)S(1)}, bf16[2,2,1,1,208,128]{5,4,3,2,1,0:T(8,128)(2,1)S(1)}, u32[]{:S(2)}, u32[]{:S(2)}) collective-permute-start(bf16[2,2,1,1,208,128]{5,4,3,2,1,0:T(8,128)(2,1)S(1)} %pad_maximum_fusion.4), channel_id=1, source_target_pairs={{0,4},{1,5},{2,6},{3,7},{4,0},{5,1},{6,2},{7,3},{8,12},{9,13},{10,... | collective-permute-start | bytes 638984 | tf_op jit(solution)/shard_map/ppermute | solution.py:23
  23.7 6.3 %collective-permute-start.5 = (bf16[2,1,2,1,208,128]{5,4,3,2,1,0:T(8,128)(2,1)S(1)}, bf16[2,1,2,1,208,128]{5,4,3,2,1,0:T(8,128)(2,1)S(1)}, u32[]{:S(2)}, u32[]{:S(2)}) collective-permute-start(bf16[2,1,2,1,208,128]{5,4,3,2,1,0:T(8,128)(2,1)S(1)} %pad_maximum_fusion.5), channel_id=1, source_target_pairs={{0,2},{1,3},{2,0},{3,1},{4,6},{5,7},{6,4},{7,5},{8,10},{9,11},{10,... | collective-permute-start | bytes 638984 | tf_op jit(solution)/shard_map/ppermute | solution.py:23
  30.2 8.9 %collective-permute-start.9 = (bf16[2,2,1,2,240,128]{5,4,3,2,1,0:T(8,128)(2,1)S(1)}, bf16[2,2,1,2,240,128]{5,4,3,2,1,0:T(8,128)(2,1)S(1)}, u32[]{:S(2)}, u32[]{:S(2)}) collective-permute-start(bf16[2,2,1,2,240,128]{5,4,3,2,1,0:T(8,128)(2,1)S(1)} %pad_maximum_fusion), channel_id=1, source_target_pairs={{0,4},{1,5},{2,6},{3,7},{4,0},{5,1},{6,2},{7,3},{8,12},{9,13},{10,... | collective-permute-start | bytes 1474568 | tf_op jit(solution)/shard_map/ppermute | solution.py:23
  30.3 8.4 %collective-permute-start.7 = (bf16[2,2,2,1,208,128]{5,4,3,2,1,0:T(8,128)(2,1)S(1)}, bf16[2,2,2,1,208,128]{5,4,3,2,1,0:T(8,128)(2,1)S(1)}, u32[]{:S(2)}, u32[]{:S(2)}) collective-permute-start(bf16[2,2,2,1,208,128]{5,4,3,2,1,0:T(8,128)(2,1)S(1)} %pad_maximum_fusion.1), channel_id=1, source_target_pairs={{0,2},{1,3},{2,0},{3,1},{4,6},{5,7},{6,4},{7,5},{8,10},{9,11},{10,... | collective-permute-start | bytes 1277960 | tf_op jit(solution)/shard_map/ppermute | solution.py:23
  30.9 8.1 %collective-permute-start.8 = (bf16[2,1,2,2,208,128]{5,4,3,2,1,0:T(8,128)(2,1)S(1)}, bf16[2,1,2,2,208,128]{5,4,3,2,1,0:T(8,128)(2,1)S(1)}, u32[]{:S(2)}, u32[]{:S(2)}) collective-permute-start(bf16[2,1,2,2,208,128]{5,4,3,2,1,0:T(8,128)(2,1)S(1)} %pad_maximum_fusion.2), channel_id=1, source_target_pairs={{0,8},{1,9},{2,10},{3,11},{4,12},{5,13},{6,14},{7,15},{8,0},{9,1},... | collective-permute-start | bytes 1277960 | tf_op jit(solution)/shard_map/ppermute | solution.py:23
  44.0 5.2 %collective-permute-start.12 = (bf16[1024,512]{1,0:T(8,128)(2,1)S(1)}, bf16[1024,512]{1,0:T(8,128)(2,1)S(1)}, u32[]{:S(2)}, u32[]{:S(2)}) collective-permute-start(bf16[1024,512]{1,0:T(8,128)(2,1)S(1)} %bitcast.51), channel_id=1, source_target_pairs={{0,1},{1,0},{2,3},{3,2},{4,5},{5,4},{6,7},{7,6},{8,9},{9,8},{10,11... | collective-permute-start | bytes 3145736 | tf_op jit(solution)/shard_map/ppermute | solution.py:23
  44.2 4.8 %collective-permute-start.15 = (bf16[128,256]{1,0:T(8,128)(2,1)S(1)}, bf16[128,256]{1,0:T(8,128)(2,1)S(1)}, u32[]{:S(2)}, u32[]{:S(2)}) collective-permute-start(bf16[128,256]{1,0:T(8,128)(2,1)S(1)} %bitcast.74), channel_id=1, source_target_pairs={{0,1},{1,0},{2,3},{3,2},{4,5},{5,4},{6,7},{7,6},{8,9},{9,8},{10,11... | collective-permute-start | bytes 196616 | tf_op jit(solution)/shard_map/ppermute | solution.py:23
  44.6 22.5 %collective-permute-start.18 = (bf16[384,1024]{1,0:T(8,128)(2,1)S(1)}, bf16[384,1024]{1,0:T(8,128)(2,1)S(1)}, u32[]{:S(2)}, u32[]{:S(2)}) collective-permute-start(bf16[384,1024]{1,0:T(8,128)(2,1)S(1)} %get-tuple-element.142), channel_id=1, source_target_pairs={{0,1},{1,0},{2,3},{3,2},{4,5},{5,4},{6,7},{7,6},{8,9},{9,8},{10,11... | collective-permute-start | bytes 2359304 | tf_op jit(solution)/shard_map/ppermute | solution.py:23
  44.7 8.3 %collective-permute-start.13 = (f32[384,128]{1,0:T(8,128)S(1)}, f32[384,128]{1,0:T(8,128)S(1)}, u32[]{:S(2)}, u32[]{:S(2)}) collective-permute-start(f32[384,128]{1,0:T(8,128)S(1)} %get-tuple-element.148), channel_id=1, source_target_pairs={{0,9},{1,10},{2,11},{3,12},{4,13},{5,14},{6,15},{7,16},{8,17},{18,... | collective-permute-start | bytes 589832 | tf_op jit(solution)/shard_map/ppermute | solution.py:19
  54.4 12.7 %collective-permute-start.19 = (bf16[384,512]{1,0:T(8,128)(2,1)S(1)}, bf16[384,512]{1,0:T(8,128)(2,1)S(1)}, u32[]{:S(2)}, u32[]{:S(2)}) collective-permute-start(bf16[384,512]{1,0:T(8,128)(2,1)S(1)} %get-tuple-element.182.refs_2_), channel_id=1, source_target_pairs={{0,1},{1,0},{2,3},{3,2},{4,5},{5,4},{6,7},{7,6},{8,9},{9,8},{10,11... | collective-permute-start | bytes 1179656 | tf_op jit(solution)/shard_map/ppermute | solution.py:23
  55.9 12.7 %collective-permute-start.17 = (bf16[384,128]{1,0:T(8,128)(2,1)S(1)}, bf16[384,128]{1,0:T(8,128)(2,1)S(1)}, u32[]{:S(2)}, u32[]{:S(2)}) collective-permute-start(bf16[384,128]{1,0:T(8,128)(2,1)S(1)} %get-tuple-element.152), channel_id=1, source_target_pairs={{9,18},{10,19},{11,20},{12,21},{13,22},{14,23},{15,24},{16,25},{17... | collective-permute-start | bytes 294920 | tf_op jit(solution)/shard_map/ppermute | solution.py:19
  56.6 12.8 %collective-permute-start.16 = (bf16[384,128]{1,0:T(8,128)(2,1)S(1)}, bf16[384,128]{1,0:T(8,128)(2,1)S(1)}, u32[]{:S(2)}, u32[]{:S(2)}) collective-permute-start(bf16[384,128]{1,0:T(8,128)(2,1)S(1)} %get-tuple-element.152), channel_id=1, source_target_pairs={{0,9},{1,10},{2,11},{3,12},{4,13},{5,14},{6,15},{7,16},{8,17},{18,... | collective-permute-start | bytes 294920 | tf_op jit(solution)/shard_map/ppermute | solution.py:19
  67.0 6.7 %collective-permute-start.22 = (f32[128,256]{1,0:T(8,128)S(1)}, f32[128,256]{1,0:T(8,128)S(1)}, u32[]{:S(2)}, u32[]{:S(2)}) collective-permute-start(f32[128,256]{1,0:T(8,128)S(1)} %get-tuple-element.170), channel_id=1, source_target_pairs={{0,1},{1,0},{2,3},{3,2},{4,5},{5,4},{6,7},{7,6},{8,9},{9,8},{10,11... | collective-permute-start | bytes 393224 | tf_op jit(solution)/shard_map/ppermute | solution.py:23
  74.1 16.8 %collective-permute-start.25 = (bf16[8,240,128]{2,1,0:T(8,128)(2,1)S(1)}, bf16[8,240,128]{2,1,0:T(8,128)(2,1)S(1)}, u32[]{:S(2)}, u32[]{:S(2)}) collective-permute-start(bf16[8,240,128]{2,1,0:T(8,128)(2,1)S(1)} %get-tuple-element.176), channel_id=1, source_target_pairs={{0,4},{1,5},{2,6},{3,7},{4,0},{5,1},{6,2},{7,3},{8,12},{9,13},{10,... | collective-permute-start | bytes 1474568 | tf_op jit(solution)/shard_map/ppermute | solution.py:23
  76.1 12.9 %collective-permute-start.23 = (bf16[8,208,128]{2,1,0:T(8,128)(2,1)S(1)}, bf16[8,208,128]{2,1,0:T(8,128)(2,1)S(1)}, u32[]{:S(2)}, u32[]{:S(2)}) collective-permute-start(bf16[8,208,128]{2,1,0:T(8,128)(2,1)S(1)} %get-tuple-element.174), channel_id=1, source_target_pairs={{0,2},{1,3},{2,0},{3,1},{4,6},{5,7},{6,4},{7,5},{8,10},{9,11},{10,... | collective-permute-start | bytes 1277960 | tf_op jit(solution)/shard_map/ppermute | solution.py:23
  79.2 11.7 %collective-permute-start.24 = (bf16[8,208,128]{2,1,0:T(8,128)(2,1)S(1)}, bf16[8,208,128]{2,1,0:T(8,128)(2,1)S(1)}, u32[]{:S(2)}, u32[]{:S(2)}) collective-permute-start(bf16[8,208,128]{2,1,0:T(8,128)(2,1)S(1)} %get-tuple-element.175), channel_id=1, source_target_pairs={{0,8},{1,9},{2,10},{3,11},{4,12},{5,13},{6,14},{7,15},{8,0},{9,1},... | collective-permute-start | bytes 1277960 | tf_op jit(solution)/shard_map/ppermute | solution.py:23
  91.2 8.4 %collective-permute-start.28 = (bf16[4,240,128]{2,1,0:T(8,128)(2,1)S(1)}, bf16[4,240,128]{2,1,0:T(8,128)(2,1)S(1)}, u32[]{:S(2)}, u32[]{:S(2)}) collective-permute-start(bf16[4,240,128]{2,1,0:T(8,128)(2,1)S(1)} %get-tuple-element.198), channel_id=1, source_target_pairs={{0,8},{1,9},{2,10},{3,11},{4,12},{5,13},{6,14},{7,15},{8,0},{9,1},... | collective-permute-start | bytes 737288 | tf_op jit(solution)/shard_map/ppermute | solution.py:23
  93.0 6.0 %collective-permute-start.26 = (bf16[4,208,128]{2,1,0:T(8,128)(2,1)S(1)}, bf16[4,208,128]{2,1,0:T(8,128)(2,1)S(1)}, u32[]{:S(2)}, u32[]{:S(2)}) collective-permute-start(bf16[4,208,128]{2,1,0:T(8,128)(2,1)S(1)} %get-tuple-element.196), channel_id=1, source_target_pairs={{0,4},{1,5},{2,6},{3,7},{4,0},{5,1},{6,2},{7,3},{8,12},{9,13},{10,... | collective-permute-start | bytes 638984 | tf_op jit(solution)/shard_map/ppermute | solution.py:23
  93.5 6.0 %collective-permute-start.27 = (bf16[4,208,128]{2,1,0:T(8,128)(2,1)S(1)}, bf16[4,208,128]{2,1,0:T(8,128)(2,1)S(1)}, u32[]{:S(2)}, u32[]{:S(2)}) collective-permute-start(bf16[4,208,128]{2,1,0:T(8,128)(2,1)S(1)} %get-tuple-element.197), channel_id=1, source_target_pairs={{0,2},{1,3},{2,0},{3,1},{4,6},{5,7},{6,4},{7,5},{8,10},{9,11},{10,... | collective-permute-start | bytes 638984 | tf_op jit(solution)/shard_map/ppermute | solution.py:23
  99.7 6.9 %collective-permute-start.31 = (bf16[2,240,128]{2,1,0:T(8,128)(2,1)S(1)}, bf16[2,240,128]{2,1,0:T(8,128)(2,1)S(1)}, u32[]{:S(2)}, u32[]{:S(2)}) collective-permute-start(bf16[2,240,128]{2,1,0:T(8,128)(2,1)S(1)} %get-tuple-element.210), channel_id=1, source_target_pairs={{0,2},{1,3},{2,0},{3,1},{4,6},{5,7},{6,4},{7,5},{8,10},{9,11},{10,... | collective-permute-start | bytes 368648 | tf_op jit(solution)/shard_map/ppermute | solution.py:23
  106.7 8.3 %collective-permute-start.32 = (bf16[656,128]{1,0:T(8,128)(2,1)S(1)}, bf16[656,128]{1,0:T(8,128)(2,1)S(1)}, u32[]{:S(2)}, u32[]{:S(2)}) collective-permute-start(bf16[656,128]{1,0:T(8,128)(2,1)S(1)} %get-tuple-element.215), channel_id=1, source_target_pairs={{0,16},{1,17},{2,18},{3,19},{4,20},{5,21},{6,22},{7,23},{8,24},{9,... | collective-permute-start | bytes 503816 | tf_op jit(solution)/shard_map/ppermute | solution.py:23
  (13 other events, 45.0 us)

commit v6 on v5

--- a/solution.py
+++ b/solution.py
@@ -228,25 +228,43 @@
     return me // step % 2 == 0
 
 
-def halo_kernel(width, step, me_ref, first_ref, second_ref, first_out_ref, second_out_ref):
-    branch = first_out_ref.shape[1]
-    sums = []
-    for ref in (first_ref, second_ref):
-        total = None
-        for j in range(3):
-            part = ref[:, j * branch : (j + 1) * branch]
-            moved = moved_rows(part, width, (j - 1) * DILATION_RATE)
-            total = moved if total is None else total + moved
-        sums.append(total)
+def column_sum(ref, width, branch):
+    total = None
+    for j in range(3):
+        moved = moved_rows(ref[:, j * branch : (j + 1) * branch], width, (j - 1) * DILATION_RATE)
+        total = moved if total is None else total + moved
+    return total
+
+
+def partner_kernel(width, first_ref, second_ref, out_ref):
+    pixels, branch = first_ref.shape[0], out_ref.shape[1]
+    out_ref[0:pixels, :] = column_sum(first_ref, width, branch)
+    out_ref[pixels : 2 * pixels, :] = column_sum(second_ref, width, branch)
+
+
+def partner_sums(width, products):
+    pixels, lanes = products[0].shape
+    out = [jax.ShapeDtypeStruct((2 * pixels, lanes // 3), jnp.float32)]
+    kernel = functools.partial(partner_kernel, width)
+    return local_call(kernel, "partner_sums", out, products, 16 * pixels * lanes, 8)[0]
+
+
+def halo_kernel(width, step, me_ref, first_ref, second_ref, came_ref, first_out_ref, second_out_ref):
+    pixels, branch = first_out_ref.shape
+    sums = [
+        column_sum(ref, width, branch) + came_ref[k * pixels : (k + 1) * pixels, :]
+        for k, ref in enumerate((first_ref, second_ref))
+    ]
     upward = is_upward(me_ref[0], step)
     first_out_ref[...] = jnp.where(upward, sums[0], sums[1])
     second_out_ref[...] = jnp.where(upward, sums[1], sums[0])
 
 
-def halo_sums(width, step, products, me):
+def halo_sums(width, step, products, came, me):
     pixels, taps = products[0].shape
     out = jax.ShapeDtypeStruct((pixels, taps // 3), jnp.float32)
-    return halo_call(functools.partial(halo_kernel, width, step), "halo_sums", out, me, *products)
+    kernel = functools.partial(halo_kernel, width, step)
+    return halo_call(kernel, "halo_sums", out, me, *products, came)
 
 
 def shift_kernel(width, step, flip, me_ref, first_ref, second_ref, first_out_ref, second_out_ref):
@@ -268,19 +286,19 @@
     return halo_call(kernel, "shift", out, me, first, second)
 
 
-def halo_call(kernel, name, out, me, first, second):
+def halo_call(kernel, name, out, me, first, *others):
     return pl.pallas_call(
         kernel,
         out_shape=(out, out),
         in_specs=[pl.BlockSpec(memory_space=pltpu.SMEM)]
-        + [pl.BlockSpec(memory_space=pltpu.VMEM)] * 2,
+        + [pl.BlockSpec(memory_space=pltpu.VMEM)] * (1 + len(others)),
         out_specs=(pl.BlockSpec(memory_space=pltpu.VMEM),) * 2,
         cost_estimate=pl.CostEstimate(
             flops=0, bytes_accessed=8 * (first.size + out.size), transcendentals=0
         ),
         compiler_params=pltpu.CompilerParams(vmem_limit_bytes=8 << 20),
         name=name,
-    )(me.reshape(1), first, second)
+    )(me.reshape(1), first, *others)
 
 
 def merge_gradient_kernel(me_ref, joined_ref, grad_out_ref, own_ref, other_ref, total_ref):
@@ -317,7 +335,7 @@
 
 
 def layout(rows, merge_rows, merge_width):
-    shares = (0, rows // 4, rows // 2, rows)
+    shares = (0, rows // 4, 3 * rows // 8, rows)
     tables = []
     for p, portion in enumerate(PORTIONS):
         table = [(k, 0, n * rows, rows) for n, k in enumerate(k for k in portion if k > 0)]
@@ -557,7 +575,7 @@
             base += stack_rows(table)
         for step in range(len(orders[0]) - 1):
             blocks = gathered(together(*blocks), [o[step] for o in orders], bit_count)
-        blocks = together(*blocks)
+        *blocks, flat_partner = together(*blocks, exchanged(flat_other, 0))
         arrived = together(*[exchanged(b, o[-1]) for b, o in zip(blocks, orders)])
         pairs = [
             x.reshape((device_count // 4,) + x.shape[-2:])
@@ -595,14 +613,20 @@
     def by_tap(product):
         return split(product, [branch] * (product.shape[1] // branch))
 
-    other_weight = [exchanged(w, 0) for w in own_weight[:2]]
-    sums = [dot_f32(flat_own, w, 1, 0) for w in own_weight[:2]]
-    other_weight[0], *sums = together(other_weight[0], *sums)
-    sums = [x + dot_f32(flat_other, w, 1, 0) for x, w in zip(sums, other_weight)]
     upward = is_upward(me, device_step)
     if paired:
-        sums = halo_sums(width, device_step, sums, me)
+        sums = partner_sums(width, [dot_f32(flat_partner, w, 1, 0) for w in own_weight[:2]])
+        sums, own_weight[0], own_weight[1] = together(sums, *own_weight[:2])
+        products = [dot_f32(flat_own, w, 1, 0) for w in own_weight[:2]]
+        came, *products = together(exchanged(sums, 0), *products)
+        sums = halo_sums(width, device_step, products, came, me)
+        other_weight = [None, None]
     else:
+        other_weight = [exchanged(w, 0) for w in own_weight[:2]]
+        sums = [
+            dot_f32(flat_own, a, 1, 0) + dot_f32(flat_other, b, 1, 0)
+            for a, b in zip(own_weight, other_weight)
+        ]
         sums = [row_sum(by_tap(x)).reshape(pixels, branch) for x in sums]
         sums = [jnp.where(upward, *sums), jnp.where(upward, *sums[::-1])]
     merge_to_relative = relative_order(joined_width, device_count, me)
@@ -653,10 +677,12 @@
     own_total, other_total = [None] * 3, [None] * 3
     own_total[2] = dot_f32(flat_own, centre_gradient, 0, 0)
     if paired:
-        flat_partner = exchanged(flat_other, 0)
         partner_gradient = exchanged(centre_gradient, 0)
         own_total[2] = own_total[2] + dot_f32(flat_partner, partner_gradient, 0, 0)
-        *halos, own_total[2] = together(*halos, own_total[2])
+        other_weight[:2] = [exchanged(w, 0) for w in own_weight[:2]]
+        *halos, own_total[2], other_weight[0], other_weight[1] = together(
+            *halos, own_total[2], *other_weight[:2]
+        )
         partner_halos = [exchanged(h, 0) for h in halos]
         gradients = [*shifted(width, device_step, *halos, me), centre_gradient]
         own_total[:2] = [dot_f32(flat_own, g, 0, 0) for g in gradients[:2]]

time: 116 us -> 115 us (level)
    ppermute x29 -> x30, starting transfers between devices: 32.9 us -> 32.1 us  [exchanged(): lax.ppermute(block, 'row', [(i, i ^ 1 << bit) for i in range(lax.axis_siz...]
    ppermute x29 -> x30, waiting for transfers between devices: 42.9 us -> 42.2 us  [exchanged(): lax.ppermute(block, 'row', [(i, i ^ 1 << bit) for i in range(lax.axis_siz...]
    pallas_call x6 -> x7, Pallas kernels: 2.09 us -> 2.43 us  [local_call(): pl.pallas_call(kernel, out_shape=out_shape, in_specs=[pl.BlockSpec(memory...]
  transfers between devices with their start and end apart: 33 -> 34, of which waited for: 19 -> 12; matrix products, arithmetic and copies ran while one was open for 7% -> 6% of each run, Pallas kernels for 6% -> 5%
where the time goes in v6:
time: 115 us
  starting transfers between devices  47.3 us (41%)
  waiting for transfers between devices  45.8 us (40%)
  Pallas kernels  10.5 us (9%)
  matrix products  7.84 us (7%)
  local copies, waits for them, and re-layouts  1.46 us (1%)
    ppermute x30, waiting for transfers between devices, exchanged(): lax.ppermute(block, 'row', [(i, i ^ 1 << bit) for i in range(lax.axis_siz...  42.2 us
    ppermute x30, starting transfers between devices, exchanged(): lax.ppermute(block, 'row', [(i, i ^ 1 << bit) for i in range(lax.axis_siz...  32.1 us
    ppermute x4, starting transfers between devices, swapped(): return lax.ppermute(block, 'row', pairs + [(b, a) for a, b in pairs])  15.2 us
    dot_general x13, matrix products, dot_f32(): lax.dot_general(left, right, (((left_dim,), (right_dim,)), ((), ())), pre...  7.84 us
    pallas_call x1, Pallas kernels, input_gradient(): pl.pallas_call(functools.partial(input_gradient_kernel, len(gradients)),...  3.78 us
    ppermute x4, waiting for transfers between devices, swapped(): return lax.ppermute(block, 'row', pairs + [(b, a) for a, b in pairs])  3.55 us
    pallas_call x7, Pallas kernels, local_call(): pl.pallas_call(kernel, out_shape=out_shape, in_specs=[pl.BlockSpec(memory...  2.43 us
  transfers between devices with their start and end apart: 34, of which 12 were waited for; matrix products, arithmetic and copies ran while one was open for 6% of the time, Pallas kernels for 5%

profile of v6, /device:TPU:0, one launch (start us, length us, event | category | flops | bytes accessed | tf_op | source)
XLA Modules:
  0.0 114.5 jit_solution(17709278728418339441)
XLA Ops:
  1.6 4.1 %collective-permute-start = (bf16[1,1,1,1,656,128]{5,4,3,2,1,0:T(8,128)(2,1)S(1)}, bf16[1,1,1,1,656,128]{5,4,3,2,1,0:T(8,128)(2,1)S(1)}, u32[]{:S(2)}, u32[]{:S(2)}) collective-permute-start(bf16[1,1,1,1,656,128]{5,4,3,2,1,0:T(8,128)(2,1)S(1)} %bitcast.66), channel_id=1, source_target_pairs={{0,16},{1,17},{2,18},{3,19},{4,20},{5,21},{6,22},{7,23},{8,24},{9,... | collective-permute-start | bytes 503816 | tf_op jit(solution)/shard_map/ppermute | solution.py:23
  5.7 1.4 %copy-done = bf16[2,192,2048]{2,1,0:T(8,128)(2,1)S(1)} copy-done((bf16[2,192,2048]{2,1,0:T(8,128)(2,1)S(1)}, bf16[2,192,2048]{2,1,0:T(8,128)(2,1)}, u32[]{:S(2)}) %copy-start) | copy-done | bytes 1572888
  8.1 5.5 %collective-permute-done = bf16[1,1,1,1,656,128]{5,4,3,2,1,0:T(8,128)(2,1)S(1)} collective-permute-done((bf16[1,1,1,1,656,128]{5,4,3,2,1,0:T(8,128)(2,1)S(1)}, bf16[1,1,1,1,656,128]{5,4,3,2,1,0:T(8,128)(2,1)S(1)}, u32[]{:S(2)}, u32[]{:S(2)}) %collective-permute-start) | collective-permute-done | bytes 167968 | tf_op jit(solution)/shard_map/ppermute | solution.py:23
  13.8 1.6 %collective-permute-start.3 = (bf16[2,1,1,1,248,128]{5,4,3,2,1,0:T(8,128)(2,1)S(1)}, bf16[2,1,1,1,248,128]{5,4,3,2,1,0:T(8,128)(2,1)S(1)}, u32[]{:S(2)}, u32[]{:S(2)}) collective-permute-start(bf16[2,1,1,1,248,128]{5,4,3,2,1,0:T(8,128)(2,1)S(1)} %pad_maximum_fusion.6), channel_id=1, source_target_pairs={{0,2},{1,3},{2,0},{3,1},{4,6},{5,7},{6,4},{7,5},{8,10},{9,11},{10,... | collective-permute-start | bytes 380936 | tf_op jit(solution)/shard_map/ppermute | solution.py:23
  16.0 1.5 %collective-permute-start.2 = (bf16[2,1,1,1,200,128]{5,4,3,2,1,0:T(8,128)(2,1)S(1)}, bf16[2,1,1,1,200,128]{5,4,3,2,1,0:T(8,128)(2,1)S(1)}, u32[]{:S(2)}, u32[]{:S(2)}) collective-permute-start(bf16[2,1,1,1,200,128]{5,4,3,2,1,0:T(8,128)(2,1)S(1)} %pad_maximum_fusion.8), channel_id=1, source_target_pairs={{0,4},{1,5},{2,6},{3,7},{4,0},{5,1},{6,2},{7,3},{8,12},{9,13},{10,... | collective-permute-start | bytes 307208 | tf_op jit(solution)/shard_map/ppermute | solution.py:23
  17.6 3.1 %collective-permute-done.2 = bf16[2,1,1,1,200,128]{5,4,3,2,1,0:T(8,128)(2,1)S(1)} collective-permute-done((bf16[2,1,1,1,200,128]{5,4,3,2,1,0:T(8,128)(2,1)S(1)}, bf16[2,1,1,1,200,128]{5,4,3,2,1,0:T(8,128)(2,1)S(1)}, u32[]{:S(2)}, u32[]{:S(2)}) %collective-permute-start.2) | collective-permute-done | bytes 102432 | tf_op jit(solution)/shard_map/ppermute | solution.py:23
  20.8 1.4 %collective-permute-start.6 = (bf16[2,1,1,2,248,128]{5,4,3,2,1,0:T(8,128)(2,1)S(1)}, bf16[2,1,1,2,248,128]{5,4,3,2,1,0:T(8,128)(2,1)S(1)}, u32[]{:S(2)}, u32[]{:S(2)}) collective-permute-start(bf16[2,1,1,2,248,128]{5,4,3,2,1,0:T(8,128)(2,1)S(1)} %pad_maximum_fusion.3), channel_id=1, source_target_pairs={{0,8},{1,9},{2,10},{3,11},{4,12},{5,13},{6,14},{7,15},{8,0},{9,1},... | collective-permute-start | bytes 761864 | tf_op jit(solution)/shard_map/ppermute | solution.py:23
  22.2 1.5 %collective-permute-start.4 = (bf16[2,2,1,1,208,128]{5,4,3,2,1,0:T(8,128)(2,1)S(1)}, bf16[2,2,1,1,208,128]{5,4,3,2,1,0:T(8,128)(2,1)S(1)}, u32[]{:S(2)}, u32[]{:S(2)}) collective-permute-start(bf16[2,2,1,1,208,128]{5,4,3,2,1,0:T(8,128)(2,1)S(1)} %pad_maximum_fusion.4), channel_id=1, source_target_pairs={{0,4},{1,5},{2,6},{3,7},{4,0},{5,1},{6,2},{7,3},{8,12},{9,13},{10,... | collective-permute-start | bytes 638984 | tf_op jit(solution)/shard_map/ppermute | solution.py:23
  24.3 5.4 %collective-permute-done.5 = bf16[2,1,2,1,200,128]{5,4,3,2,1,0:T(8,128)(2,1)S(1)} collective-permute-done((bf16[2,1,2,1,200,128]{5,4,3,2,1,0:T(8,128)(2,1)S(1)}, bf16[2,1,2,1,200,128]{5,4,3,2,1,0:T(8,128)(2,1)S(1)}, u32[]{:S(2)}, u32[]{:S(2)}) %collective-permute-start.5) | collective-permute-done | bytes 204832 | tf_op jit(solution)/shard_map/ppermute | solution.py:23
  31.4 7.2 %collective-permute-done.9 = bf16[2,1,2,2,200,128]{5,4,3,2,1,0:T(8,128)(2,1)S(1)} collective-permute-done((bf16[2,1,2,2,200,128]{5,4,3,2,1,0:T(8,128)(2,1)S(1)}, bf16[2,1,2,2,200,128]{5,4,3,2,1,0:T(8,128)(2,1)S(1)}, u32[]{:S(2)}, u32[]{:S(2)}) %collective-permute-start.9) | collective-permute-done | bytes 409632 | tf_op jit(solution)/shard_map/ppermute | solution.py:23
  44.0 3.3 %collective-permute-start.13 = (f32[384,128]{1,0:T(8,128)S(1)}, f32[384,128]{1,0:T(8,128)S(1)}, u32[]{:S(2)}, u32[]{:S(2)}) collective-permute-start(f32[384,128]{1,0:T(8,128)S(1)} %get-tuple-element.158), channel_id=1, source_target_pairs={{0,9},{1,10},{2,11},{3,12},{4,13},{5,14},{6,15},{7,16},{8,17},{18,... | collective-permute-start | bytes 589832 | tf_op jit(solution)/shard_map/ppermute | solution.py:19
  49.4 2.8 %collective-permute-done.13.above_ref = f32[384,128]{1,0:T(8,128)S(1)} collective-permute-done((f32[384,128]{1,0:T(8,128)S(1)}, f32[384,128]{1,0:T(8,128)S(1)}, u32[]{:S(2)}, u32[]{:S(2)}) %collective-permute-start.13) | collective-permute-done | bytes 196640 | tf_op jit(solution)/shard_map/ppermute | solution.py:19
  55.9 10.6 %collective-permute-start.16 = (bf16[384,128]{1,0:T(8,128)(2,1)S(1)}, bf16[384,128]{1,0:T(8,128)(2,1)S(1)}, u32[]{:S(2)}, u32[]{:S(2)}) collective-permute-start(bf16[384,128]{1,0:T(8,128)(2,1)S(1)} %get-tuple-element.162), channel_id=1, source_target_pairs={{0,9},{1,10},{2,11},{3,12},{4,13},{5,14},{6,15},{7,16},{8,17},{18,... | collective-permute-start | bytes 294920 | tf_op jit(solution)/shard_map/ppermute | solution.py:19
  74.9 3.1 %collective-permute-start.24 = (bf16[8,208,128]{2,1,0:T(8,128)(2,1)S(1)}, bf16[8,208,128]{2,1,0:T(8,128)(2,1)S(1)}, u32[]{:S(2)}, u32[]{:S(2)}) collective-permute-start(bf16[8,208,128]{2,1,0:T(8,128)(2,1)S(1)} %get-tuple-element.184), channel_id=1, source_target_pairs={{0,2},{1,3},{2,0},{3,1},{4,6},{5,7},{6,4},{7,5},{8,10},{9,11},{10,... | collective-permute-start | bytes 1277960 | tf_op jit(solution)/shard_map/ppermute | solution.py:23
  78.1 1.8 %collective-permute-start.25 = (bf16[8,200,128]{2,1,0:T(8,128)(2,1)S(1)}, bf16[8,200,128]{2,1,0:T(8,128)(2,1)S(1)}, u32[]{:S(2)}, u32[]{:S(2)}) collective-permute-start(bf16[8,200,128]{2,1,0:T(8,128)(2,1)S(1)} %get-tuple-element.185), channel_id=1, source_target_pairs={{0,8},{1,9},{2,10},{3,11},{4,12},{5,13},{6,14},{7,15},{8,0},{9,1},... | collective-permute-start | bytes 1228808 | tf_op jit(solution)/shard_map/ppermute | solution.py:23
  79.9 3.8 %input_gradient.1 = bf16[384,2048]{1,0:T(8,128)(2,1)} custom-call(s32[1]{0:T(128)} %bitcast.3.me_ref, bf16[384,384]{1,0:T(8,128)(2,1)S(1)} %get-tuple-element.190.refs_0_, bf16[384,384]{1,0:T(8,128)(2,1)S(1)} %get-tuple-element.191.refs_1_, bf16[384,512]{1,0:T(8,128)(2,1)S(1)} %get-tuple-element.192.refs_2_, bf16[1024,384]{1,0:T(8,128)(2,1)S(1)} %bitcast.52, ...), custom_call_target="tpu_custom_call" | custom-call | flops 2013265920 | bytes 7798784 | tf_op jit(solution)/shard_map/input_gradient/pallas_call | solution.py:153
  83.6 5.8 %collective-permute-done.25.refs_4_ = bf16[8,200,128]{2,1,0:T(8,128)(2,1)S(1)} collective-permute-done((bf16[8,200,128]{2,1,0:T(8,128)(2,1)S(1)}, bf16[8,200,128]{2,1,0:T(8,128)(2,1)S(1)}, u32[]{:S(2)}, u32[]{:S(2)}) %collective-permute-start.25) | collective-permute-done | bytes 409632 | tf_op jit(solution)/shard_map/ppermute | solution.py:23
  89.7 1.8 %collective-permute-start.29 = (bf16[4,248,128]{2,1,0:T(8,128)(2,1)S(1)}, bf16[4,248,128]{2,1,0:T(8,128)(2,1)S(1)}, u32[]{:S(2)}, u32[]{:S(2)}) collective-permute-start(bf16[4,248,128]{2,1,0:T(8,128)(2,1)S(1)} %get-tuple-element.210), channel_id=1, source_target_pairs={{0,8},{1,9},{2,10},{3,11},{4,12},{5,13},{6,14},{7,15},{8,0},{9,1},... | collective-permute-start | bytes 761864 | tf_op jit(solution)/shard_map/ppermute | solution.py:23
  91.5 1.6 %collective-permute-start.27 = (bf16[4,208,128]{2,1,0:T(8,128)(2,1)S(1)}, bf16[4,208,128]{2,1,0:T(8,128)(2,1)S(1)}, u32[]{:S(2)}, u32[]{:S(2)}) collective-permute-start(bf16[4,208,128]{2,1,0:T(8,128)(2,1)S(1)} %get-tuple-element.208), channel_id=1, source_target_pairs={{0,4},{1,5},{2,6},{3,7},{4,0},{5,1},{6,2},{7,3},{8,12},{9,13},{10,... | collective-permute-start | bytes 638984 | tf_op jit(solution)/shard_map/ppermute | solution.py:23
  94.2 4.7 %collective-permute-done.28.refs_4_ = bf16[4,200,128]{2,1,0:T(8,128)(2,1)S(1)} collective-permute-done((bf16[4,200,128]{2,1,0:T(8,128)(2,1)S(1)}, bf16[4,200,128]{2,1,0:T(8,128)(2,1)S(1)}, u32[]{:S(2)}, u32[]{:S(2)}) %collective-permute-start.28) | collective-permute-done | bytes 204832 | tf_op jit(solution)/shard_map/ppermute | solution.py:23
  99.0 1.5 %collective-permute-start.32 = (bf16[2,248,128]{2,1,0:T(8,128)(2,1)S(1)}, bf16[2,248,128]{2,1,0:T(8,128)(2,1)S(1)}, u32[]{:S(2)}, u32[]{:S(2)}) collective-permute-start(bf16[2,248,128]{2,1,0:T(8,128)(2,1)S(1)} %get-tuple-element.222), channel_id=1, source_target_pairs={{0,2},{1,3},{2,0},{3,1},{4,6},{5,7},{6,4},{7,5},{8,10},{9,11},{10,... | collective-permute-start | bytes 380936 | tf_op jit(solution)/shard_map/ppermute | solution.py:23
  102.1 3.4 %collective-permute-done.31.refs_4_ = bf16[2,200,128]{2,1,0:T(8,128)(2,1)S(1)} collective-permute-done((bf16[2,200,128]{2,1,0:T(8,128)(2,1)S(1)}, bf16[2,200,128]{2,1,0:T(8,128)(2,1)S(1)}, u32[]{:S(2)}, u32[]{:S(2)}) %collective-permute-start.31) | collective-permute-done | bytes 102432 | tf_op jit(solution)/shard_map/ppermute | solution.py:23
  105.6 2.4 %collective-permute-start.33 = (bf16[656,128]{1,0:T(8,128)(2,1)S(1)}, bf16[656,128]{1,0:T(8,128)(2,1)S(1)}, u32[]{:S(2)}, u32[]{:S(2)}) collective-permute-start(bf16[656,128]{1,0:T(8,128)(2,1)S(1)} %get-tuple-element.227), channel_id=1, source_target_pairs={{0,16},{1,17},{2,18},{3,19},{4,20},{5,21},{6,22},{7,23},{8,24},{9,... | collective-permute-start | bytes 503816 | tf_op jit(solution)/shard_map/ppermute | solution.py:23
  108.1 5.7 %collective-permute-done.33.arrived_ref = bf16[656,128]{1,0:T(8,128)(2,1)S(1)} collective-permute-done((bf16[656,128]{1,0:T(8,128)(2,1)S(1)}, bf16[656,128]{1,0:T(8,128)(2,1)S(1)}, u32[]{:S(2)}, u32[]{:S(2)}) %collective-permute-start.33) | collective-permute-done | bytes 167968 | tf_op jit(solution)/shard_map/ppermute | solution.py:23
  (100 shorter events, 28.2 us)
Async XLA Ops:
  1.6 12.0 %collective-permute-start = (bf16[1,1,1,1,656,128]{5,4,3,2,1,0:T(8,128)(2,1)S(1)}, bf16[1,1,1,1,656,128]{5,4,3,2,1,0:T(8,128)(2,1)S(1)}, u32[]{:S(2)}, u32[]{:S(2)}) collective-permute-start(bf16[1,1,1,1,656,128]{5,4,3,2,1,0:T(8,128)(2,1)S(1)} %bitcast.66), channel_id=1, source_target_pairs={{0,16},{1,17},{2,18},{3,19},{4,20},{5,21},{6,22},{7,23},{8,24},{9,... | collective-permute-start | bytes 503816 | tf_op jit(solution)/shard_map/ppermute | solution.py:23
  13.8 6.9 %collective-permute-start.3 = (bf16[2,1,1,1,248,128]{5,4,3,2,1,0:T(8,128)(2,1)S(1)}, bf16[2,1,1,1,248,128]{5,4,3,2,1,0:T(8,128)(2,1)S(1)}, u32[]{:S(2)}, u32[]{:S(2)}) collective-permute-start(bf16[2,1,1,1,248,128]{5,4,3,2,1,0:T(8,128)(2,1)S(1)} %pad_maximum_fusion.6), channel_id=1, source_target_pairs={{0,2},{1,3},{2,0},{3,1},{4,6},{5,7},{6,4},{7,5},{8,10},{9,11},{10,... | collective-permute-start | bytes 380936 | tf_op jit(solution)/shard_map/ppermute | solution.py:23
  17.6 12.3 %collective-permute-start.7 = (bf16[384,1024]{1,0:T(8,128)(2,1)S(1)}, bf16[384,1024]{1,0:T(8,128)(2,1)S(1)}, u32[]{:S(2)}, u32[]{:S(2)}) collective-permute-start(bf16[384,1024]{1,0:T(8,128)(2,1)S(1)} %get-tuple-element.137), channel_id=1, source_target_pairs={{0,1},{1,0},{2,3},{3,2},{4,5},{5,4},{6,7},{7,6},{8,9},{9,8},{10,11... | collective-permute-start | bytes 2359304 | tf_op jit(solution)/shard_map/ppermute | solution.py:23
  20.8 8.9 %collective-permute-start.6 = (bf16[2,1,1,2,248,128]{5,4,3,2,1,0:T(8,128)(2,1)S(1)}, bf16[2,1,1,2,248,128]{5,4,3,2,1,0:T(8,128)(2,1)S(1)}, u32[]{:S(2)}, u32[]{:S(2)}) collective-permute-start(bf16[2,1,1,2,248,128]{5,4,3,2,1,0:T(8,128)(2,1)S(1)} %pad_maximum_fusion.3), channel_id=1, source_target_pairs={{0,8},{1,9},{2,10},{3,11},{4,12},{5,13},{6,14},{7,15},{8,0},{9,1},... | collective-permute-start | bytes 761864 | tf_op jit(solution)/shard_map/ppermute | solution.py:23
  22.2 7.5 %collective-permute-start.4 = (bf16[2,2,1,1,208,128]{5,4,3,2,1,0:T(8,128)(2,1)S(1)}, bf16[2,2,1,1,208,128]{5,4,3,2,1,0:T(8,128)(2,1)S(1)}, u32[]{:S(2)}, u32[]{:S(2)}) collective-permute-start(bf16[2,2,1,1,208,128]{5,4,3,2,1,0:T(8,128)(2,1)S(1)} %pad_maximum_fusion.4), channel_id=1, source_target_pairs={{0,4},{1,5},{2,6},{3,7},{4,0},{5,1},{6,2},{7,3},{8,12},{9,13},{10,... | collective-permute-start | bytes 638984 | tf_op jit(solution)/shard_map/ppermute | solution.py:23
  23.7 5.9 %collective-permute-start.5 = (bf16[2,1,2,1,200,128]{5,4,3,2,1,0:T(8,128)(2,1)S(1)}, bf16[2,1,2,1,200,128]{5,4,3,2,1,0:T(8,128)(2,1)S(1)}, u32[]{:S(2)}, u32[]{:S(2)}) collective-permute-start(bf16[2,1,2,1,200,128]{5,4,3,2,1,0:T(8,128)(2,1)S(1)} %pad_maximum_fusion.5), channel_id=1, source_target_pairs={{0,2},{1,3},{2,0},{3,1},{4,6},{5,7},{6,4},{7,5},{8,10},{9,11},{10,... | collective-permute-start | bytes 614408 | tf_op jit(solution)/shard_map/ppermute | solution.py:23
  29.8 9.5 %collective-permute-start.10 = (bf16[2,2,1,2,248,128]{5,4,3,2,1,0:T(8,128)(2,1)S(1)}, bf16[2,2,1,2,248,128]{5,4,3,2,1,0:T(8,128)(2,1)S(1)}, u32[]{:S(2)}, u32[]{:S(2)}) collective-permute-start(bf16[2,2,1,2,248,128]{5,4,3,2,1,0:T(8,128)(2,1)S(1)} %pad_maximum_fusion), channel_id=1, source_target_pairs={{0,4},{1,5},{2,6},{3,7},{4,0},{5,1},{6,2},{7,3},{8,12},{9,13},{10,... | collective-permute-start | bytes 1523720 | tf_op jit(solution)/shard_map/ppermute | solution.py:23
  30.2 8.4 %collective-permute-start.8 = (bf16[2,2,2,1,208,128]{5,4,3,2,1,0:T(8,128)(2,1)S(1)}, bf16[2,2,2,1,208,128]{5,4,3,2,1,0:T(8,128)(2,1)S(1)}, u32[]{:S(2)}, u32[]{:S(2)}) collective-permute-start(bf16[2,2,2,1,208,128]{5,4,3,2,1,0:T(8,128)(2,1)S(1)} %pad_maximum_fusion.1), channel_id=1, source_target_pairs={{0,2},{1,3},{2,0},{3,1},{4,6},{5,7},{6,4},{7,5},{8,10},{9,11},{10,... | collective-permute-start | bytes 1277960 | tf_op jit(solution)/shard_map/ppermute | solution.py:23
  30.7 8.0 %collective-permute-start.9 = (bf16[2,1,2,2,200,128]{5,4,3,2,1,0:T(8,128)(2,1)S(1)}, bf16[2,1,2,2,200,128]{5,4,3,2,1,0:T(8,128)(2,1)S(1)}, u32[]{:S(2)}, u32[]{:S(2)}) collective-permute-start(bf16[2,1,2,2,200,128]{5,4,3,2,1,0:T(8,128)(2,1)S(1)} %pad_maximum_fusion.2), channel_id=1, source_target_pairs={{0,8},{1,9},{2,10},{3,11},{4,12},{5,13},{6,14},{7,15},{8,0},{9,1},... | collective-permute-start | bytes 1228808 | tf_op jit(solution)/shard_map/ppermute | solution.py:23
  44.0 8.2 %collective-permute-start.13 = (f32[384,128]{1,0:T(8,128)S(1)}, f32[384,128]{1,0:T(8,128)S(1)}, u32[]{:S(2)}, u32[]{:S(2)}) collective-permute-start(f32[384,128]{1,0:T(8,128)S(1)} %get-tuple-element.158), channel_id=1, source_target_pairs={{0,9},{1,10},{2,11},{3,12},{4,13},{5,14},{6,15},{7,16},{8,17},{18,... | collective-permute-start | bytes 589832 | tf_op jit(solution)/shard_map/ppermute | solution.py:19
  53.7 12.8 %collective-permute-start.18 = (bf16[384,512]{1,0:T(8,128)(2,1)S(1)}, bf16[384,512]{1,0:T(8,128)(2,1)S(1)}, u32[]{:S(2)}, u32[]{:S(2)}) collective-permute-start(bf16[384,512]{1,0:T(8,128)(2,1)S(1)} %get-tuple-element.192.refs_2_), channel_id=1, source_target_pairs={{0,1},{1,0},{2,3},{3,2},{4,5},{5,4},{6,7},{7,6},{8,9},{9,8},{10,11... | collective-permute-start | bytes 1179656 | tf_op jit(solution)/shard_map/ppermute | solution.py:23
  54.7 13.4 %collective-permute-start.19 = (bf16[1024,384]{1,0:T(8,128)(2,1)S(1)}, bf16[1024,384]{1,0:T(8,128)(2,1)S(1)}, u32[]{:S(2)}, u32[]{:S(2)}) collective-permute-start(bf16[1024,384]{1,0:T(8,128)(2,1)S(1)} %bitcast.51), channel_id=1, source_target_pairs={{0,1},{1,0},{2,3},{3,2},{4,5},{5,4},{6,7},{7,6},{8,9},{9,8},{10,11... | collective-permute-start | bytes 2359304 | tf_op jit(solution)/shard_map/ppermute | solution.py:23
  54.8 13.3 %collective-permute-start.20 = (bf16[1024,384]{1,0:T(8,128)(2,1)S(1)}, bf16[1024,384]{1,0:T(8,128)(2,1)S(1)}, u32[]{:S(2)}, u32[]{:S(2)}) collective-permute-start(bf16[1024,384]{1,0:T(8,128)(2,1)S(1)} %bitcast.55), channel_id=1, source_target_pairs={{0,1},{1,0},{2,3},{3,2},{4,5},{5,4},{6,7},{7,6},{8,9},{9,8},{10,11... | collective-permute-start | bytes 2359304 | tf_op jit(solution)/shard_map/ppermute | solution.py:23
  55.2 12.9 %collective-permute-start.17 = (bf16[384,128]{1,0:T(8,128)(2,1)S(1)}, bf16[384,128]{1,0:T(8,128)(2,1)S(1)}, u32[]{:S(2)}, u32[]{:S(2)}) collective-permute-start(bf16[384,128]{1,0:T(8,128)(2,1)S(1)} %get-tuple-element.162), channel_id=1, source_target_pairs={{9,18},{10,19},{11,20},{12,21},{13,22},{14,23},{15,24},{16,25},{17... | collective-permute-start | bytes 294920 | tf_op jit(solution)/shard_map/ppermute | solution.py:19
  55.9 12.9 %collective-permute-start.16 = (bf16[384,128]{1,0:T(8,128)(2,1)S(1)}, bf16[384,128]{1,0:T(8,128)(2,1)S(1)}, u32[]{:S(2)}, u32[]{:S(2)}) collective-permute-start(bf16[384,128]{1,0:T(8,128)(2,1)S(1)} %get-tuple-element.162), channel_id=1, source_target_pairs={{0,9},{1,10},{2,11},{3,12},{4,13},{5,14},{6,15},{7,16},{8,17},{18,... | collective-permute-start | bytes 294920 | tf_op jit(solution)/shard_map/ppermute | solution.py:19
  66.5 6.8 %collective-permute-start.23 = (f32[128,256]{1,0:T(8,128)S(1)}, f32[128,256]{1,0:T(8,128)S(1)}, u32[]{:S(2)}, u32[]{:S(2)}) collective-permute-start(f32[128,256]{1,0:T(8,128)S(1)} %get-tuple-element.180), channel_id=1, source_target_pairs={{0,1},{1,0},{2,3},{3,2},{4,5},{5,4},{6,7},{7,6},{8,9},{9,8},{10,11... | collective-permute-start | bytes 393224 | tf_op jit(solution)/shard_map/ppermute | solution.py:23
  73.6 15.8 %collective-permute-start.26 = (bf16[8,248,128]{2,1,0:T(8,128)(2,1)S(1)}, bf16[8,248,128]{2,1,0:T(8,128)(2,1)S(1)}, u32[]{:S(2)}, u32[]{:S(2)}) collective-permute-start(bf16[8,248,128]{2,1,0:T(8,128)(2,1)S(1)} %get-tuple-element.186), channel_id=1, source_target_pairs={{0,4},{1,5},{2,6},{3,7},{4,0},{5,1},{6,2},{7,3},{8,12},{9,13},{10,... | collective-permute-start | bytes 1523720 | tf_op jit(solution)/shard_map/ppermute | solution.py:23
  74.9 14.5 %collective-permute-start.24 = (bf16[8,208,128]{2,1,0:T(8,128)(2,1)S(1)}, bf16[8,208,128]{2,1,0:T(8,128)(2,1)S(1)}, u32[]{:S(2)}, u32[]{:S(2)}) collective-permute-start(bf16[8,208,128]{2,1,0:T(8,128)(2,1)S(1)} %get-tuple-element.184), channel_id=1, source_target_pairs={{0,2},{1,3},{2,0},{3,1},{4,6},{5,7},{6,4},{7,5},{8,10},{9,11},{10,... | collective-permute-start | bytes 1277960 | tf_op jit(solution)/shard_map/ppermute | solution.py:23
  78.1 11.4 %collective-permute-start.25 = (bf16[8,200,128]{2,1,0:T(8,128)(2,1)S(1)}, bf16[8,200,128]{2,1,0:T(8,128)(2,1)S(1)}, u32[]{:S(2)}, u32[]{:S(2)}) collective-permute-start(bf16[8,200,128]{2,1,0:T(8,128)(2,1)S(1)} %get-tuple-element.185), channel_id=1, source_target_pairs={{0,8},{1,9},{2,10},{3,11},{4,12},{5,13},{6,14},{7,15},{8,0},{9,1},... | collective-permute-start | bytes 1228808 | tf_op jit(solution)/shard_map/ppermute | solution.py:23
  89.7 9.2 %collective-permute-start.29 = (bf16[4,248,128]{2,1,0:T(8,128)(2,1)S(1)}, bf16[4,248,128]{2,1,0:T(8,128)(2,1)S(1)}, u32[]{:S(2)}, u32[]{:S(2)}) collective-permute-start(bf16[4,248,128]{2,1,0:T(8,128)(2,1)S(1)} %get-tuple-element.210), channel_id=1, source_target_pairs={{0,8},{1,9},{2,10},{3,11},{4,12},{5,13},{6,14},{7,15},{8,0},{9,1},... | collective-permute-start | bytes 761864 | tf_op jit(solution)/shard_map/ppermute | solution.py:23
  91.5 7.3 %collective-permute-start.27 = (bf16[4,208,128]{2,1,0:T(8,128)(2,1)S(1)}, bf16[4,208,128]{2,1,0:T(8,128)(2,1)S(1)}, u32[]{:S(2)}, u32[]{:S(2)}) collective-permute-start(bf16[4,208,128]{2,1,0:T(8,128)(2,1)S(1)} %get-tuple-element.208), channel_id=1, source_target_pairs={{0,4},{1,5},{2,6},{3,7},{4,0},{5,1},{6,2},{7,3},{8,12},{9,13},{10,... | collective-permute-start | bytes 638984 | tf_op jit(solution)/shard_map/ppermute | solution.py:23
  93.1 5.8 %collective-permute-start.28 = (bf16[4,200,128]{2,1,0:T(8,128)(2,1)S(1)}, bf16[4,200,128]{2,1,0:T(8,128)(2,1)S(1)}, u32[]{:S(2)}, u32[]{:S(2)}) collective-permute-start(bf16[4,200,128]{2,1,0:T(8,128)(2,1)S(1)} %get-tuple-element.209), channel_id=1, source_target_pairs={{0,2},{1,3},{2,0},{3,1},{4,6},{5,7},{6,4},{7,5},{8,10},{9,11},{10,... | collective-permute-start | bytes 614408 | tf_op jit(solution)/shard_map/ppermute | solution.py:23
  99.0 6.6 %collective-permute-start.32 = (bf16[2,248,128]{2,1,0:T(8,128)(2,1)S(1)}, bf16[2,248,128]{2,1,0:T(8,128)(2,1)S(1)}, u32[]{:S(2)}, u32[]{:S(2)}) collective-permute-start(bf16[2,248,128]{2,1,0:T(8,128)(2,1)S(1)} %get-tuple-element.222), channel_id=1, source_target_pairs={{0,2},{1,3},{2,0},{3,1},{4,6},{5,7},{6,4},{7,5},{8,10},{9,11},{10,... | collective-permute-start | bytes 380936 | tf_op jit(solution)/shard_map/ppermute | solution.py:23
  105.6 8.1 %collective-permute-start.33 = (bf16[656,128]{1,0:T(8,128)(2,1)S(1)}, bf16[656,128]{1,0:T(8,128)(2,1)S(1)}, u32[]{:S(2)}, u32[]{:S(2)}) collective-permute-start(bf16[656,128]{1,0:T(8,128)(2,1)S(1)} %get-tuple-element.227), channel_id=1, source_target_pairs={{0,16},{1,17},{2,18},{3,19},{4,20},{5,21},{6,22},{7,23},{8,24},{9,... | collective-permute-start | bytes 503816 | tf_op jit(solution)/shard_map/ppermute | solution.py:23
  (14 other events, 51.9 us)

commit v7 on v6

--- a/solution.py
+++ b/solution.py
@@ -124,8 +124,9 @@
     me = me_ref[0]
     chip, core = me // 2, me % 2
     gradients = refs[:portion_count]
-    own, other = refs[portion_count : 2 * portion_count], refs[2 * portion_count : -1]
-    out_ref = refs[-1]
+    own, other = refs[portion_count : 2 * portion_count], refs[2 * portion_count : -3]
+    merged_ref, out_ref, merged_out_ref = refs[-3:]
+    merged_out_ref[...] = merged_ref[...]
     rows = LANES // 2
 
     def step(t, carry):
@@ -145,17 +146,20 @@
     lax.fori_loop(0, out_ref.shape[1] // (2 * LANES), step, 0, unroll=True)
 
 
-def input_gradient(gradients, own, other, me):
+def input_gradient(gradients, own, other, me, merged):
     pixels = gradients[0].shape[0]
     half = own[0].shape[0]
-    operands = [pltpu.with_memory_space_constraint(x, pltpu.VMEM) for x in (*gradients, *own, *other)]
+    operands = [pltpu.with_memory_space_constraint(x, pltpu.VMEM) for x in (*gradients, *own, *other, merged)]
     columns = sum(g.shape[1] for g in gradients)
     return pl.pallas_call(
         functools.partial(input_gradient_kernel, len(gradients)),
-        out_shape=jax.ShapeDtypeStruct((pixels, 2 * half), jnp.bfloat16),
+        out_shape=(
+            jax.ShapeDtypeStruct((pixels, 2 * half), jnp.bfloat16),
+            jax.ShapeDtypeStruct(merged.shape, merged.dtype),
+        ),
         in_specs=[pl.BlockSpec(memory_space=pltpu.SMEM)]
         + [pl.BlockSpec(memory_space=pltpu.VMEM)] * len(operands),
-        out_specs=pl.BlockSpec(memory_space=pltpu.VMEM),
+        out_specs=(pl.BlockSpec(memory_space=pltpu.VMEM),) * 2,
         cost_estimate=pl.CostEstimate(
             flops=4 * pixels * columns * half,
             bytes_accessed=2 * (pixels * columns + 2 * half * columns + 2 * pixels * half),
@@ -712,7 +716,9 @@
                 x.remove(b)
             if step == 0:
                 *sent, g0, g1, g2 = together(*sent, *gradients)
-                input_grad = input_gradient([g0, g1, g2], own_weight, other_weight, me)
+                input_grad, merged = input_gradient(
+                    [g0, g1, g2], own_weight, other_weight, me, merged
+                )
             else:
                 sent = together(*sent)
             arrived = together(*[exchanged(t, b) for t, b in zip(sent, bits_now)])

time: 115 us -> 114 us (level)
  no operation moved by 1% of the time
where the time goes in v7:
time: 114 us
  starting transfers between devices  47.3 us (41%)
  waiting for transfers between devices  45.8 us (40%)
  Pallas kernels  9.96 us (9%)
  matrix products  7.84 us (7%)
  local copies, waits for them, and re-layouts  1.46 us (1%)
    ppermute x30, waiting for transfers between devices, exchanged(): lax.ppermute(block, 'row', [(i, i ^ 1 << bit) for i in range(lax.axis_siz...  42.2 us
    ppermute x30, starting transfers between devices, exchanged(): lax.ppermute(block, 'row', [(i, i ^ 1 << bit) for i in range(lax.axis_siz...  32.1 us
    ppermute x4, starting transfers between devices, swapped(): return lax.ppermute(block, 'row', pairs + [(b, a) for a, b in pairs])  15.2 us
    dot_general x13, matrix products, dot_f32(): lax.dot_general(left, right, (((left_dim,), (right_dim,)), ((), ())), pre...  7.84 us
    pallas_call x1, Pallas kernels, input_gradient(): pl.pallas_call(functools.partial(input_gradient_kernel, len(gradients)),...  3.78 us
    ppermute x4, waiting for transfers between devices, swapped(): return lax.ppermute(block, 'row', pairs + [(b, a) for a, b in pairs])  3.55 us
    pallas_call x7, Pallas kernels, local_call(): pl.pallas_call(kernel, out_shape=out_shape, in_specs=[pl.BlockSpec(memory...  2.43 us
  transfers between devices with their start and end apart: 34, of which 12 were waited for; matrix products, arithmetic and copies ran while one was open for 6% of the time, Pallas kernels for 5%

profile of v7, /device:TPU:0, one launch (start us, length us, event | category | flops | bytes accessed | tf_op | source)
XLA Modules:
  0.0 114.0 jit_solution(18420966203498888338)
XLA Ops:
  1.6 4.1 %collective-permute-start = (bf16[1,1,1,1,656,128]{5,4,3,2,1,0:T(8,128)(2,1)S(1)}, bf16[1,1,1,1,656,128]{5,4,3,2,1,0:T(8,128)(2,1)S(1)}, u32[]{:S(2)}, u32[]{:S(2)}) collective-permute-start(bf16[1,1,1,1,656,128]{5,4,3,2,1,0:T(8,128)(2,1)S(1)} %bitcast.66), channel_id=1, source_target_pairs={{0,16},{1,17},{2,18},{3,19},{4,20},{5,21},{6,22},{7,23},{8,24},{9,... | collective-permute-start | bytes 503816 | tf_op jit(solution)/shard_map/ppermute | solution.py:23
  5.7 1.4 %copy-done = bf16[2,192,2048]{2,1,0:T(8,128)(2,1)S(1)} copy-done((bf16[2,192,2048]{2,1,0:T(8,128)(2,1)S(1)}, bf16[2,192,2048]{2,1,0:T(8,128)(2,1)}, u32[]{:S(2)}) %copy-start) | copy-done | bytes 1572888
  8.1 5.5 %collective-permute-done = bf16[1,1,1,1,656,128]{5,4,3,2,1,0:T(8,128)(2,1)S(1)} collective-permute-done((bf16[1,1,1,1,656,128]{5,4,3,2,1,0:T(8,128)(2,1)S(1)}, bf16[1,1,1,1,656,128]{5,4,3,2,1,0:T(8,128)(2,1)S(1)}, u32[]{:S(2)}, u32[]{:S(2)}) %collective-permute-start) | collective-permute-done | bytes 167968 | tf_op jit(solution)/shard_map/ppermute | solution.py:23
  13.8 1.6 %collective-permute-start.3 = (bf16[2,1,1,1,248,128]{5,4,3,2,1,0:T(8,128)(2,1)S(1)}, bf16[2,1,1,1,248,128]{5,4,3,2,1,0:T(8,128)(2,1)S(1)}, u32[]{:S(2)}, u32[]{:S(2)}) collective-permute-start(bf16[2,1,1,1,248,128]{5,4,3,2,1,0:T(8,128)(2,1)S(1)} %pad_maximum_fusion.6), channel_id=1, source_target_pairs={{0,2},{1,3},{2,0},{3,1},{4,6},{5,7},{6,4},{7,5},{8,10},{9,11},{10,... | collective-permute-start | bytes 380936 | tf_op jit(solution)/shard_map/ppermute | solution.py:23
  16.0 1.5 %collective-permute-start.2 = (bf16[2,1,1,1,200,128]{5,4,3,2,1,0:T(8,128)(2,1)S(1)}, bf16[2,1,1,1,200,128]{5,4,3,2,1,0:T(8,128)(2,1)S(1)}, u32[]{:S(2)}, u32[]{:S(2)}) collective-permute-start(bf16[2,1,1,1,200,128]{5,4,3,2,1,0:T(8,128)(2,1)S(1)} %pad_maximum_fusion.8), channel_id=1, source_target_pairs={{0,4},{1,5},{2,6},{3,7},{4,0},{5,1},{6,2},{7,3},{8,12},{9,13},{10,... | collective-permute-start | bytes 307208 | tf_op jit(solution)/shard_map/ppermute | solution.py:23
  17.6 3.1 %collective-permute-done.2 = bf16[2,1,1,1,200,128]{5,4,3,2,1,0:T(8,128)(2,1)S(1)} collective-permute-done((bf16[2,1,1,1,200,128]{5,4,3,2,1,0:T(8,128)(2,1)S(1)}, bf16[2,1,1,1,200,128]{5,4,3,2,1,0:T(8,128)(2,1)S(1)}, u32[]{:S(2)}, u32[]{:S(2)}) %collective-permute-start.2) | collective-permute-done | bytes 102432 | tf_op jit(solution)/shard_map/ppermute | solution.py:23
  20.8 1.4 %collective-permute-start.6 = (bf16[2,1,1,2,248,128]{5,4,3,2,1,0:T(8,128)(2,1)S(1)}, bf16[2,1,1,2,248,128]{5,4,3,2,1,0:T(8,128)(2,1)S(1)}, u32[]{:S(2)}, u32[]{:S(2)}) collective-permute-start(bf16[2,1,1,2,248,128]{5,4,3,2,1,0:T(8,128)(2,1)S(1)} %pad_maximum_fusion.3), channel_id=1, source_target_pairs={{0,8},{1,9},{2,10},{3,11},{4,12},{5,13},{6,14},{7,15},{8,0},{9,1},... | collective-permute-start | bytes 761864 | tf_op jit(solution)/shard_map/ppermute | solution.py:23
  22.2 1.5 %collective-permute-start.4 = (bf16[2,2,1,1,208,128]{5,4,3,2,1,0:T(8,128)(2,1)S(1)}, bf16[2,2,1,1,208,128]{5,4,3,2,1,0:T(8,128)(2,1)S(1)}, u32[]{:S(2)}, u32[]{:S(2)}) collective-permute-start(bf16[2,2,1,1,208,128]{5,4,3,2,1,0:T(8,128)(2,1)S(1)} %pad_maximum_fusion.4), channel_id=1, source_target_pairs={{0,4},{1,5},{2,6},{3,7},{4,0},{5,1},{6,2},{7,3},{8,12},{9,13},{10,... | collective-permute-start | bytes 638984 | tf_op jit(solution)/shard_map/ppermute | solution.py:23
  24.3 5.4 %collective-permute-done.5 = bf16[2,1,2,1,200,128]{5,4,3,2,1,0:T(8,128)(2,1)S(1)} collective-permute-done((bf16[2,1,2,1,200,128]{5,4,3,2,1,0:T(8,128)(2,1)S(1)}, bf16[2,1,2,1,200,128]{5,4,3,2,1,0:T(8,128)(2,1)S(1)}, u32[]{:S(2)}, u32[]{:S(2)}) %collective-permute-start.5) | collective-permute-done | bytes 204832 | tf_op jit(solution)/shard_map/ppermute | solution.py:23
  31.4 7.2 %collective-permute-done.9 = bf16[2,1,2,2,200,128]{5,4,3,2,1,0:T(8,128)(2,1)S(1)} collective-permute-done((bf16[2,1,2,2,200,128]{5,4,3,2,1,0:T(8,128)(2,1)S(1)}, bf16[2,1,2,2,200,128]{5,4,3,2,1,0:T(8,128)(2,1)S(1)}, u32[]{:S(2)}, u32[]{:S(2)}) %collective-permute-start.9) | collective-permute-done | bytes 409632 | tf_op jit(solution)/shard_map/ppermute | solution.py:23
  44.0 3.3 %collective-permute-start.13 = (f32[384,128]{1,0:T(8,128)S(1)}, f32[384,128]{1,0:T(8,128)S(1)}, u32[]{:S(2)}, u32[]{:S(2)}) collective-permute-start(f32[384,128]{1,0:T(8,128)S(1)} %get-tuple-element.160), channel_id=1, source_target_pairs={{0,9},{1,10},{2,11},{3,12},{4,13},{5,14},{6,15},{7,16},{8,17},{18,... | collective-permute-start | bytes 589832 | tf_op jit(solution)/shard_map/ppermute | solution.py:19
  49.4 2.8 %collective-permute-done.13.above_ref = f32[384,128]{1,0:T(8,128)S(1)} collective-permute-done((f32[384,128]{1,0:T(8,128)S(1)}, f32[384,128]{1,0:T(8,128)S(1)}, u32[]{:S(2)}, u32[]{:S(2)}) %collective-permute-start.13) | collective-permute-done | bytes 196640 | tf_op jit(solution)/shard_map/ppermute | solution.py:19
  55.3 10.6 %collective-permute-start.16 = (bf16[384,128]{1,0:T(8,128)(2,1)S(1)}, bf16[384,128]{1,0:T(8,128)(2,1)S(1)}, u32[]{:S(2)}, u32[]{:S(2)}) collective-permute-start(bf16[384,128]{1,0:T(8,128)(2,1)S(1)} %get-tuple-element.163), channel_id=1, source_target_pairs={{0,9},{1,10},{2,11},{3,12},{4,13},{5,14},{6,15},{7,16},{8,17},{18,... | collective-permute-start | bytes 294920 | tf_op jit(solution)/shard_map/ppermute | solution.py:19
  74.4 3.1 %collective-permute-start.24 = (bf16[8,208,128]{2,1,0:T(8,128)(2,1)S(1)}, bf16[8,208,128]{2,1,0:T(8,128)(2,1)S(1)}, u32[]{:S(2)}, u32[]{:S(2)}) collective-permute-start(bf16[8,208,128]{2,1,0:T(8,128)(2,1)S(1)} %get-tuple-element.192), channel_id=1, source_target_pairs={{0,2},{1,3},{2,0},{3,1},{4,6},{5,7},{6,4},{7,5},{8,10},{9,11},{10,... | collective-permute-start | bytes 1277960 | tf_op jit(solution)/shard_map/ppermute | solution.py:23
  77.5 1.8 %collective-permute-start.25 = (bf16[8,200,128]{2,1,0:T(8,128)(2,1)S(1)}, bf16[8,200,128]{2,1,0:T(8,128)(2,1)S(1)}, u32[]{:S(2)}, u32[]{:S(2)}) collective-permute-start(bf16[8,200,128]{2,1,0:T(8,128)(2,1)S(1)} %get-tuple-element.193), channel_id=1, source_target_pairs={{0,8},{1,9},{2,10},{3,11},{4,12},{5,13},{6,14},{7,15},{8,0},{9,1},... | collective-permute-start | bytes 1228808 | tf_op jit(solution)/shard_map/ppermute | solution.py:23
  79.3 3.8 %input_gradient.1 = (bf16[384,2048]{1,0:T(8,128)(2,1)}, bf16[384,256]{1,0:T(8,128)(2,1)}) custom-call(s32[1]{0:T(128)} %bitcast.2.me_ref, bf16[384,384]{1,0:T(8,128)(2,1)S(1)} %get-tuple-element.185.refs_0_, bf16[384,384]{1,0:T(8,128)(2,1)S(1)} %get-tuple-element.186.refs_1_, bf16[384,512]{1,0:T(8,128)(2,1)S(1)} %get-tuple-element.187.refs_2_, ...), custom_call_target="tpu_custom_call" | custom-call | flops 2013265920 | bytes 7798784 | tf_op jit(solution)/shard_map/input_gradient/pallas_call | solution.py:154
  83.1 5.8 %collective-permute-done.25.refs_4_ = bf16[8,200,128]{2,1,0:T(8,128)(2,1)S(1)} collective-permute-done((bf16[8,200,128]{2,1,0:T(8,128)(2,1)S(1)}, bf16[8,200,128]{2,1,0:T(8,128)(2,1)S(1)}, u32[]{:S(2)}, u32[]{:S(2)}) %collective-permute-start.25) | collective-permute-done | bytes 409632 | tf_op jit(solution)/shard_map/ppermute | solution.py:23
  89.2 1.8 %collective-permute-start.29 = (bf16[4,248,128]{2,1,0:T(8,128)(2,1)S(1)}, bf16[4,248,128]{2,1,0:T(8,128)(2,1)S(1)}, u32[]{:S(2)}, u32[]{:S(2)}) collective-permute-start(bf16[4,248,128]{2,1,0:T(8,128)(2,1)S(1)} %get-tuple-element.214), channel_id=1, source_target_pairs={{0,8},{1,9},{2,10},{3,11},{4,12},{5,13},{6,14},{7,15},{8,0},{9,1},... | collective-permute-start | bytes 761864 | tf_op jit(solution)/shard_map/ppermute | solution.py:23
  91.0 1.6 %collective-permute-start.27 = (bf16[4,208,128]{2,1,0:T(8,128)(2,1)S(1)}, bf16[4,208,128]{2,1,0:T(8,128)(2,1)S(1)}, u32[]{:S(2)}, u32[]{:S(2)}) collective-permute-start(bf16[4,208,128]{2,1,0:T(8,128)(2,1)S(1)} %get-tuple-element.212), channel_id=1, source_target_pairs={{0,4},{1,5},{2,6},{3,7},{4,0},{5,1},{6,2},{7,3},{8,12},{9,13},{10,... | collective-permute-start | bytes 638984 | tf_op jit(solution)/shard_map/ppermute | solution.py:23
  93.6 4.7 %collective-permute-done.28.refs_4_ = bf16[4,200,128]{2,1,0:T(8,128)(2,1)S(1)} collective-permute-done((bf16[4,200,128]{2,1,0:T(8,128)(2,1)S(1)}, bf16[4,200,128]{2,1,0:T(8,128)(2,1)S(1)}, u32[]{:S(2)}, u32[]{:S(2)}) %collective-permute-start.28) | collective-permute-done | bytes 204832 | tf_op jit(solution)/shard_map/ppermute | solution.py:23
  98.5 1.5 %collective-permute-start.32 = (bf16[2,248,128]{2,1,0:T(8,128)(2,1)S(1)}, bf16[2,248,128]{2,1,0:T(8,128)(2,1)S(1)}, u32[]{:S(2)}, u32[]{:S(2)}) collective-permute-start(bf16[2,248,128]{2,1,0:T(8,128)(2,1)S(1)} %get-tuple-element.226), channel_id=1, source_target_pairs={{0,2},{1,3},{2,0},{3,1},{4,6},{5,7},{6,4},{7,5},{8,10},{9,11},{10,... | collective-permute-start | bytes 380936 | tf_op jit(solution)/shard_map/ppermute | solution.py:23
  101.6 3.4 %collective-permute-done.31.refs_4_ = bf16[2,200,128]{2,1,0:T(8,128)(2,1)S(1)} collective-permute-done((bf16[2,200,128]{2,1,0:T(8,128)(2,1)S(1)}, bf16[2,200,128]{2,1,0:T(8,128)(2,1)S(1)}, u32[]{:S(2)}, u32[]{:S(2)}) %collective-permute-start.31) | collective-permute-done | bytes 102432 | tf_op jit(solution)/shard_map/ppermute | solution.py:23
  105.1 2.4 %collective-permute-start.33 = (bf16[656,128]{1,0:T(8,128)(2,1)S(1)}, bf16[656,128]{1,0:T(8,128)(2,1)S(1)}, u32[]{:S(2)}, u32[]{:S(2)}) collective-permute-start(bf16[656,128]{1,0:T(8,128)(2,1)S(1)} %get-tuple-element.231), channel_id=1, source_target_pairs={{0,16},{1,17},{2,18},{3,19},{4,20},{5,21},{6,22},{7,23},{8,24},{9,... | collective-permute-start | bytes 503816 | tf_op jit(solution)/shard_map/ppermute | solution.py:23
  107.5 5.7 %collective-permute-done.33.arrived_ref = bf16[656,128]{1,0:T(8,128)(2,1)S(1)} collective-permute-done((bf16[656,128]{1,0:T(8,128)(2,1)S(1)}, bf16[656,128]{1,0:T(8,128)(2,1)S(1)}, u32[]{:S(2)}, u32[]{:S(2)}) %collective-permute-start.33) | collective-permute-done | bytes 167968 | tf_op jit(solution)/shard_map/ppermute | solution.py:23
  (100 shorter events, 27.7 us)
Async XLA Ops:
  1.6 12.0 %collective-permute-start = (bf16[1,1,1,1,656,128]{5,4,3,2,1,0:T(8,128)(2,1)S(1)}, bf16[1,1,1,1,656,128]{5,4,3,2,1,0:T(8,128)(2,1)S(1)}, u32[]{:S(2)}, u32[]{:S(2)}) collective-permute-start(bf16[1,1,1,1,656,128]{5,4,3,2,1,0:T(8,128)(2,1)S(1)} %bitcast.66), channel_id=1, source_target_pairs={{0,16},{1,17},{2,18},{3,19},{4,20},{5,21},{6,22},{7,23},{8,24},{9,... | collective-permute-start | bytes 503816 | tf_op jit(solution)/shard_map/ppermute | solution.py:23
  13.8 6.9 %collective-permute-start.3 = (bf16[2,1,1,1,248,128]{5,4,3,2,1,0:T(8,128)(2,1)S(1)}, bf16[2,1,1,1,248,128]{5,4,3,2,1,0:T(8,128)(2,1)S(1)}, u32[]{:S(2)}, u32[]{:S(2)}) collective-permute-start(bf16[2,1,1,1,248,128]{5,4,3,2,1,0:T(8,128)(2,1)S(1)} %pad_maximum_fusion.6), channel_id=1, source_target_pairs={{0,2},{1,3},{2,0},{3,1},{4,6},{5,7},{6,4},{7,5},{8,10},{9,11},{10,... | collective-permute-start | bytes 380936 | tf_op jit(solution)/shard_map/ppermute | solution.py:23
  17.6 12.3 %collective-permute-start.7 = (bf16[384,1024]{1,0:T(8,128)(2,1)S(1)}, bf16[384,1024]{1,0:T(8,128)(2,1)S(1)}, u32[]{:S(2)}, u32[]{:S(2)}) collective-permute-start(bf16[384,1024]{1,0:T(8,128)(2,1)S(1)} %get-tuple-element.139), channel_id=1, source_target_pairs={{0,1},{1,0},{2,3},{3,2},{4,5},{5,4},{6,7},{7,6},{8,9},{9,8},{10,11... | collective-permute-start | bytes 2359304 | tf_op jit(solution)/shard_map/ppermute | solution.py:23
  20.8 8.9 %collective-permute-start.6 = (bf16[2,1,1,2,248,128]{5,4,3,2,1,0:T(8,128)(2,1)S(1)}, bf16[2,1,1,2,248,128]{5,4,3,2,1,0:T(8,128)(2,1)S(1)}, u32[]{:S(2)}, u32[]{:S(2)}) collective-permute-start(bf16[2,1,1,2,248,128]{5,4,3,2,1,0:T(8,128)(2,1)S(1)} %pad_maximum_fusion.3), channel_id=1, source_target_pairs={{0,8},{1,9},{2,10},{3,11},{4,12},{5,13},{6,14},{7,15},{8,0},{9,1},... | collective-permute-start | bytes 761864 | tf_op jit(solution)/shard_map/ppermute | solution.py:23
  22.2 7.5 %collective-permute-start.4 = (bf16[2,2,1,1,208,128]{5,4,3,2,1,0:T(8,128)(2,1)S(1)}, bf16[2,2,1,1,208,128]{5,4,3,2,1,0:T(8,128)(2,1)S(1)}, u32[]{:S(2)}, u32[]{:S(2)}) collective-permute-start(bf16[2,2,1,1,208,128]{5,4,3,2,1,0:T(8,128)(2,1)S(1)} %pad_maximum_fusion.4), channel_id=1, source_target_pairs={{0,4},{1,5},{2,6},{3,7},{4,0},{5,1},{6,2},{7,3},{8,12},{9,13},{10,... | collective-permute-start | bytes 638984 | tf_op jit(solution)/shard_map/ppermute | solution.py:23
  23.7 5.9 %collective-permute-start.5 = (bf16[2,1,2,1,200,128]{5,4,3,2,1,0:T(8,128)(2,1)S(1)}, bf16[2,1,2,1,200,128]{5,4,3,2,1,0:T(8,128)(2,1)S(1)}, u32[]{:S(2)}, u32[]{:S(2)}) collective-permute-start(bf16[2,1,2,1,200,128]{5,4,3,2,1,0:T(8,128)(2,1)S(1)} %pad_maximum_fusion.5), channel_id=1, source_target_pairs={{0,2},{1,3},{2,0},{3,1},{4,6},{5,7},{6,4},{7,5},{8,10},{9,11},{10,... | collective-permute-start | bytes 614408 | tf_op jit(solution)/shard_map/ppermute | solution.py:23
  29.8 9.5 %collective-permute-start.10 = (bf16[2,2,1,2,248,128]{5,4,3,2,1,0:T(8,128)(2,1)S(1)}, bf16[2,2,1,2,248,128]{5,4,3,2,1,0:T(8,128)(2,1)S(1)}, u32[]{:S(2)}, u32[]{:S(2)}) collective-permute-start(bf16[2,2,1,2,248,128]{5,4,3,2,1,0:T(8,128)(2,1)S(1)} %pad_maximum_fusion), channel_id=1, source_target_pairs={{0,4},{1,5},{2,6},{3,7},{4,0},{5,1},{6,2},{7,3},{8,12},{9,13},{10,... | collective-permute-start | bytes 1523720 | tf_op jit(solution)/shard_map/ppermute | solution.py:23
  30.2 8.4 %collective-permute-start.8 = (bf16[2,2,2,1,208,128]{5,4,3,2,1,0:T(8,128)(2,1)S(1)}, bf16[2,2,2,1,208,128]{5,4,3,2,1,0:T(8,128)(2,1)S(1)}, u32[]{:S(2)}, u32[]{:S(2)}) collective-permute-start(bf16[2,2,2,1,208,128]{5,4,3,2,1,0:T(8,128)(2,1)S(1)} %pad_maximum_fusion.1), channel_id=1, source_target_pairs={{0,2},{1,3},{2,0},{3,1},{4,6},{5,7},{6,4},{7,5},{8,10},{9,11},{10,... | collective-permute-start | bytes 1277960 | tf_op jit(solution)/shard_map/ppermute | solution.py:23
  30.7 8.0 %collective-permute-start.9 = (bf16[2,1,2,2,200,128]{5,4,3,2,1,0:T(8,128)(2,1)S(1)}, bf16[2,1,2,2,200,128]{5,4,3,2,1,0:T(8,128)(2,1)S(1)}, u32[]{:S(2)}, u32[]{:S(2)}) collective-permute-start(bf16[2,1,2,2,200,128]{5,4,3,2,1,0:T(8,128)(2,1)S(1)} %pad_maximum_fusion.2), channel_id=1, source_target_pairs={{0,8},{1,9},{2,10},{3,11},{4,12},{5,13},{6,14},{7,15},{8,0},{9,1},... | collective-permute-start | bytes 1228808 | tf_op jit(solution)/shard_map/ppermute | solution.py:23
  44.0 8.2 %collective-permute-start.13 = (f32[384,128]{1,0:T(8,128)S(1)}, f32[384,128]{1,0:T(8,128)S(1)}, u32[]{:S(2)}, u32[]{:S(2)}) collective-permute-start(f32[384,128]{1,0:T(8,128)S(1)} %get-tuple-element.160), channel_id=1, source_target_pairs={{0,9},{1,10},{2,11},{3,12},{4,13},{5,14},{6,15},{7,16},{8,17},{18,... | collective-permute-start | bytes 589832 | tf_op jit(solution)/shard_map/ppermute | solution.py:19
  53.1 12.8 %collective-permute-start.18 = (bf16[384,512]{1,0:T(8,128)(2,1)S(1)}, bf16[384,512]{1,0:T(8,128)(2,1)S(1)}, u32[]{:S(2)}, u32[]{:S(2)}) collective-permute-start(bf16[384,512]{1,0:T(8,128)(2,1)S(1)} %get-tuple-element.187.refs_2_), channel_id=1, source_target_pairs={{0,1},{1,0},{2,3},{3,2},{4,5},{5,4},{6,7},{7,6},{8,9},{9,8},{10,11... | collective-permute-start | bytes 1179656 | tf_op jit(solution)/shard_map/ppermute | solution.py:23
  54.2 13.4 %collective-permute-start.19 = (bf16[1024,384]{1,0:T(8,128)(2,1)S(1)}, bf16[1024,384]{1,0:T(8,128)(2,1)S(1)}, u32[]{:S(2)}, u32[]{:S(2)}) collective-permute-start(bf16[1024,384]{1,0:T(8,128)(2,1)S(1)} %bitcast.53), channel_id=1, source_target_pairs={{0,1},{1,0},{2,3},{3,2},{4,5},{5,4},{6,7},{7,6},{8,9},{9,8},{10,11... | collective-permute-start | bytes 2359304 | tf_op jit(solution)/shard_map/ppermute | solution.py:23
  54.2 13.3 %collective-permute-start.20 = (bf16[1024,384]{1,0:T(8,128)(2,1)S(1)}, bf16[1024,384]{1,0:T(8,128)(2,1)S(1)}, u32[]{:S(2)}, u32[]{:S(2)}) collective-permute-start(bf16[1024,384]{1,0:T(8,128)(2,1)S(1)} %bitcast.57), channel_id=1, source_target_pairs={{0,1},{1,0},{2,3},{3,2},{4,5},{5,4},{6,7},{7,6},{8,9},{9,8},{10,11... | collective-permute-start | bytes 2359304 | tf_op jit(solution)/shard_map/ppermute | solution.py:23
  54.7 12.9 %collective-permute-start.17 = (bf16[384,128]{1,0:T(8,128)(2,1)S(1)}, bf16[384,128]{1,0:T(8,128)(2,1)S(1)}, u32[]{:S(2)}, u32[]{:S(2)}) collective-permute-start(bf16[384,128]{1,0:T(8,128)(2,1)S(1)} %get-tuple-element.163), channel_id=1, source_target_pairs={{9,18},{10,19},{11,20},{12,21},{13,22},{14,23},{15,24},{16,25},{17... | collective-permute-start | bytes 294920 | tf_op jit(solution)/shard_map/ppermute | solution.py:19
  55.3 12.9 %collective-permute-start.16 = (bf16[384,128]{1,0:T(8,128)(2,1)S(1)}, bf16[384,128]{1,0:T(8,128)(2,1)S(1)}, u32[]{:S(2)}, u32[]{:S(2)}) collective-permute-start(bf16[384,128]{1,0:T(8,128)(2,1)S(1)} %get-tuple-element.163), channel_id=1, source_target_pairs={{0,9},{1,10},{2,11},{3,12},{4,13},{5,14},{6,15},{7,16},{8,17},{18,... | collective-permute-start | bytes 294920 | tf_op jit(solution)/shard_map/ppermute | solution.py:19
  65.9 6.8 %collective-permute-start.23 = (f32[128,256]{1,0:T(8,128)S(1)}, f32[128,256]{1,0:T(8,128)S(1)}, u32[]{:S(2)}, u32[]{:S(2)}) collective-permute-start(f32[128,256]{1,0:T(8,128)S(1)} %get-tuple-element.181), channel_id=1, source_target_pairs={{0,1},{1,0},{2,3},{3,2},{4,5},{5,4},{6,7},{7,6},{8,9},{9,8},{10,11... | collective-permute-start | bytes 393224 | tf_op jit(solution)/shard_map/ppermute | solution.py:23
  73.1 15.8 %collective-permute-start.26 = (bf16[8,248,128]{2,1,0:T(8,128)(2,1)S(1)}, bf16[8,248,128]{2,1,0:T(8,128)(2,1)S(1)}, u32[]{:S(2)}, u32[]{:S(2)}) collective-permute-start(bf16[8,248,128]{2,1,0:T(8,128)(2,1)S(1)} %get-tuple-element.194), channel_id=1, source_target_pairs={{0,4},{1,5},{2,6},{3,7},{4,0},{5,1},{6,2},{7,3},{8,12},{9,13},{10,... | collective-permute-start | bytes 1523720 | tf_op jit(solution)/shard_map/ppermute | solution.py:23
  74.4 14.5 %collective-permute-start.24 = (bf16[8,208,128]{2,1,0:T(8,128)(2,1)S(1)}, bf16[8,208,128]{2,1,0:T(8,128)(2,1)S(1)}, u32[]{:S(2)}, u32[]{:S(2)}) collective-permute-start(bf16[8,208,128]{2,1,0:T(8,128)(2,1)S(1)} %get-tuple-element.192), channel_id=1, source_target_pairs={{0,2},{1,3},{2,0},{3,1},{4,6},{5,7},{6,4},{7,5},{8,10},{9,11},{10,... | collective-permute-start | bytes 1277960 | tf_op jit(solution)/shard_map/ppermute | solution.py:23
  77.5 11.4 %collective-permute-start.25 = (bf16[8,200,128]{2,1,0:T(8,128)(2,1)S(1)}, bf16[8,200,128]{2,1,0:T(8,128)(2,1)S(1)}, u32[]{:S(2)}, u32[]{:S(2)}) collective-permute-start(bf16[8,200,128]{2,1,0:T(8,128)(2,1)S(1)} %get-tuple-element.193), channel_id=1, source_target_pairs={{0,8},{1,9},{2,10},{3,11},{4,12},{5,13},{6,14},{7,15},{8,0},{9,1},... | collective-permute-start | bytes 1228808 | tf_op jit(solution)/shard_map/ppermute | solution.py:23
  89.2 9.2 %collective-permute-start.29 = (bf16[4,248,128]{2,1,0:T(8,128)(2,1)S(1)}, bf16[4,248,128]{2,1,0:T(8,128)(2,1)S(1)}, u32[]{:S(2)}, u32[]{:S(2)}) collective-permute-start(bf16[4,248,128]{2,1,0:T(8,128)(2,1)S(1)} %get-tuple-element.214), channel_id=1, source_target_pairs={{0,8},{1,9},{2,10},{3,11},{4,12},{5,13},{6,14},{7,15},{8,0},{9,1},... | collective-permute-start | bytes 761864 | tf_op jit(solution)/shard_map/ppermute | solution.py:23
  91.0 7.3 %collective-permute-start.27 = (bf16[4,208,128]{2,1,0:T(8,128)(2,1)S(1)}, bf16[4,208,128]{2,1,0:T(8,128)(2,1)S(1)}, u32[]{:S(2)}, u32[]{:S(2)}) collective-permute-start(bf16[4,208,128]{2,1,0:T(8,128)(2,1)S(1)} %get-tuple-element.212), channel_id=1, source_target_pairs={{0,4},{1,5},{2,6},{3,7},{4,0},{5,1},{6,2},{7,3},{8,12},{9,13},{10,... | collective-permute-start | bytes 638984 | tf_op jit(solution)/shard_map/ppermute | solution.py:23
  92.5 5.8 %collective-permute-start.28 = (bf16[4,200,128]{2,1,0:T(8,128)(2,1)S(1)}, bf16[4,200,128]{2,1,0:T(8,128)(2,1)S(1)}, u32[]{:S(2)}, u32[]{:S(2)}) collective-permute-start(bf16[4,200,128]{2,1,0:T(8,128)(2,1)S(1)} %get-tuple-element.213), channel_id=1, source_target_pairs={{0,2},{1,3},{2,0},{3,1},{4,6},{5,7},{6,4},{7,5},{8,10},{9,11},{10,... | collective-permute-start | bytes 614408 | tf_op jit(solution)/shard_map/ppermute | solution.py:23
  98.5 6.6 %collective-permute-start.32 = (bf16[2,248,128]{2,1,0:T(8,128)(2,1)S(1)}, bf16[2,248,128]{2,1,0:T(8,128)(2,1)S(1)}, u32[]{:S(2)}, u32[]{:S(2)}) collective-permute-start(bf16[2,248,128]{2,1,0:T(8,128)(2,1)S(1)} %get-tuple-element.226), channel_id=1, source_target_pairs={{0,2},{1,3},{2,0},{3,1},{4,6},{5,7},{6,4},{7,5},{8,10},{9,11},{10,... | collective-permute-start | bytes 380936 | tf_op jit(solution)/shard_map/ppermute | solution.py:23
  105.1 8.1 %collective-permute-start.33 = (bf16[656,128]{1,0:T(8,128)(2,1)S(1)}, bf16[656,128]{1,0:T(8,128)(2,1)S(1)}, u32[]{:S(2)}, u32[]{:S(2)}) collective-permute-start(bf16[656,128]{1,0:T(8,128)(2,1)S(1)} %get-tuple-element.231), channel_id=1, source_target_pairs={{0,16},{1,17},{2,18},{3,19},{4,20},{5,21},{6,22},{7,23},{8,24},{9,... | collective-permute-start | bytes 503816 | tf_op jit(solution)/shard_map/ppermute | solution.py:23
  (14 other events, 51.9 us)
